TPU v7x, 32 devices: a whole 2x2x4 slice. The times are simulated.
32 devices in a mesh: gz: 2 (over x), gy: 4 (over z), gx: 4 (over y, core).
Axes of the slice: x: 2, y: 2, z: 4, core: 2. Of those that a mesh axis runs over, the one named last changes fastest.
Arguments:
- images: bfloat16 [2, 640, 640], P('gz', 'gy', 'gx'), may hold values from -6 to 6
- tissue_mask: int32 [2, 16, 16], P('gz', 'gy', 'gx'), may hold values 0 or 1
Outputs:
- flow_fields: float32 [4, 2, 16, 16], P(None, 'gz', 'gy', 'gx')
- mesh_offsets: float32 [2, 2, 16, 16], P(None, 'gz', 'gy', 'gx')
Inputs may be any that keep to these rules, and one draw needn't show every extreme that they name: `tissue_mask`: 0 or 1 for each patch.
All inputs are finite; a program needn't handle non-finite values. No bound on the sum of `tissue_mask` on one device may be relied on, other than what follows from the above.
Results may differ from a plain program's by a relative error of at most 0.0003.
Values may be sent and summed in bfloat16 or wider, within the bound.
No kernel may reach another device: no remote copies, remote signals or barrier semaphores. Data moves between devices by JAX's collectives and lax.ppermute only.
A program may use at most 128 MiB of HBM per device.

v0:
```python
import functools
import math

import jax
import jax.numpy as jnp
import numpy as np
from jax import lax
from jax.experimental import pallas as pl
from jax.experimental.pallas import tpu as pltpu
from jax.sharding import PartitionSpec as P

PATCH = 160
STRIDE = 40
RELAX = 4


EPSILON = 1e-06
STIFFNESS = 0.5
STEP_SIZE = 0.2


def shifted(value, axis, steps):
    count = lax.axis_size(axis)
    initial, last = (max(0, -steps), min(count, count - steps))
    return lax.ppermute(value, axis, [(source, source + steps) for source in range(initial, last)])


def padded_2(x, sides, width):
    for axis, dim in sides:
        size, length = (lax.axis_size(axis), x.shape[dim])
        up = [(i, (i + 1) % size) for i in range(size - 1)]
        down = [(j, i) for i, j in up]
        last = lax.slice_in_dim(x, length - width, length, axis=dim)
        initial = lax.slice_in_dim(x, 0, width, axis=dim)
        before = lax.ppermute(last, axis, up)
        after = lax.ppermute(initial, axis, down)
        x = jnp.concatenate([before, x, after], axis=dim)
    return x


def windows(section):
    repeats = PATCH // STRIDE
    count_y = section.shape[0] // STRIDE - repeats + 1
    count_x = section.shape[1] // STRIDE - repeats + 1
    blocks = section.reshape(section.shape[0] // STRIDE, STRIDE, section.shape[1] // STRIDE, STRIDE)
    pieces = []
    for first in range(repeats):
        row_pieces = [
            blocks[first : first + count_y, :, second : second + count_x, :]
            for second in range(repeats)
        ]
        pieces.append(jnp.stack(row_pieces, 0))
    stacked = jnp.stack(pieces, 0)
    stacked = jnp.transpose(stacked, (2, 4, 0, 3, 1, 5))
    return stacked.reshape(count_y * count_x, PATCH, PATCH)


def tables():
    indices = jnp.arange(PATCH, dtype=jnp.int32)
    phases = indices[:, None] * indices[None, :] % PATCH
    angles = phases.astype(jnp.float32) * (2.0 * math.pi / PATCH)
    cosine_table = jnp.cos(angles)
    sine_table = jnp.sin(angles)
    left_table = jnp.concatenate([cosine_table, sine_table], 0)
    right_table = jnp.concatenate([cosine_table, sine_table], 1)
    return (left_table, right_table)


def spectrum(section, left_table, right_table):
    patches = windows(section)
    halfway = jnp.einsum("pnm,mk->pnk", patches, right_table, precision=lax.Precision.HIGHEST)
    products = jnp.einsum("kn,pnm->pkm", left_table, halfway, precision=lax.Precision.HIGHEST)
    cos_a = products[:, :PATCH, :PATCH]
    cos_b = products[:, :PATCH, PATCH:]
    sin_a = products[:, PATCH:, :PATCH]
    sin_b = products[:, PATCH:, PATCH:]
    return (cos_a - sin_b, -(cos_b + sin_a))


def flow_between(own_re, own_im, next_re, next_im, left_table, count_y, count_x):
    cross_re = next_re * own_re + next_im * own_im
    cross_im = next_im * own_re - next_re * own_im
    stacked = jnp.concatenate([cross_re, cross_im], 2)
    products = jnp.einsum("kn,pnm->pkm", left_table, stacked, precision=lax.Precision.HIGHEST)
    mixed_re = products[:, :PATCH, :PATCH] - products[:, PATCH:, PATCH:]
    mixed_im = products[:, :PATCH, PATCH:] + products[:, PATCH:, :PATCH]
    joined = jnp.concatenate([mixed_re, -mixed_im], 2)
    correl = jnp.einsum("pnm,mk->pnk", joined, left_table, precision=lax.Precision.HIGHEST) / (
        PATCH * PATCH
    )
    squared = correl * correl
    weights = squared * squared
    totals = jnp.sum(weights, axis=(1, 2)) + EPSILON
    shifts = ((jnp.arange(PATCH, dtype=jnp.int32) + PATCH // 2) % PATCH - PATCH // 2).astype(
        jnp.float32
    )
    flow_y = jnp.sum(weights * shifts[None, :, None], axis=(1, 2)) / totals
    flow_x = jnp.sum(weights * shifts[None, None, :], axis=(1, 2)) / totals
    return jnp.stack([flow_y, flow_x], 0).reshape(2, count_y, count_x)


def laplacian(widened, offsets):
    return (
        widened[:, :, :-2, 1:-1]
        + widened[:, :, 2:, 1:-1]
        + widened[:, :, 1:-1, :-2]
        + widened[:, :, 1:-1, 2:]
        - 4.0 * offsets
    )


def remote_neighbours(offsets):
    up_one = shifted(offsets, "gz", -1)
    up_two = shifted(offsets, "gz", -2)
    down_one = shifted(offsets, "gz", 1)
    down_two = shifted(offsets, "gz", 2)
    return (up_one, up_two, down_one, down_two)


def mesh_step(offsets, laplace, coeffs):
    up_one, up_two, down_one, down_two = remote_neighbours(offsets)
    forces = STIFFNESS * laplace
    forces = forces + coeffs[2:3] * (up_one - offsets - coeffs[0:2])
    forces = forces + coeffs[5:6] * (up_two - offsets - coeffs[3:5])
    forces = forces - coeffs[8:9] * (offsets - down_one - coeffs[6:8])
    forces = forces - coeffs[11:12] * (offsets - down_two - coeffs[9:11])
    return offsets + STEP_SIZE * forces


def general_body(images, tissue_mask):
    margin = (PATCH - STRIDE) // 2
    count_y = images.shape[1] // STRIDE
    count_x = images.shape[2] // STRIDE
    padded = padded_2(images, (("gy", 1), ("gx", 2)), margin)
    left_table, right_table = tables()
    own_mask = tissue_mask.astype(jnp.float32)
    own_re, own_im = spectrum(padded[0].astype(jnp.float32), left_table, right_table)
    next_re, next_im, next_mask = shifted((own_re, own_im, own_mask), "gz", -1)
    far_re, far_im, far_mask = shifted((own_re, own_im, own_mask), "gz", -2)
    flow_one = flow_between(own_re, own_im, next_re, next_im, left_table, count_y, count_x)
    flow_two = flow_between(own_re, own_im, far_re, far_im, left_table, count_y, count_x)
    weight_one = own_mask * next_mask
    weight_two = own_mask * far_mask
    low_flow_one, low_weight_one = shifted((flow_one, weight_one), "gz", 1)
    low_flow_two, low_weight_two = shifted((flow_two, weight_two), "gz", 2)
    coeffs = jnp.concatenate(
        [
            flow_one,
            weight_one,
            flow_two,
            weight_two,
            low_flow_one,
            low_weight_one,
            low_flow_two,
            low_weight_two,
        ],
        0,
    )[:, None]
    spread = padded_2(coeffs, (("gy", 2), ("gx", 3)), RELAX)
    global_y = lax.axis_index("gy") * count_y + jnp.arange(-RELAX, count_y + RELAX, dtype=jnp.int32)
    global_x = lax.axis_index("gx") * count_x + jnp.arange(-RELAX, count_x + RELAX, dtype=jnp.int32)
    inside_y = (global_y >= 0) & (global_y < count_y * lax.axis_size("gy"))
    inside_x = (global_x >= 0) & (global_x < count_x * lax.axis_size("gx"))
    inside = (inside_y[:, None] & inside_x[None, :]).astype(jnp.float32)
    offsets = jnp.zeros((2, 1, count_y + 2 * RELAX, count_x + 2 * RELAX), jnp.float32)
    for _ in range(RELAX):
        widened = jnp.pad(offsets, ((0, 0), (0, 0), (1, 1), (1, 1)))
        offsets = mesh_step(offsets, laplacian(widened, offsets), spread) * inside[None, None]
    offsets = offsets[:, :, RELAX : RELAX + count_y, RELAX : RELAX + count_x]
    flow_fields = jnp.concatenate([flow_one, flow_two], 0)[:, None]
    return (flow_fields, offsets)


MARGIN = (PATCH - STRIDE) // 2
HALF = PATCH // 2 + 1
LANES = 128
SUBLANES = 8
ROWS_K = -(-HALF // SUBLANES) * SUBLANES
HALO = -(-MARGIN // 16) * 16
RADIUS = RELAX - 1


def split_table(table):
    high = table.astype(jnp.bfloat16)
    low = (table - high.astype(np.float64)).astype(jnp.bfloat16)
    return np.stack([high, low])


def trig(first, second):
    angle = 2.0 * np.pi / PATCH * ((first[:, None] * second[None, :]) % PATCH)
    return np.cos(angle), np.sin(angle)


def column_table():
    cosine, sine = trig(np.arange(PATCH), np.arange(HALF))
    table = np.zeros((PATCH, 2 * LANES))
    table[:, :HALF] = cosine
    table[:, LANES : LANES + HALF] = sine
    return split_table(table)


def row_table(halves, rows):
    table = np.zeros((halves, rows, 2 * ROWS_K, PATCH + HALO))
    for half in range(halves):
        halo_first = PATCH - HALO if half == 0 else 0
        position = np.concatenate([np.arange(PATCH), halo_first + np.arange(HALO)])
        cosine, sine = trig(np.arange(HALF), position)
        for row in range(rows):
            start = (half * rows + row) * STRIDE - MARGIN
            own = (np.arange(PATCH) >= start) & (np.arange(PATCH) < start + PATCH)
            offset = -PATCH if half == 0 else PATCH
            outer = halo_first + np.arange(HALO) + offset
            outer = (outer >= start) & (outer < start + PATCH)
            used = np.concatenate([own, outer])
            table[half, row, :HALF] = cosine * used
            table[half, row, ROWS_K : ROWS_K + HALF] = sine * used
    table = table.reshape(halves, rows * 2 * ROWS_K, PATCH + HALO)
    return np.stack([split_table(table[half]) for half in range(halves)])


def inverse_tables():
    cosine, sine = trig(np.arange(PATCH), np.arange(HALF))
    weight = np.full((HALF,), 2.0 / PATCH)
    weight[0] = weight[-1] = 1.0 / PATCH
    left = np.zeros((PATCH, 2 * ROWS_K))
    left[:, :HALF] = cosine * weight
    left[:, ROWS_K : ROWS_K + HALF] = -sine * weight
    right = np.zeros((2 * LANES, PATCH))
    right[:HALF] = (cosine * weight).T
    right[LANES : LANES + HALF] = -(sine * weight).T
    return split_table(left), split_table(right)


def dot(left, right):
    return jnp.dot(left, right, preferred_element_type=jnp.float32)


def halves_of(value):
    high = value.astype(jnp.bfloat16)
    return high, (value - high.astype(jnp.float32)).astype(jnp.bfloat16)


def table_first(table, value):
    high, low = halves_of(value)
    return dot(table[0], high) + dot(table[1], high) + dot(table[0], low)


def table_last(value, table):
    high, low = halves_of(value)
    return dot(high, table[0]) + dot(high, table[1]) + dot(low, table[0])


def flow_kernel(rows, columns, where_ref, own_ref, other_ref, diagonal_ref, first_ref, second_ref,
                mask_ref, column_ref, row_ref, left_ref, right_ref, out_ref, rows_ref):
    half = where_ref[0]
    odd = where_ref[1] == 1
    lane = lax.broadcasted_iota(jnp.int32, (PATCH + HALO, LANES), 1)
    wide = lax.broadcasted_iota(jnp.int32, (PATCH + HALO, PATCH), 1)
    held = []
    for image in range(2):
        tile = own_ref[0] if image == 0 else other_ref[0]
        mine = jnp.concatenate([tile, diagonal_ref[1 - image]], 0).astype(jnp.float32)
        one = first_ref[image].astype(jnp.float32)
        two = second_ref[image].astype(jnp.float32)
        before = jnp.where(odd, one, two)
        after = jnp.where(odd, two, one)
        beside = jnp.concatenate(
            [jnp.where(lane < LANES // 2, after, before), before[:, : PATCH - LANES]], 1
        )
        held.append((mine, beside))
    sign = jnp.where(half == 0, 1.0, -1.0).astype(jnp.float32)
    window_rows = 2 * ROWS_K
    count = rows * columns
    for column in range(columns):
        start = column * STRIDE - MARGIN
        inside = wide < start + PATCH if start < 0 else wide >= start
        spectra = []
        for mine, beside in held:
            pixels = jnp.where(inside, mine, beside).astype(jnp.bfloat16)
            partial = dot(pixels, column_ref[0]) + dot(pixels, column_ref[1])
            high, low = halves_of(partial)
            spectra.append(
                dot(row_ref[half, 0], high) + dot(row_ref[half, 1], high) + dot(row_ref[half, 0], low)
            )
        for row in range(rows):
            parts = []
            for spectrum_of in spectra:
                top = spectrum_of[row * window_rows : row * window_rows + ROWS_K]
                low = spectrum_of[row * window_rows + ROWS_K : (row + 1) * window_rows]
                parts.append((top[:, :LANES], top[:, LANES:], low[:, :LANES], low[:, LANES:]))
            (acc, acs, asc, ass), (bcc, bcs, bsc, bss) = parts
            even = acc * bcc + asc * bsc + acs * bcs + ass * bss
            by_row = sign * (asc * bcc - acc * bsc + ass * bcs - acs * bss)
            by_column = sign * (acs * bcc - acc * bcs + ass * bsc - asc * bss)
            both = acc * bss + ass * bcc - asc * bcs - acs * bsc
            cross = jnp.concatenate(
                [jnp.concatenate([even, by_column], 1), jnp.concatenate([by_row, both], 1)], 0
            )
            correl = table_last(table_first(left_ref, cross), right_ref)
            squared = correl * correl
            weights = squared * squared
            total = weights[:SUBLANES]
            based = jnp.zeros_like(total)
            for group in range(1, PATCH // SUBLANES):
                piece = weights[group * SUBLANES : (group + 1) * SUBLANES]
                base = group * SUBLANES
                base = base - PATCH if base >= PATCH // 2 else base
                total = total + piece
                based = based + piece * float(base)
            step = lax.broadcasted_iota(jnp.int32, (SUBLANES, PATCH), 0).astype(jnp.float32)
            based = based + step * total
            patch = row * columns + column
            rows_ref[0, pl.ds(patch, 1)] = jnp.sum(total, 0, keepdims=True)
            rows_ref[1, pl.ds(patch, 1)] = jnp.sum(based, 0, keepdims=True)
    totals = rows_ref[0]
    shift = lax.broadcasted_iota(jnp.int32, (count, PATCH), 1)
    shift = jnp.where(shift >= PATCH // 2, shift - PATCH, shift).astype(jnp.float32)
    below = jnp.sum(totals, 1, keepdims=True) + EPSILON
    flow_y = jnp.sum(rows_ref[1], 1, keepdims=True) / below
    flow_x = jnp.sum(totals * shift, 1, keepdims=True) / below
    at = lax.broadcasted_iota(jnp.int32, (count, LANES), 1)
    patch = lax.broadcasted_iota(jnp.int32, (count, LANES), 0)
    line = jnp.where(at == patch, flow_y, 0.0) + jnp.where(at == patch + count, flow_x, 0.0)
    line = jnp.sum(line, 0, keepdims=True)
    lanes = lax.broadcasted_iota(jnp.int32, (1, LANES), 1)
    mask = mask_ref[0].astype(jnp.float32)
    for row in range(mask.shape[0]):
        for column in range(columns):
            spot = 2 * count + row * columns + column
            line = jnp.where(lanes == spot, mask[row : row + 1, column : column + 1], line)
    out_ref[...] = jnp.broadcast_to(line, out_ref.shape)


def relax_kernel(rows, columns, grid_shape, where_ref, got_ref, flow_ref, offsets_ref):
    _, size_y, size_x = grid_shape
    half, at_y, at_x = where_ref[0], where_ref[2], where_ref[3]
    count = rows * columns
    tile_rows = 2 * rows
    width = columns + 2 * RADIUS
    height = tile_rows + 2 * RADIUS
    devices = got_ref.shape[0]
    lane = lax.broadcasted_iota(jnp.int32, (1, LANES), 1).astype(jnp.float32)
    line = jnp.floor((lane + 0.5) * (1.0 / width))
    across = lane - line * width
    node_y = line.astype(jnp.int32) - RADIUS + at_y * tile_rows
    node_x = across.astype(jnp.int32) - RADIUS + at_x * columns
    inside = (node_y >= 0) & (node_y < tile_rows * size_y) & (node_x >= 0)
    inside = inside & (node_x < columns * size_x) & (line < height)

    def parts(value, size):
        whole = jnp.floor((value.astype(jnp.float32) + 0.5) * (1.0 / size)).astype(jnp.int32)
        return whole, value - whole * size

    tile_y, in_y = parts(node_y, tile_rows)
    tile_x, in_x = parts(node_x, columns)
    side, in_half = parts(in_y, rows)
    tile = tile_y * size_x + tile_x
    per_section = size_y * size_x
    flow_key = jnp.where(inside, (side * per_section + tile) * count + in_half * columns + in_x, -1)
    mask_key = jnp.where(inside, tile * (2 * count) + in_y * columns + in_x, -1)
    got = got_ref[...]
    source = lax.broadcasted_iota(jnp.int32, (devices, LANES), 0)
    sums = [jnp.zeros((devices, LANES), jnp.float32) for _ in range(2)]
    for node in range(count):
        hit = source * count + node == flow_key
        for axis in range(2):
            spot = axis * count + node
            sums[axis] = sums[axis] + jnp.where(hit, got[:, spot : spot + 1], 0.0)
    masks = [jnp.zeros((per_section, LANES), jnp.float32) for _ in range(2)]
    source = source[:per_section]
    for node in range(2 * count):
        hit = source * (2 * count) + node == mask_key
        spot = 2 * count + node
        for section in range(2):
            piece = got[section * per_section : (section + 1) * per_section, spot : spot + 1]
            masks[section] = masks[section] + jnp.where(hit, piece, 0.0)
    flows = jnp.concatenate([jnp.sum(total, 0, keepdims=True) for total in sums], 0)
    weight = jnp.sum(masks[0], 0, keepdims=True) * jnp.sum(masks[1], 0, keepdims=True)
    kept = inside.astype(jnp.float32)
    upper = jnp.zeros((2, LANES), jnp.float32)
    lower = jnp.zeros((2, LANES), jnp.float32)

    def laplacian_of(value):
        left = jnp.where(across < 0.5, 0.0, pltpu.roll(value, 1, 1))
        right = jnp.where(across > width - 1.5, 0.0, pltpu.roll(value, LANES - 1, 1))
        return pltpu.roll(value, width, 1) + pltpu.roll(value, LANES - width, 1) + left + right - 4.0 * value

    for _ in range(RELAX):
        pull = weight * (upper - lower - flows)
        lower, upper = (
            (lower + STEP_SIZE * (STIFFNESS * laplacian_of(lower) + pull)) * kept,
            (upper + STEP_SIZE * (STIFFNESS * laplacian_of(upper) - pull)) * kept,
        )
    first = half == 0
    result = jnp.where(first, lower, upper)
    flows = jnp.where(first, flows, 0.0)
    flow_ref[...] = jnp.zeros_like(flow_ref)
    for row in range(tile_rows):
        start = (RADIUS + row) * width + RADIUS
        for axis in range(2):
            offsets_ref[axis, 0, pl.ds(row, 1)] = result[axis : axis + 1, start : start + columns]
            flow_ref[axis, 0, pl.ds(row, 1)] = flows[axis : axis + 1, start : start + columns]


def vmem(count):
    return [pl.BlockSpec(memory_space=pltpu.VMEM)] * count


def pair_body(images, tissue_mask):
    sections, size_y, size_x = (lax.axis_size(name) for name in ("gz", "gy", "gx"))
    count_y = images.shape[1] // STRIDE
    count_x = images.shape[2] // STRIDE
    rows = count_y // 2
    half, at_y, at_x = (lax.axis_index(name) for name in ("gz", "gy", "gx"))
    odd = at_x % 2
    where = jnp.stack([half, odd, at_y, at_x]).astype(jnp.int32)
    other = lax.ppermute(images, "gz", [(0, 1), (1, 0)])
    both = jnp.concatenate([images, other], 0)
    edge = jnp.where(half == 1, both[:, PATCH - HALO :], both[:, :HALO])
    diagonal = []
    for tile in range(1, size_y):
        diagonal += [(size_y + tile - 1, tile), (tile, size_y + tile - 1)]
    beyond = lax.ppermute(edge, ("gz", "gy"), diagonal)
    tall = jnp.concatenate([both, beyond[::-1]], 1)
    low_side = tall[:, :, :LANES]
    high_side = jnp.concatenate([tall[:, :, LANES:], tall[:, :, PATCH - LANES : LANES]], 2)
    is_odd = odd == 1
    swaps = [
        [pair for left in range(offset, size_x - 1, 2) for pair in ((left, left + 1), (left + 1, left))]
        for offset in range(2)
    ]
    first = lax.ppermute(jnp.where(is_odd, low_side, high_side), "gx", swaps[0])
    second = lax.ppermute(jnp.where(is_odd, high_side, low_side), "gx", swaps[1])
    devices = sections * size_y * size_x
    left, right = inverse_tables()
    scalars = pl.BlockSpec(memory_space=pltpu.SMEM)
    lines = pl.pallas_call(
        functools.partial(flow_kernel, rows, count_x),
        out_shape=jax.ShapeDtypeStruct((devices, LANES), jnp.float32),
        in_specs=[scalars] + vmem(10),
        out_specs=vmem(1)[0],
        scratch_shapes=[pltpu.VMEM((2, rows * count_x, PATCH), jnp.float32)],
        name="flows",
    )(
        where,
        images,
        other,
        beyond,
        first,
        second,
        tissue_mask,
        jnp.asarray(column_table()),
        jnp.asarray(row_table(2, rows)),
        jnp.asarray(left),
        jnp.asarray(right),
    )
    got = lax.all_to_all(lines, ("gz", "gy", "gx"), 0, 0, tiled=True)
    return pl.pallas_call(
        functools.partial(relax_kernel, rows, count_x, (sections, size_y, size_x)),
        out_shape=(
            jax.ShapeDtypeStruct((4, 1, count_y, count_x), jnp.float32),
            jax.ShapeDtypeStruct((2, 1, count_y, count_x), jnp.float32),
        ),
        in_specs=[scalars] + vmem(1),
        out_specs=tuple(vmem(2)),
        name="relax",
    )(where, got)


def body(images, tissue_mask):
    paired = lax.axis_size("gz") == 2 and images.shape == (1, PATCH, PATCH)
    return (pair_body if paired else general_body)(images, tissue_mask)


def solution(mesh):
    placed = (P("gz", "gy", "gx"), P("gz", "gy", "gx"))
    return jax.shard_map(
        body,
        mesh=mesh,
        in_specs=placed,
        out_specs=(P(None, "gz", "gy", "gx"), P(None, "gz", "gy", "gx")),
        check_vma=False,
    )
```

profile of v0, /device:TPU:0, one launch (start us, length us, event | category | flops | bytes accessed | tf_op | source)
XLA Modules:
  0.0 43.1 jit_solution(2931722910690462173)
XLA Ops:
  0.6 3.0 %collective-permute-start = (bf16[1,160,160]{2,1,0:T(8,128)(2,1)}, bf16[1,160,160]{2,1,0:T(8,128)(2,1)S(1)}, u32[]{:S(2)}, u32[]{:S(2)}) collective-permute-start(bf16[1,160,160]{2,1,0:T(8,128)(2,1)} %own_ref.1), channel_id=1, source_target_pairs={{0,16},{16,0},{1,17},{17,1},{2,18},{18,2},{3,19},{19,3},{4,20},{20... | collective-permute-start | bytes 153608 | tf_op jit(solution)/shard_map/ppermute | solution.py:417
  3.7 0.9 %constant_dynamic-update-slice_fusion.1 = bf16[2,160,160]{2,1,0:T(8,128)(2,1)S(1)} fusion(bf16[1,160,160]{2,1,0:T(8,128)(2,1)} %own_ref.1), kind=kLoop, calls=%fused_computation.15 | loop fusion | bytes 133120
  4.6 1.7 %collective-permute-done.other_ref = bf16[1,160,160]{2,1,0:T(8,128)(2,1)S(1)} collective-permute-done((bf16[1,160,160]{2,1,0:T(8,128)(2,1)}, bf16[1,160,160]{2,1,0:T(8,128)(2,1)S(1)}, u32[]{:S(2)}, u32[]{:S(2)}) %collective-permute-start) | collective-permute-done | bytes 51232 | tf_op jit(solution)/shard_map/ppermute | solution.py:417
  6.3 0.0 copy-start
  6.3 0.6 %copy-done = bf16[1,160,160]{2,1,0:T(8,128)(2,1)} copy-done((bf16[1,160,160]{2,1,0:T(8,128)(2,1)}, bf16[1,160,160]{2,1,0:T(8,128)(2,1)S(1)}, u32[]{:S(2)}) %copy-start) | copy-done | bytes 51224
  7.0 0.7 %collective-permute-start.1 = (bf16[2,64,160]{2,1,0:T(8,128)(2,1)S(1)}, bf16[2,64,160]{2,1,0:T(8,128)(2,1)S(1)}, u32[]{:S(2)}, u32[]{:S(2)}) collective-permute-start(bf16[2,64,160]{2,1,0:T(8,128)(2,1)S(1)} %slice_select_fusion), channel_id=1, source_target_pairs={{16,4},{4,16},{20,8},{8,20},{24,12},{12,24},{17,5},{5,17},{21,9},{... | collective-permute-start | bytes 122888 | tf_op jit(solution)/shard_map/ppermute | solution.py:423
  7.6 0.0 collective-permute-done.1.diagonal_ref
  7.7 0.0 copy-start.1
  7.7 0.6 %copy-done.1 = bf16[2,64,160]{2,1,0:T(8,128)(2,1)} copy-done((bf16[2,64,160]{2,1,0:T(8,128)(2,1)}, bf16[2,64,160]{2,1,0:T(8,128)(2,1)S(1)}, u32[]{:S(2)}) %copy-start.1) | copy-done | bytes 40984
  8.3 0.1 broadcast_select_fusion
  8.3 0.7 %collective-permute-start.3 = (bf16[2,224,128]{2,1,0:T(8,128)(2,1)S(1)}, bf16[2,224,128]{2,1,0:T(8,128)(2,1)S(1)}, u32[]{:S(2)}, u32[]{:S(2)}) collective-permute-start(bf16[2,224,128]{2,1,0:T(8,128)(2,1)S(1)} %get-tuple-element.2), channel_id=1, source_target_pairs={{1,2},{2,1},{5,6},{6,5},{9,10},{10,9},{13,14},{14,13},{17,18},{18,... | collective-permute-start | bytes 344072 | tf_op jit(solution)/shard_map/ppermute | solution.py:433
  9.0 3.4 %collective-permute-start.2 = (bf16[2,224,128]{2,1,0:T(8,128)(2,1)S(1)}, bf16[2,224,128]{2,1,0:T(8,128)(2,1)S(1)}, u32[]{:S(2)}, u32[]{:S(2)}) collective-permute-start(bf16[2,224,128]{2,1,0:T(8,128)(2,1)S(1)} %get-tuple-element.3), channel_id=1, source_target_pairs={{0,1},{1,0},{2,3},{3,2},{4,5},{5,4},{6,7},{7,6},{8,9},{9,8},{10,11... | collective-permute-start | bytes 344072 | tf_op jit(solution)/shard_map/ppermute | solution.py:432
  12.5 0.6 %pad_add_fusion.where_ref = s32[4]{0:T(128)} fusion(s32[1]{0:T(128)} %bitcast.3, s32[1]{0:T(128)} %bitcast.2, s32[1]{0:T(128)} %bitcast.1, s32[1]{0:T(128)} %bitcast), kind=kLoop, calls=%fused_computation.16 | loop fusion | flops 12 | bytes 32 | tf_op jit(solution)/shard_map/stack | solution.py:416
  13.0 0.0 collective-permute-done.3.second_ref
  13.0 0.0 copy-start.2
  13.0 0.4 collective-permute-done.2.first_ref
  13.4 0.3 copy-done.2
  13.7 0.0 copy-start.3
  13.7 0.6 %copy-done.3 = bf16[2,224,128]{2,1,0:T(8,128)(2,1)} copy-done((bf16[2,224,128]{2,1,0:T(8,128)(2,1)}, bf16[2,224,128]{2,1,0:T(8,128)(2,1)S(1)}, u32[]{:S(2)}) %copy-start.3) | copy-done | bytes 114712
  14.3 6.5 %flows.1 = f32[32,128]{1,0:T(8,128)} custom-call(s32[4]{0:T(128)} %pad_add_fusion.where_ref, bf16[1,160,160]{2,1,0:T(8,128)(2,1)} %own_ref.1, bf16[1,160,160]{2,1,0:T(8,128)(2,1)} %copy-done, bf16[2,64,160]{2,1,0:T(8,128)(2,1)} %copy-done.1, bf16[2,224,128]{2,1,0:T(8,128)(2,1)} %copy-done.3, bf16[2,224,128]{2,1,0:T(8,128)(2,1)} %copy-done.2, ...), custom_call_target="tpu_custom_call" | custom-call | tf_op jit(solution)/shard_map/flows/pallas_call | solution.py:437
  20.8 20.3 %all_to_all.11 = f32[32,1,128]{2,1,0:T(1,128)} all-to-all(f32[32,1,128]{2,1,0:T(1,128)} %bitcast.8), channel_id=1, replica_groups=mesh['gz'=2,'gy'=4,'gx'=4] {'gz','gy','gx'}, dimensions={0} | all-to-all | bytes 32768 | tf_op jit(solution)/shard_map/all_to_all | solution.py:457
  41.1 1.9 %relax.1 = (f32[4,1,4,4]{3,2,1,0:T(4,128)}, f32[2,1,4,4]{3,2,1,0:T(4,128)}) custom-call(s32[4]{0:T(128)} %pad_add_fusion.where_ref, f32[32,128]{1,0:T(8,128)} %bitcast.9), custom_call_target="tpu_custom_call" | custom-call | tf_op jit(solution)/shard_map/relax/pallas_call | solution.py:458
  (4 shorter events, 0.0 us)
Async XLA Ops:
  0.6 5.7 %collective-permute-start = (bf16[1,160,160]{2,1,0:T(8,128)(2,1)}, bf16[1,160,160]{2,1,0:T(8,128)(2,1)S(1)}, u32[]{:S(2)}, u32[]{:S(2)}) collective-permute-start(bf16[1,160,160]{2,1,0:T(8,128)(2,1)} %own_ref.1), channel_id=1, source_target_pairs={{0,16},{16,0},{1,17},{17,1},{2,18},{18,2},{3,19},{19,3},{4,20},{20... | collective-permute-start | bytes 153608 | tf_op jit(solution)/shard_map/ppermute | solution.py:417
  6.3 0.6 %copy-start = (bf16[1,160,160]{2,1,0:T(8,128)(2,1)}, bf16[1,160,160]{2,1,0:T(8,128)(2,1)S(1)}, u32[]{:S(2)}) copy-start(bf16[1,160,160]{2,1,0:T(8,128)(2,1)S(1)} %collective-permute-done.other_ref) | copy-start | bytes 153604
  7.0 0.7 %collective-permute-start.1 = (bf16[2,64,160]{2,1,0:T(8,128)(2,1)S(1)}, bf16[2,64,160]{2,1,0:T(8,128)(2,1)S(1)}, u32[]{:S(2)}, u32[]{:S(2)}) collective-permute-start(bf16[2,64,160]{2,1,0:T(8,128)(2,1)S(1)} %slice_select_fusion), channel_id=1, source_target_pairs={{16,4},{4,16},{20,8},{8,20},{24,12},{12,24},{17,5},{5,17},{21,9},{... | collective-permute-start | bytes 122888 | tf_op jit(solution)/shard_map/ppermute | solution.py:423
  7.7 0.6 %copy-start.1 = (bf16[2,64,160]{2,1,0:T(8,128)(2,1)}, bf16[2,64,160]{2,1,0:T(8,128)(2,1)S(1)}, u32[]{:S(2)}) copy-start(bf16[2,64,160]{2,1,0:T(8,128)(2,1)S(1)} %collective-permute-done.1.diagonal_ref) | copy-start | bytes 122884
  8.3 4.7 %collective-permute-start.3 = (bf16[2,224,128]{2,1,0:T(8,128)(2,1)S(1)}, bf16[2,224,128]{2,1,0:T(8,128)(2,1)S(1)}, u32[]{:S(2)}, u32[]{:S(2)}) collective-permute-start(bf16[2,224,128]{2,1,0:T(8,128)(2,1)S(1)} %get-tuple-element.2), channel_id=1, source_target_pairs={{1,2},{2,1},{5,6},{6,5},{9,10},{10,9},{13,14},{14,13},{17,18},{18,... | collective-permute-start | bytes 344072 | tf_op jit(solution)/shard_map/ppermute | solution.py:433
  9.0 4.4 %collective-permute-start.2 = (bf16[2,224,128]{2,1,0:T(8,128)(2,1)S(1)}, bf16[2,224,128]{2,1,0:T(8,128)(2,1)S(1)}, u32[]{:S(2)}, u32[]{:S(2)}) collective-permute-start(bf16[2,224,128]{2,1,0:T(8,128)(2,1)S(1)} %get-tuple-element.3), channel_id=1, source_target_pairs={{0,1},{1,0},{2,3},{3,2},{4,5},{5,4},{6,7},{7,6},{8,9},{9,8},{10,11... | collective-permute-start | bytes 344072 | tf_op jit(solution)/shard_map/ppermute | solution.py:432
  13.0 0.6 %copy-start.2 = (bf16[2,224,128]{2,1,0:T(8,128)(2,1)}, bf16[2,224,128]{2,1,0:T(8,128)(2,1)S(1)}, u32[]{:S(2)}) copy-start(bf16[2,224,128]{2,1,0:T(8,128)(2,1)S(1)} %collective-permute-done.3.second_ref) | copy-start | bytes 344068
  13.7 0.6 %copy-start.3 = (bf16[2,224,128]{2,1,0:T(8,128)(2,1)}, bf16[2,224,128]{2,1,0:T(8,128)(2,1)S(1)}, u32[]{:S(2)}) copy-start(bf16[2,224,128]{2,1,0:T(8,128)(2,1)S(1)} %collective-permute-done.2.first_ref) | copy-start | bytes 344068
where the time goes:
time: 43.3 us; the launch traced here: 43.1 us
  blocking collectives  20.3 us (47%)
  Pallas kernels  8.39 us (19%)
  starting transfers between devices  7.81 us (18%)
  local copies, waits for them, and re-layouts  3.02 us (7%)
  waiting for transfers between devices  2.12 us (5%)
  between operations  0.71 us (2%)
  other arithmetic  0.69 us (2%)
    all_to_all x1, blocking collectives, pair_body(): got = lax.all_to_all(lines, ('gz', 'gy', 'gx'), 0, 0, tiled=True)  20.3 us
    pallas_call x1, Pallas kernels, pair_body(): pl.pallas_call(functools.partial(flow_kernel, rows, count_x), out_shape=j...  6.48 us
    ppermute x1, starting transfers between devices, pair_body(): first = lax.ppermute(jnp.where(is_odd, low_side, high_side), 'gx', swaps[0])  3.44 us
    ppermute x1, starting transfers between devices, pair_body(): other = lax.ppermute(images, 'gz', [(0, 1), (1, 0)])  3.03 us
    unnamed x9, local copies, waits for them, and re-layouts  3.01 us
    pallas_call x1, Pallas kernels, pair_body(): pl.pallas_call(functools.partial(relax_kernel, rows, count_x, (sections,...  1.91 us
    ppermute x1, waiting for transfers between devices, pair_body(): other = lax.ppermute(images, 'gz', [(0, 1), (1, 0)])  1.73 us
  transfers between devices with their start and end apart: 4, of which 2 were waited for; matrix products, arithmetic and copies ran while one was open for 3% of the time, Pallas kernels for 0%

commit v1 on v0

--- a/solution.py
+++ b/solution.py
@@ -440,6 +440,7 @@
         in_specs=[scalars] + vmem(10),
         out_specs=vmem(1)[0],
         scratch_shapes=[pltpu.VMEM((2, rows * count_x, PATCH), jnp.float32)],
+        compiler_params=pltpu.CompilerParams(vmem_limit_bytes=24 * 2**20),
         name="flows",
     )(
         where,
@@ -463,6 +464,7 @@
         ),
         in_specs=[scalars] + vmem(1),
         out_specs=tuple(vmem(2)),
+        compiler_params=pltpu.CompilerParams(vmem_limit_bytes=4 * 2**20),
         name="relax",
     )(where, got)
 

time: 43.3 us -> 39.1 us (0.903)
  local copies, waits for them, and re-layouts: 3.02 us -> 0.97 us
  Pallas kernels: 8.39 us -> 6.67 us
  blocking collectives: 20.3 us -> 19.8 us
  waiting for transfers between devices: 2.12 us -> 2.62 us
  other arithmetic: 0.69 us -> 0.19 us
    unnamed x9 -> x13, local copies, waits for them, and re-layouts: 3.01 us -> 0.96 us
    pallas_call x1, Pallas kernels: 6.48 us -> 4.94 us  [pair_body(): pl.pallas_call(functools.partial(flow_kernel, rows, count_x), out_shape=j...]
    all_to_all x1, blocking collectives: 20.3 us -> 19.8 us  [pair_body(): got = lax.all_to_all(lines, ('gz', 'gy', 'gx'), 0, 0, tiled=True)]
    another operation x1, other arithmetic: 0.58 us -> 0.08 us  [pair_body(): where = jnp.stack([half, odd, at_y, at_x]).astype(jnp.int32)]
    ppermute x1, waiting for transfers between devices: 0.38 us -> 0.88 us  [pair_body(): first = lax.ppermute(jnp.where(is_odd, low_side, high_side), 'gx', swaps[0])]
where the time goes in v1:
time: 39.1 us; the launch traced here: 38.9 us
  blocking collectives  19.8 us (51%)
  starting transfers between devices  7.94 us (20%)
  Pallas kernels  6.67 us (17%)
  waiting for transfers between devices  2.62 us (7%)
  local copies, waits for them, and re-layouts  0.97 us (2%)
  between operations  0.76 us (2%)
    all_to_all x1, blocking collectives, pair_body(): got = lax.all_to_all(lines, ('gz', 'gy', 'gx'), 0, 0, tiled=True)  19.8 us
    pallas_call x1, Pallas kernels, pair_body(): pl.pallas_call(functools.partial(flow_kernel, rows, count_x), out_shape=j...  4.94 us
    ppermute x1, starting transfers between devices, pair_body(): first = lax.ppermute(jnp.where(is_odd, low_side, high_side), 'gx', swaps[0])  3.44 us
    ppermute x1, starting transfers between devices, pair_body(): other = lax.ppermute(images, 'gz', [(0, 1), (1, 0)])  3.03 us
    ppermute x1, waiting for transfers between devices, pair_body(): other = lax.ppermute(images, 'gz', [(0, 1), (1, 0)])  1.73 us
    pallas_call x1, Pallas kernels, pair_body(): pl.pallas_call(functools.partial(relax_kernel, rows, count_x, (sections,...  1.73 us
    unnamed x13, local copies, waits for them, and re-layouts  0.96 us
    ppermute x1, waiting for transfers between devices, pair_body(): first = lax.ppermute(jnp.where(is_odd, low_side, high_side), 'gx', swaps[0])  0.88 us
  transfers between devices with their start and end apart: 4, of which 2 were waited for; matrix products, arithmetic and copies ran while one was open for 3% of the time, Pallas kernels for 0%

profile of v1, /device:TPU:0, one launch (start us, length us, event | category | flops | bytes accessed | tf_op | source)
XLA Modules:
  0.0 38.9 jit_solution(18290908128281301815)
XLA Ops:
  0.6 3.0 %collective-permute-start = (bf16[1,160,160]{2,1,0:T(8,128)(2,1)}, bf16[1,160,160]{2,1,0:T(8,128)(2,1)S(1)}, u32[]{:S(2)}, u32[]{:S(2)}) collective-permute-start(bf16[1,160,160]{2,1,0:T(8,128)(2,1)} %own_ref.1), channel_id=1, source_target_pairs={{0,16},{16,0},{1,17},{17,1},{2,18},{18,2},{3,19},{19,3},{4,20},{20... | collective-permute-start | bytes 153608 | tf_op jit(solution)/shard_map/ppermute | solution.py:417
  3.7 0.9 %constant_dynamic-update-slice_fusion.1 = bf16[2,160,160]{2,1,0:T(8,128)(2,1)S(1)} fusion(bf16[1,160,160]{2,1,0:T(8,128)(2,1)} %own_ref.1), kind=kLoop, calls=%fused_computation.15 | loop fusion | bytes 133120
  4.6 0.0 copy-start
  4.6 1.7 %collective-permute-done.other_ref = bf16[1,160,160]{2,1,0:T(8,128)(2,1)S(1)} collective-permute-done((bf16[1,160,160]{2,1,0:T(8,128)(2,1)}, bf16[1,160,160]{2,1,0:T(8,128)(2,1)S(1)}, u32[]{:S(2)}, u32[]{:S(2)}) %collective-permute-start) | collective-permute-done | bytes 51232 | tf_op jit(solution)/shard_map/ppermute | solution.py:417
  6.3 0.7 %collective-permute-start.1 = (bf16[2,64,160]{2,1,0:T(8,128)(2,1)S(1)}, bf16[2,64,160]{2,1,0:T(8,128)(2,1)S(1)}, u32[]{:S(2)}, u32[]{:S(2)}) collective-permute-start(bf16[2,64,160]{2,1,0:T(8,128)(2,1)S(1)} %slice_select_fusion), channel_id=1, source_target_pairs={{16,4},{4,16},{20,8},{8,20},{24,12},{12,24},{17,5},{5,17},{21,9},{... | collective-permute-start | bytes 122888 | tf_op jit(solution)/shard_map/ppermute | solution.py:423
  7.0 0.0 collective-permute-done.1.diagonal_ref
  7.0 0.0 copy-start.4
  7.1 0.0 copy-start.1
  7.1 0.0 copy-start.2
  7.1 0.0 copy-start.3
  7.1 0.1 broadcast_select_fusion
  7.2 0.8 %collective-permute-start.3 = (bf16[2,224,128]{2,1,0:T(8,128)(2,1)S(1)}, bf16[2,224,128]{2,1,0:T(8,128)(2,1)S(1)}, u32[]{:S(2)}, u32[]{:S(2)}) collective-permute-start(bf16[2,224,128]{2,1,0:T(8,128)(2,1)S(1)} %get-tuple-element.2), channel_id=1, source_target_pairs={{1,2},{2,1},{5,6},{6,5},{9,10},{10,9},{13,14},{14,13},{17,18},{18,... | collective-permute-start | bytes 344072 | tf_op jit(solution)/shard_map/ppermute | solution.py:433
  8.0 3.4 %collective-permute-start.2 = (bf16[2,224,128]{2,1,0:T(8,128)(2,1)S(1)}, bf16[2,224,128]{2,1,0:T(8,128)(2,1)S(1)}, u32[]{:S(2)}, u32[]{:S(2)}) collective-permute-start(bf16[2,224,128]{2,1,0:T(8,128)(2,1)S(1)} %get-tuple-element.3), channel_id=1, source_target_pairs={{0,1},{1,0},{2,3},{3,2},{4,5},{5,4},{6,7},{7,6},{8,9},{9,8},{10,11... | collective-permute-start | bytes 344072 | tf_op jit(solution)/shard_map/ppermute | solution.py:432
  11.5 0.0 copy-start.5
  11.5 0.1 pad_add_fusion.where_ref
  11.5 0.0 collective-permute-done.3.second_ref
  11.5 0.9 %collective-permute-done.2.first_ref = bf16[2,224,128]{2,1,0:T(8,128)(2,1)S(1)} collective-permute-done((bf16[2,224,128]{2,1,0:T(8,128)(2,1)S(1)}, bf16[2,224,128]{2,1,0:T(8,128)(2,1)S(1)}, u32[]{:S(2)}, u32[]{:S(2)}) %collective-permute-start.2) | collective-permute-done | bytes 114720 | tf_op jit(solution)/shard_map/ppermute | solution.py:432
  12.4 0.0 copy-done
  12.4 0.0 copy-done.4
  12.4 0.0 copy-done.1
  12.4 0.0 copy-done.2
  12.4 0.0 copy-done.3
  12.5 0.0 copy-done.5
  12.5 4.9 %flows.1 = f32[32,128]{1,0:T(8,128)S(1)} custom-call(s32[4]{0:T(128)S(1)} %pad_add_fusion.where_ref, bf16[1,160,160]{2,1,0:T(8,128)(2,1)S(1)} %copy-done.1, bf16[1,160,160]{2,1,0:T(8,128)(2,1)S(1)} %collective-permute-done.other_ref, bf16[2,64,160]{2,1,0:T(8,128)(2,1)S(1)} %collective-permute-done.1.diagonal_ref, ...), custom_call_target="tpu_custom_call" | custom-call | tf_op jit(solution)/shard_map/flows/pallas_call | solution.py:437
  17.4 19.8 %all_to_all.11 = f32[32,1,128]{2,1,0:T(1,128)S(1)} all-to-all(f32[32,1,128]{2,1,0:T(1,128)S(1)} %bitcast.8), channel_id=1, replica_groups=mesh['gz'=2,'gy'=4,'gx'=4] {'gz','gy','gx'}, dimensions={0} | all-to-all | bytes 32768 | tf_op jit(solution)/shard_map/all_to_all | solution.py:458
  37.2 1.7 %relax.1 = (f32[4,1,4,4]{3,2,1,0:T(4,128)}, f32[2,1,4,4]{3,2,1,0:T(4,128)}) custom-call(s32[4]{0:T(128)S(1)} %pad_add_fusion.where_ref, f32[32,128]{1,0:T(8,128)S(1)} %bitcast.9), custom_call_target="tpu_custom_call" | custom-call | tf_op jit(solution)/shard_map/relax/pallas_call | solution.py:459
  (4 shorter events, 0.0 us)
Async XLA Ops:
  0.6 5.7 %collective-permute-start = (bf16[1,160,160]{2,1,0:T(8,128)(2,1)}, bf16[1,160,160]{2,1,0:T(8,128)(2,1)S(1)}, u32[]{:S(2)}, u32[]{:S(2)}) collective-permute-start(bf16[1,160,160]{2,1,0:T(8,128)(2,1)} %own_ref.1), channel_id=1, source_target_pairs={{0,16},{16,0},{1,17},{17,1},{2,18},{18,2},{3,19},{19,3},{4,20},{20... | collective-permute-start | bytes 153608 | tf_op jit(solution)/shard_map/ppermute | solution.py:417
  4.6 7.8 %copy-start = (bf16[2,2,352,224]{3,2,1,0:T(8,128)(2,1)S(1)}, bf16[2,2,352,224]{3,2,1,0:T(8,128)(2,1)}, u32[]{:S(2)}) copy-start(bf16[2,2,352,224]{3,2,1,0:T(8,128)(2,1)} %constant.36.clone.row_ref) | copy-start | bytes 1892356
  6.3 0.7 %collective-permute-start.1 = (bf16[2,64,160]{2,1,0:T(8,128)(2,1)S(1)}, bf16[2,64,160]{2,1,0:T(8,128)(2,1)S(1)}, u32[]{:S(2)}, u32[]{:S(2)}) collective-permute-start(bf16[2,64,160]{2,1,0:T(8,128)(2,1)S(1)} %slice_select_fusion), channel_id=1, source_target_pairs={{16,4},{4,16},{20,8},{8,20},{24,12},{12,24},{17,5},{5,17},{21,9},{... | collective-permute-start | bytes 122888 | tf_op jit(solution)/shard_map/ppermute | solution.py:423
  7.0 5.4 %copy-start.4 = (bf16[2,160,256]{2,1,0:T(8,128)(2,1)S(1)}, bf16[2,160,256]{2,1,0:T(8,128)(2,1)}, u32[]{:S(2)}) copy-start(bf16[2,160,256]{2,1,0:T(8,128)(2,1)} %constant.35.clone.column_ref) | copy-start | bytes 491524
  7.1 5.3 %copy-start.1 = (bf16[1,160,160]{2,1,0:T(8,128)(2,1)S(1)}, bf16[1,160,160]{2,1,0:T(8,128)(2,1)}, u32[]{:S(2)}) copy-start(bf16[1,160,160]{2,1,0:T(8,128)(2,1)} %own_ref.1) | copy-start | bytes 153604
  7.1 5.3 %copy-start.2 = (bf16[2,256,160]{2,1,0:T(8,128)(2,1)S(1)}, bf16[2,256,160]{2,1,0:T(8,128)(2,1)}, u32[]{:S(2)}) copy-start(bf16[2,256,160]{2,1,0:T(8,128)(2,1)} %constant.38.clone.right_ref) | copy-start | bytes 491524
  7.1 5.3 %copy-start.3 = (bf16[2,160,176]{2,1,0:T(8,128)(2,1)S(1)}, bf16[2,160,176]{2,1,0:T(8,128)(2,1)}, u32[]{:S(2)}) copy-start(bf16[2,160,176]{2,1,0:T(8,128)(2,1)} %constant.37.clone.left_ref) | copy-start | bytes 337924
  7.2 4.3 %collective-permute-start.3 = (bf16[2,224,128]{2,1,0:T(8,128)(2,1)S(1)}, bf16[2,224,128]{2,1,0:T(8,128)(2,1)S(1)}, u32[]{:S(2)}, u32[]{:S(2)}) collective-permute-start(bf16[2,224,128]{2,1,0:T(8,128)(2,1)S(1)} %get-tuple-element.2), channel_id=1, source_target_pairs={{1,2},{2,1},{5,6},{6,5},{9,10},{10,9},{13,14},{14,13},{17,18},{18,... | collective-permute-start | bytes 344072 | tf_op jit(solution)/shard_map/ppermute | solution.py:433
  8.0 4.4 %collective-permute-start.2 = (bf16[2,224,128]{2,1,0:T(8,128)(2,1)S(1)}, bf16[2,224,128]{2,1,0:T(8,128)(2,1)S(1)}, u32[]{:S(2)}, u32[]{:S(2)}) collective-permute-start(bf16[2,224,128]{2,1,0:T(8,128)(2,1)S(1)} %get-tuple-element.3), channel_id=1, source_target_pairs={{0,1},{1,0},{2,3},{3,2},{4,5},{5,4},{6,7},{7,6},{8,9},{9,8},{10,11... | collective-permute-start | bytes 344072 | tf_op jit(solution)/shard_map/ppermute | solution.py:432
  11.5 1.0 %copy-start.5 = (s32[1,4,4]{2,1,0:T(4,128)S(1)}, s32[1,4,4]{2,1,0:T(4,128)}, u32[]{:S(2)}) copy-start(s32[1,4,4]{2,1,0:T(4,128)} %mask_ref.1) | copy-start | bytes 196

commit v2 on v1

--- a/solution.py
+++ b/solution.py
@@ -250,33 +250,31 @@
     return dot(high, table[0]) + dot(high, table[1]) + dot(low, table[0])
 
 
-def flow_kernel(rows, columns, where_ref, own_ref, other_ref, diagonal_ref, first_ref, second_ref,
-                mask_ref, column_ref, row_ref, left_ref, right_ref, out_ref, rows_ref):
+def flow_kernel(rows, columns, late, where_ref, own_ref, other_ref, diagonal_ref, beside_ref,
+                before_ref, column_ref, row_ref, left_ref, right_ref, out_ref, rows_ref):
     half = where_ref[0]
-    odd = where_ref[1] == 1
-    lane = lax.broadcasted_iota(jnp.int32, (PATCH + HALO, LANES), 1)
-    wide = lax.broadcasted_iota(jnp.int32, (PATCH + HALO, PATCH), 1)
+    side = where_ref[1] if late else 1 - where_ref[1]
+    lane = lax.broadcasted_iota(jnp.int32, (PATCH + HALO, PATCH), 1)
+    group = columns // 2
+    base = side * group
     held = []
     for image in range(2):
         tile = own_ref[0] if image == 0 else other_ref[0]
         mine = jnp.concatenate([tile, diagonal_ref[1 - image]], 0).astype(jnp.float32)
-        one = first_ref[image].astype(jnp.float32)
-        two = second_ref[image].astype(jnp.float32)
-        before = jnp.where(odd, one, two)
-        after = jnp.where(odd, two, one)
-        beside = jnp.concatenate(
-            [jnp.where(lane < LANES // 2, after, before), before[:, : PATCH - LANES]], 1
-        )
-        held.append((mine, beside))
+        halo = beside_ref[image].astype(jnp.float32)
+        halo = jnp.concatenate([halo, halo[:, : PATCH - LANES]], 1)
+        held.append((mine, halo))
     sign = jnp.where(half == 0, 1.0, -1.0).astype(jnp.float32)
     window_rows = 2 * ROWS_K
-    count = rows * columns
-    for column in range(columns):
-        start = column * STRIDE - MARGIN
-        inside = wide < start + PATCH if start < 0 else wide >= start
+    count = rows * group
+    for column in range(group):
+        start = (base + column) * STRIDE - MARGIN
+        low_lane = jnp.where(side == 0, 0, start)
+        high_lane = jnp.where(side == 0, start + PATCH, PATCH)
+        inside = (lane >= low_lane) & (lane < high_lane)
         spectra = []
-        for mine, beside in held:
-            pixels = jnp.where(inside, mine, beside).astype(jnp.bfloat16)
+        for mine, halo in held:
+            pixels = jnp.where(inside, mine, halo).astype(jnp.bfloat16)
             partial = dot(pixels, column_ref[0]) + dot(pixels, column_ref[1])
             high, low = halves_of(partial)
             spectra.append(
@@ -301,15 +299,15 @@
             weights = squared * squared
             total = weights[:SUBLANES]
             based = jnp.zeros_like(total)
-            for group in range(1, PATCH // SUBLANES):
-                piece = weights[group * SUBLANES : (group + 1) * SUBLANES]
-                base = group * SUBLANES
-                base = base - PATCH if base >= PATCH // 2 else base
+            for piece_at in range(1, PATCH // SUBLANES):
+                piece = weights[piece_at * SUBLANES : (piece_at + 1) * SUBLANES]
+                shift = piece_at * SUBLANES
+                shift = shift - PATCH if shift >= PATCH // 2 else shift
                 total = total + piece
-                based = based + piece * float(base)
+                based = based + piece * float(shift)
             step = lax.broadcasted_iota(jnp.int32, (SUBLANES, PATCH), 0).astype(jnp.float32)
             based = based + step * total
-            patch = row * columns + column
+            patch = row * group + column
             rows_ref[0, pl.ds(patch, 1)] = jnp.sum(total, 0, keepdims=True)
             rows_ref[1, pl.ds(patch, 1)] = jnp.sum(based, 0, keepdims=True)
     totals = rows_ref[0]
@@ -320,14 +318,18 @@
     flow_x = jnp.sum(totals * shift, 1, keepdims=True) / below
     at = lax.broadcasted_iota(jnp.int32, (count, LANES), 1)
     patch = lax.broadcasted_iota(jnp.int32, (count, LANES), 0)
-    line = jnp.where(at == patch, flow_y, 0.0) + jnp.where(at == patch + count, flow_x, 0.0)
+    spot = patch + group * (patch >= group).astype(jnp.int32) + base
+    line = jnp.where(at == spot, flow_y, 0.0) + jnp.where(at == spot + 2 * count, flow_x, 0.0)
     line = jnp.sum(line, 0, keepdims=True)
-    lanes = lax.broadcasted_iota(jnp.int32, (1, LANES), 1)
-    mask = mask_ref[0].astype(jnp.float32)
-    for row in range(mask.shape[0]):
-        for column in range(columns):
-            spot = 2 * count + row * columns + column
-            line = jnp.where(lanes == spot, mask[row : row + 1, column : column + 1], line)
+    if late:
+        line = line + before_ref[...]
+    else:
+        lanes = lax.broadcasted_iota(jnp.int32, (1, LANES), 1)
+        mask = before_ref[0].astype(jnp.float32)
+        for row in range(mask.shape[0]):
+            for column in range(columns):
+                spot = 4 * count + row * columns + column
+                line = jnp.where(lanes == spot, mask[row : row + 1, column : column + 1], line)
     out_ref[...] = jnp.broadcast_to(line, out_ref.shape)
 
 
@@ -434,27 +436,24 @@
     devices = sections * size_y * size_x
     left, right = inverse_tables()
     scalars = pl.BlockSpec(memory_space=pltpu.SMEM)
-    lines = pl.pallas_call(
-        functools.partial(flow_kernel, rows, count_x),
-        out_shape=jax.ShapeDtypeStruct((devices, LANES), jnp.float32),
-        in_specs=[scalars] + vmem(10),
-        out_specs=vmem(1)[0],
-        scratch_shapes=[pltpu.VMEM((2, rows * count_x, PATCH), jnp.float32)],
-        compiler_params=pltpu.CompilerParams(vmem_limit_bytes=24 * 2**20),
-        name="flows",
-    )(
-        where,
-        images,
-        other,
-        beyond,
-        first,
-        second,
-        tissue_mask,
-        jnp.asarray(column_table()),
-        jnp.asarray(row_table(2, rows)),
-        jnp.asarray(left),
-        jnp.asarray(right),
-    )
+    tables = [jnp.asarray(column_table()), jnp.asarray(row_table(2, rows)), jnp.asarray(left), jnp.asarray(right)]
+
+    def flows(late, beside, before, lines):
+        patches = rows * count_x // 2
+        return pl.pallas_call(
+            functools.partial(flow_kernel, rows, count_x, late),
+            out_shape=jax.ShapeDtypeStruct((lines, LANES), jnp.float32),
+            in_specs=[scalars] + vmem(9),
+            out_specs=vmem(1)[0],
+            scratch_shapes=[pltpu.VMEM((2, patches, PATCH), jnp.float32)],
+            compiler_params=pltpu.CompilerParams(vmem_limit_bytes=16 * 2**20),
+            cost_estimate=pl.CostEstimate(
+                flops=patches * 2 * 2400 * 256 * 256, bytes_accessed=2**21, transcendentals=0
+            ),
+            name="flows",
+        )(where, images, other, beyond, beside, before, *tables)
+
+    lines = flows(True, second, flows(False, first, tissue_mask, 1), devices)
     got = lax.all_to_all(lines, ("gz", "gy", "gx"), 0, 0, tiled=True)
     return pl.pallas_call(
         functools.partial(relax_kernel, rows, count_x, (sections, size_y, size_x)),

time: 39.1 us -> 37.4 us (0.957)
  starting transfers between devices: 7.94 us -> 4.43 us
  Pallas kernels: 6.67 us -> 7.92 us
  blocking collectives: 19.8 us -> 20.5 us
    ppermute x1, starting transfers between devices: 3.44 us -> 0.07 us  [pair_body(): first = lax.ppermute(jnp.where(is_odd, low_side, high_side), 'gx', swaps[0])]
    pallas_call x1 -> x2, Pallas kernels: 4.94 us -> 6.19 us  [flows(): pl.pallas_call(functools.partial(flow_kernel, rows, count_x, late), out_s...]
    all_to_all x1, blocking collectives: 19.8 us -> 20.5 us  [pair_body(): got = lax.all_to_all(lines, ('gz', 'gy', 'gx'), 0, 0, tiled=True)]
  transfers between devices with their start and end apart: 4 -> 4, of which waited for: 2 -> 2; matrix products, arithmetic and copies ran while one was open for 3% -> 3% of each run, Pallas kernels for 0% -> 8%
where the time goes in v2:
time: 37.4 us; the launch traced here: 37.2 us
  blocking collectives  20.5 us (55%)
  Pallas kernels  7.92 us (21%)
  starting transfers between devices  4.43 us (12%)
  waiting for transfers between devices  2.29 us (6%)
  local copies, waits for them, and re-layouts  0.98 us (3%)
  between operations  0.81 us (2%)
    all_to_all x1, blocking collectives, pair_body(): got = lax.all_to_all(lines, ('gz', 'gy', 'gx'), 0, 0, tiled=True)  20.5 us
    pallas_call x2, Pallas kernels, flows(): pl.pallas_call(functools.partial(flow_kernel, rows, count_x, late), out_s...  6.19 us
    ppermute x1, starting transfers between devices, pair_body(): other = lax.ppermute(images, 'gz', [(0, 1), (1, 0)])  3.03 us
    ppermute x1, waiting for transfers between devices, pair_body(): other = lax.ppermute(images, 'gz', [(0, 1), (1, 0)])  1.73 us
    pallas_call x1, Pallas kernels, pair_body(): pl.pallas_call(functools.partial(relax_kernel, rows, count_x, (sections,...  1.73 us
    unnamed x13, local copies, waits for them, and re-layouts  0.97 us
  transfers between devices with their start and end apart: 4, of which 2 were waited for; matrix products, arithmetic and copies ran while one was open for 3% of the time, Pallas kernels for 8%

profile of v2, /device:TPU:0, one launch (start us, length us, event | category | flops | bytes accessed | tf_op | source)
XLA Modules:
  0.0 37.2 jit_solution(15997149344142816172)
XLA Ops:
  0.6 3.0 %collective-permute-start = (bf16[1,160,160]{2,1,0:T(8,128)(2,1)}, bf16[1,160,160]{2,1,0:T(8,128)(2,1)S(1)}, u32[]{:S(2)}, u32[]{:S(2)}) collective-permute-start(bf16[1,160,160]{2,1,0:T(8,128)(2,1)} %own_ref.3), channel_id=1, source_target_pairs={{0,16},{16,0},{1,17},{17,1},{2,18},{18,2},{3,19},{19,3},{4,20},{20... | collective-permute-start | bytes 153608 | tf_op jit(solution)/shard_map/ppermute | solution.py:419
  3.7 0.9 %constant_dynamic-update-slice_fusion.1 = bf16[2,160,160]{2,1,0:T(8,128)(2,1)S(1)} fusion(bf16[1,160,160]{2,1,0:T(8,128)(2,1)} %own_ref.3), kind=kLoop, calls=%fused_computation.12 | loop fusion | bytes 133120
  4.6 1.7 %collective-permute-done.other_ref = bf16[1,160,160]{2,1,0:T(8,128)(2,1)S(1)} collective-permute-done((bf16[1,160,160]{2,1,0:T(8,128)(2,1)}, bf16[1,160,160]{2,1,0:T(8,128)(2,1)S(1)}, u32[]{:S(2)}, u32[]{:S(2)}) %collective-permute-start) | collective-permute-done | bytes 51232 | tf_op jit(solution)/shard_map/ppermute | solution.py:419
  6.3 0.7 %collective-permute-start.1 = (bf16[2,64,160]{2,1,0:T(8,128)(2,1)S(1)}, bf16[2,64,160]{2,1,0:T(8,128)(2,1)S(1)}, u32[]{:S(2)}, u32[]{:S(2)}) collective-permute-start(bf16[2,64,160]{2,1,0:T(8,128)(2,1)S(1)} %slice_select_fusion), channel_id=1, source_target_pairs={{16,4},{4,16},{20,8},{8,20},{24,12},{12,24},{17,5},{5,17},{21,9},{... | collective-permute-start | bytes 122888 | tf_op jit(solution)/shard_map/ppermute | solution.py:425
  7.0 0.0 collective-permute-done.1.diagonal_ref
  7.0 0.0 copy-start.2
  7.1 0.1 fusion
  7.2 0.0 copy-start
  7.2 0.0 copy-start.3
  7.2 0.0 copy-start.4
  7.2 0.0 copy-start.5
  7.3 0.1 broadcast_select_fusion
  7.4 0.1 collective-permute-start.3
  7.5 0.0 copy-start.1
  7.5 0.1 pad_add_fusion.where_ref
  7.6 0.7 %collective-permute-start.2 = (bf16[2,224,128]{2,1,0:T(8,128)(2,1)S(1)}, bf16[2,224,128]{2,1,0:T(8,128)(2,1)S(1)}, u32[]{:S(2)}, u32[]{:S(2)}) collective-permute-start(bf16[2,224,128]{2,1,0:T(8,128)(2,1)S(1)} %get-tuple-element.3), channel_id=1, source_target_pairs={{1,2},{2,1},{5,6},{6,5},{9,10},{10,9},{13,14},{14,13},{17,18},{18,... | collective-permute-start | bytes 344072 | tf_op jit(solution)/shard_map/ppermute | solution.py:435
  8.2 0.6 %collective-permute-done.3.beside_ref = bf16[2,224,128]{2,1,0:T(8,128)(2,1)S(1)} collective-permute-done((bf16[2,224,128]{2,1,0:T(8,128)(2,1)S(1)}, bf16[2,224,128]{2,1,0:T(8,128)(2,1)S(1)}, u32[]{:S(2)}, u32[]{:S(2)}) %collective-permute-start.3) | collective-permute-done | bytes 114720 | tf_op jit(solution)/shard_map/ppermute | solution.py:434
  8.8 0.0 copy-done.2
  8.8 0.0 copy-done
  8.8 0.0 copy-done.3
  8.8 0.0 copy-done.4
  8.8 0.0 copy-done.5
  8.8 0.0 copy-done.1
  8.8 3.1 %flows.2.before_ref = f32[1,128]{1,0:T(1,128)S(1)} custom-call(s32[4]{0:T(128)S(1)} %pad_add_fusion.where_ref, bf16[1,160,160]{2,1,0:T(8,128)(2,1)S(1)} %copy-done, bf16[1,160,160]{2,1,0:T(8,128)(2,1)S(1)} %collective-permute-done.other_ref, bf16[2,64,160]{2,1,0:T(8,128)(2,1)S(1)} %collective-permute-done.1.diagonal_ref, ...), custom_call_target="tpu_custom_call" | custom-call | flops 1258291200 | bytes 2097152 | tf_op jit(solution)/shard_map/flows/pallas_call | solution.py:443
  11.9 0.0 collective-permute-done.2.beside_ref
  11.9 3.1 %flows.3 = f32[32,128]{1,0:T(8,128)S(1)} custom-call(s32[4]{0:T(128)S(1)} %pad_add_fusion.where_ref, bf16[1,160,160]{2,1,0:T(8,128)(2,1)S(1)} %copy-done, bf16[1,160,160]{2,1,0:T(8,128)(2,1)S(1)} %collective-permute-done.other_ref, bf16[2,64,160]{2,1,0:T(8,128)(2,1)S(1)} %collective-permute-done.1.diagonal_ref, ...), custom_call_target="tpu_custom_call" | custom-call | flops 1258291200 | bytes 2097152 | tf_op jit(solution)/shard_map/flows/pallas_call | solution.py:443
  15.0 20.5 %all_to_all.11 = f32[32,1,128]{2,1,0:T(1,128)S(1)} all-to-all(f32[32,1,128]{2,1,0:T(1,128)S(1)} %bitcast.9), channel_id=1, replica_groups=mesh['gz'=2,'gy'=4,'gx'=4] {'gz','gy','gx'}, dimensions={0} | all-to-all | bytes 32768 | tf_op jit(solution)/shard_map/all_to_all | solution.py:457
  35.5 1.7 %relax.1 = (f32[4,1,4,4]{3,2,1,0:T(4,128)}, f32[2,1,4,4]{3,2,1,0:T(4,128)}) custom-call(s32[4]{0:T(128)S(1)} %pad_add_fusion.where_ref, f32[32,128]{1,0:T(8,128)S(1)} %bitcast.8), custom_call_target="tpu_custom_call" | custom-call | tf_op jit(solution)/shard_map/relax/pallas_call | solution.py:458
  (4 shorter events, 0.0 us)
Async XLA Ops:
  0.6 5.7 %collective-permute-start = (bf16[1,160,160]{2,1,0:T(8,128)(2,1)}, bf16[1,160,160]{2,1,0:T(8,128)(2,1)S(1)}, u32[]{:S(2)}, u32[]{:S(2)}) collective-permute-start(bf16[1,160,160]{2,1,0:T(8,128)(2,1)} %own_ref.3), channel_id=1, source_target_pairs={{0,16},{16,0},{1,17},{17,1},{2,18},{18,2},{3,19},{19,3},{4,20},{20... | collective-permute-start | bytes 153608 | tf_op jit(solution)/shard_map/ppermute | solution.py:419
  6.3 0.7 %collective-permute-start.1 = (bf16[2,64,160]{2,1,0:T(8,128)(2,1)S(1)}, bf16[2,64,160]{2,1,0:T(8,128)(2,1)S(1)}, u32[]{:S(2)}, u32[]{:S(2)}) collective-permute-start(bf16[2,64,160]{2,1,0:T(8,128)(2,1)S(1)} %slice_select_fusion), channel_id=1, source_target_pairs={{16,4},{4,16},{20,8},{8,20},{24,12},{12,24},{17,5},{5,17},{21,9},{... | collective-permute-start | bytes 122888 | tf_op jit(solution)/shard_map/ppermute | solution.py:425
  7.0 1.7 %copy-start.2 = (bf16[2,2,352,224]{3,2,1,0:T(8,128)(2,1)S(1)}, bf16[2,2,352,224]{3,2,1,0:T(8,128)(2,1)}, u32[]{:S(2)}) copy-start(bf16[2,2,352,224]{3,2,1,0:T(8,128)(2,1)} %constant.36.clone.row_ref) | copy-start | bytes 1892356
  7.2 1.6 %copy-start = (bf16[1,160,160]{2,1,0:T(8,128)(2,1)S(1)}, bf16[1,160,160]{2,1,0:T(8,128)(2,1)}, u32[]{:S(2)}) copy-start(bf16[1,160,160]{2,1,0:T(8,128)(2,1)} %own_ref.3) | copy-start | bytes 153604
  7.2 1.6 %copy-start.3 = (bf16[2,256,160]{2,1,0:T(8,128)(2,1)S(1)}, bf16[2,256,160]{2,1,0:T(8,128)(2,1)}, u32[]{:S(2)}) copy-start(bf16[2,256,160]{2,1,0:T(8,128)(2,1)} %constant.38.clone.right_ref) | copy-start | bytes 491524
  7.2 1.6 %copy-start.4 = (bf16[2,160,176]{2,1,0:T(8,128)(2,1)S(1)}, bf16[2,160,176]{2,1,0:T(8,128)(2,1)}, u32[]{:S(2)}) copy-start(bf16[2,160,176]{2,1,0:T(8,128)(2,1)} %constant.37.clone.left_ref) | copy-start | bytes 337924
  7.2 1.6 %copy-start.5 = (bf16[2,160,256]{2,1,0:T(8,128)(2,1)S(1)}, bf16[2,160,256]{2,1,0:T(8,128)(2,1)}, u32[]{:S(2)}) copy-start(bf16[2,160,256]{2,1,0:T(8,128)(2,1)} %constant.35.clone.column_ref) | copy-start | bytes 491524
  7.4 1.4 %collective-permute-start.3 = (bf16[2,224,128]{2,1,0:T(8,128)(2,1)S(1)}, bf16[2,224,128]{2,1,0:T(8,128)(2,1)S(1)}, u32[]{:S(2)}, u32[]{:S(2)}) collective-permute-start(bf16[2,224,128]{2,1,0:T(8,128)(2,1)S(1)} %get-tuple-element.2), channel_id=1, source_target_pairs={{0,1},{1,0},{2,3},{3,2},{4,5},{5,4},{6,7},{7,6},{8,9},{9,8},{10,11... | collective-permute-start | bytes 344072 | tf_op jit(solution)/shard_map/ppermute | solution.py:434
  7.5 1.3 %copy-start.1 = (s32[1,4,4]{2,1,0:T(4,128)S(1)}, s32[1,4,4]{2,1,0:T(4,128)}, u32[]{:S(2)}) copy-start(s32[1,4,4]{2,1,0:T(4,128)} %before_ref.1) | copy-start | bytes 196
  7.6 4.4 %collective-permute-start.2 = (bf16[2,224,128]{2,1,0:T(8,128)(2,1)S(1)}, bf16[2,224,128]{2,1,0:T(8,128)(2,1)S(1)}, u32[]{:S(2)}, u32[]{:S(2)}) collective-permute-start(bf16[2,224,128]{2,1,0:T(8,128)(2,1)S(1)} %get-tuple-element.3), channel_id=1, source_target_pairs={{1,2},{2,1},{5,6},{6,5},{9,10},{10,9},{13,14},{14,13},{17,18},{18,... | collective-permute-start | bytes 344072 | tf_op jit(solution)/shard_map/ppermute | solution.py:435

commit v3 on v2

--- a/solution.py
+++ b/solution.py
@@ -175,9 +175,13 @@
 HALF = PATCH // 2 + 1
 LANES = 128
 SUBLANES = 8
-ROWS_K = -(-HALF // SUBLANES) * SUBLANES
+BAND = HALF - 1
 HALO = -(-MARGIN // 16) * 16
 RADIUS = RELAX - 1
+STEP_ROWS = (PATCH - MARGIN, MARGIN - STRIDE)
+STEP_HELD = STRIDE + SUBLANES
+TOP_CUT = PATCH - HALO
+LOW_CUT = HALO - SUBLANES
 
 
 def split_table(table):
@@ -199,36 +203,37 @@
     return split_table(table)
 
 
-def row_table(halves, rows):
-    table = np.zeros((halves, rows, 2 * ROWS_K, PATCH + HALO))
-    for half in range(halves):
-        halo_first = PATCH - HALO if half == 0 else 0
-        position = np.concatenate([np.arange(PATCH), halo_first + np.arange(HALO)])
-        cosine, sine = trig(np.arange(HALF), position)
-        for row in range(rows):
-            start = (half * rows + row) * STRIDE - MARGIN
-            own = (np.arange(PATCH) >= start) & (np.arange(PATCH) < start + PATCH)
-            offset = -PATCH if half == 0 else PATCH
-            outer = halo_first + np.arange(HALO) + offset
-            outer = (outer >= start) & (outer < start + PATCH)
-            used = np.concatenate([own, outer])
-            table[half, row, :HALF] = cosine * used
-            table[half, row, ROWS_K : ROWS_K + HALF] = sine * used
-    table = table.reshape(halves, rows * 2 * ROWS_K, PATCH + HALO)
-    return np.stack([split_table(table[half]) for half in range(halves)])
+def stacked(table):
+    high, low = split_table(table)
+    return np.concatenate([high, low, high], 1)
+
+
+def frequency_rows(positions):
+    cosine, sine = trig(np.arange(HALF), positions)
+    return np.concatenate([cosine[:BAND], cosine[BAND:], sine[1:BAND]], 0)
+
+
+def row_tables():
+    whole = stacked(frequency_rows(np.arange(PATCH)))
+    changes = []
+    for half in range(2):
+        first = (STEP_ROWS[half] // SUBLANES) * SUBLANES
+        positions = first + np.arange(STEP_HELD)
+        used = (positions >= STEP_ROWS[half]) & (positions < STEP_ROWS[half] + STRIDE)
+        changes.append(stacked(frequency_rows(positions) * used))
+    return whole, np.stack(changes)
 
 
 def inverse_tables():
     cosine, sine = trig(np.arange(PATCH), np.arange(HALF))
     weight = np.full((HALF,), 2.0 / PATCH)
     weight[0] = weight[-1] = 1.0 / PATCH
-    left = np.zeros((PATCH, 2 * ROWS_K))
-    left[:, :HALF] = cosine * weight
-    left[:, ROWS_K : ROWS_K + HALF] = -sine * weight
+    cosine, sine = cosine * weight, sine * weight
+    left = np.concatenate([cosine[:, :BAND], cosine[:, BAND:], -sine[:, 1:BAND]], 1)
     right = np.zeros((2 * LANES, PATCH))
-    right[:HALF] = (cosine * weight).T
-    right[LANES : LANES + HALF] = -(sine * weight).T
-    return split_table(left), split_table(right)
+    right[:HALF] = cosine.T
+    right[LANES : LANES + HALF] = -sine.T
+    return stacked(left), split_table(right)
 
 
 def dot(left, right):
@@ -242,74 +247,121 @@
 
 def table_first(table, value):
     high, low = halves_of(value)
-    return dot(table[0], high) + dot(table[1], high) + dot(table[0], low)
-
-
-def table_last(value, table):
-    high, low = halves_of(value)
-    return dot(high, table[0]) + dot(high, table[1]) + dot(low, table[0])
-
-
-def flow_kernel(rows, columns, late, where_ref, own_ref, other_ref, diagonal_ref, beside_ref,
-                before_ref, column_ref, row_ref, left_ref, right_ref, out_ref, rows_ref):
-    half = where_ref[0]
-    side = where_ref[1] if late else 1 - where_ref[1]
-    lane = lax.broadcasted_iota(jnp.int32, (PATCH + HALO, PATCH), 1)
+    return dot(table, jnp.concatenate([high, high, low], 0))
+
+
+def cross_spectrum(first, second, sign):
+    (acc, acs, asc, ass), (bcc, bcs, bsc, bss) = (
+        (value[:BAND, :LANES], value[:BAND, LANES:], value[BAND:, :LANES], value[BAND:, LANES:])
+        for value in (first, second)
+    )
+    even_0 = acc * bcc + acs * bcs
+    even_1 = asc * bsc + ass * bss
+    column_0 = acs * bcc - acc * bcs
+    column_1 = ass * bsc - asc * bss
+    by_row = sign * (asc * bcc - acc * bsc + ass * bcs - acs * bss)
+    both = acc * bss + ass * bcc - asc * bcs - acs * bsc
+    top = SUBLANES
+    lone = lax.broadcasted_iota(jnp.int32, (top, LANES), 0) == 0
+
+    def with_top(usual, single):
+        return jnp.concatenate([jnp.where(lone, single[:top], usual[:top]), usual[top:]], 0)
+
+    even = with_top(even_0 + even_1, even_0)
+    by_row = with_top(by_row, even_1)
+    by_column = sign * with_top(column_0 + column_1, column_0)
+    both = with_top(both, sign * column_1[:top])
+    return jnp.concatenate(
+        [jnp.concatenate([even, by_column], 1), jnp.concatenate([by_row, both], 1)], 0
+    )
+
+
+def flow_kernel(columns, late, own_ref, other_ref, diagonal_ref, beside_ref, before_ref, column_ref,
+                whole_ref, change_ref, left_ref, right_ref, out_ref, pixel_ref, partial_ref,
+                high_ref, low_ref, rows_ref):
+    half = lax.axis_index("gz")
+    odd = lax.rem(lax.axis_index("gx"), 2)
+    side = odd if late else 1 - odd
+    held = PATCH + HALO
+    lane = lax.broadcasted_iota(jnp.int32, (held, PATCH), 1)
     group = columns // 2
     base = side * group
-    held = []
     for image in range(2):
         tile = own_ref[0] if image == 0 else other_ref[0]
         mine = jnp.concatenate([tile, diagonal_ref[1 - image]], 0).astype(jnp.float32)
         halo = beside_ref[image].astype(jnp.float32)
         halo = jnp.concatenate([halo, halo[:, : PATCH - LANES]], 1)
-        held.append((mine, halo))
+        for column in range(group):
+            start = (base + column) * STRIDE - MARGIN
+            low_lane = jnp.where(side == 0, 0, start)
+            high_lane = jnp.where(side == 0, start + PATCH, PATCH)
+            inside = (lane >= low_lane) & (lane < high_lane)
+            spot = (2 * column + image) * held
+            pixel_ref[spot : spot + held] = jnp.where(inside, mine, halo).astype(jnp.bfloat16)
+    pixels = pixel_ref[...]
+    partial_ref[...] = dot(pixels, column_ref[0]) + dot(pixels, column_ref[1])
     sign = jnp.where(half == 0, 1.0, -1.0).astype(jnp.float32)
-    window_rows = 2 * ROWS_K
-    count = rows * group
+    upper = half == 0
+    inner = lax.broadcasted_iota(jnp.int32, (SUBLANES, 2 * LANES), 0) < PATCH - MARGIN - TOP_CUT
     for column in range(group):
-        start = (base + column) * STRIDE - MARGIN
-        low_lane = jnp.where(side == 0, 0, start)
-        high_lane = jnp.where(side == 0, start + PATCH, PATCH)
-        inside = (lane >= low_lane) & (lane < high_lane)
         spectra = []
-        for mine, halo in held:
-            pixels = jnp.where(inside, mine, halo).astype(jnp.bfloat16)
-            partial = dot(pixels, column_ref[0]) + dot(pixels, column_ref[1])
-            high, low = halves_of(partial)
-            spectra.append(
-                dot(row_ref[half, 0], high) + dot(row_ref[half, 1], high) + dot(row_ref[half, 0], low)
+        for image in range(2):
+            spot = (2 * column + image) * held
+            halo_spot = spot + PATCH
+
+            def rows_at(upper_start, lower_start, size):
+                start = pl.multiple_of(jnp.where(upper, upper_start, lower_start), SUBLANES)
+                return partial_ref[pl.ds(start, size)]
+
+            low_mix = jnp.where(
+                inner & (half == 1),
+                partial_ref[halo_spot + LOW_CUT : halo_spot + HALO],
+                partial_ref[spot + LOW_CUT : spot + HALO],
             )
-        for row in range(rows):
-            parts = []
-            for spectrum_of in spectra:
-                top = spectrum_of[row * window_rows : row * window_rows + ROWS_K]
-                low = spectrum_of[row * window_rows + ROWS_K : (row + 1) * window_rows]
-                parts.append((top[:, :LANES], top[:, LANES:], low[:, :LANES], low[:, LANES:]))
-            (acc, acs, asc, ass), (bcc, bcs, bsc, bss) = parts
-            even = acc * bcc + asc * bsc + acs * bcs + ass * bss
-            by_row = sign * (asc * bcc - acc * bsc + ass * bcs - acs * bss)
-            by_column = sign * (acs * bcc - acc * bcs + ass * bsc - asc * bss)
-            both = acc * bss + ass * bcc - asc * bcs - acs * bsc
-            cross = jnp.concatenate(
-                [jnp.concatenate([even, by_column], 1), jnp.concatenate([by_row, both], 1)], 0
+            top_mix = jnp.where(
+                inner | (half == 1),
+                partial_ref[spot + TOP_CUT : spot + TOP_CUT + SUBLANES],
+                partial_ref[halo_spot : halo_spot + SUBLANES],
             )
-            correl = table_last(table_first(left_ref, cross), right_ref)
-            squared = correl * correl
-            weights = squared * squared
-            total = weights[:SUBLANES]
-            based = jnp.zeros_like(total)
-            for piece_at in range(1, PATCH // SUBLANES):
-                piece = weights[piece_at * SUBLANES : (piece_at + 1) * SUBLANES]
-                shift = piece_at * SUBLANES
-                shift = shift - PATCH if shift >= PATCH // 2 else shift
-                total = total + piece
-                based = based + piece * float(shift)
-            step = lax.broadcasted_iota(jnp.int32, (SUBLANES, PATCH), 0).astype(jnp.float32)
-            based = based + step * total
-            patch = row * group + column
-            rows_ref[0, pl.ds(patch, 1)] = jnp.sum(total, 0, keepdims=True)
-            rows_ref[1, pl.ds(patch, 1)] = jnp.sum(based, 0, keepdims=True)
+            window = jnp.concatenate(
+                [
+                    rows_at(spot, halo_spot, LOW_CUT),
+                    low_mix,
+                    partial_ref[spot + HALO : spot + TOP_CUT],
+                    top_mix,
+                    rows_at(halo_spot + SUBLANES, spot + TOP_CUT + SUBLANES, HALO - SUBLANES),
+                ],
+                0,
+            )
+            change = rows_at(spot + TOP_CUT, spot + HALO - STEP_HELD, STEP_HELD)
+            change = change - rows_at(halo_spot, halo_spot + HALO - STEP_HELD, STEP_HELD)
+            near = table_first(whole_ref[...], window)
+            spectra.append((near, near + table_first(change_ref[half], change)))
+        for row in range(2):
+            cross = cross_spectrum(spectra[0][row], spectra[1][row], sign)
+            high, low = halves_of(table_first(left_ref[...], cross))
+            spot = (row * group + column) * PATCH
+            high_ref[spot : spot + PATCH] = high
+            low_ref[spot : spot + PATCH] = low
+    correl = dot(high_ref[...], right_ref[0]) + dot(high_ref[...], right_ref[1])
+    correl = correl + dot(low_ref[...], right_ref[0])
+    count = 2 * group
+    for patch in range(count):
+        squared = correl[patch * PATCH : (patch + 1) * PATCH]
+        squared = squared * squared
+        weights = squared * squared
+        total = weights[:SUBLANES]
+        based = jnp.zeros_like(total)
+        for piece_at in range(1, PATCH // SUBLANES):
+            piece = weights[piece_at * SUBLANES : (piece_at + 1) * SUBLANES]
+            shift = piece_at * SUBLANES
+            shift = shift - PATCH if shift >= PATCH // 2 else shift
+            total = total + piece
+            based = based + piece * float(shift)
+        step = lax.broadcasted_iota(jnp.int32, (SUBLANES, PATCH), 0).astype(jnp.float32)
+        based = based + step * total
+        rows_ref[0, pl.ds(patch, 1)] = jnp.sum(total, 0, keepdims=True)
+        rows_ref[1, pl.ds(patch, 1)] = jnp.sum(based, 0, keepdims=True)
     totals = rows_ref[0]
     shift = lax.broadcasted_iota(jnp.int32, (count, PATCH), 1)
     shift = jnp.where(shift >= PATCH // 2, shift - PATCH, shift).astype(jnp.float32)
@@ -318,7 +370,9 @@
     flow_x = jnp.sum(totals * shift, 1, keepdims=True) / below
     at = lax.broadcasted_iota(jnp.int32, (count, LANES), 1)
     patch = lax.broadcasted_iota(jnp.int32, (count, LANES), 0)
-    spot = patch + group * (patch >= group).astype(jnp.int32) + base
+    second_row = (patch >= group).astype(jnp.int32)
+    row = jnp.where(upper, second_row, 1 - second_row)
+    spot = patch - group * second_row + columns * row + base
     line = jnp.where(at == spot, flow_y, 0.0) + jnp.where(at == spot + 2 * count, flow_x, 0.0)
     line = jnp.sum(line, 0, keepdims=True)
     if late:
@@ -333,14 +387,14 @@
     out_ref[...] = jnp.broadcast_to(line, out_ref.shape)
 
 
-def relax_kernel(rows, columns, grid_shape, where_ref, got_ref, flow_ref, offsets_ref):
-    _, size_y, size_x = grid_shape
-    half, at_y, at_x = where_ref[0], where_ref[2], where_ref[3]
+def relax_kernel(rows, columns, got_ref, flow_ref, offsets_ref):
+    size_y, size_x = lax.axis_size("gy"), lax.axis_size("gx")
+    half, at_y, at_x = lax.axis_index("gz"), lax.axis_index("gy"), lax.axis_index("gx")
     count = rows * columns
     tile_rows = 2 * rows
     width = columns + 2 * RADIUS
     height = tile_rows + 2 * RADIUS
-    devices = got_ref.shape[0]
+    per_section = size_y * size_x
     lane = lax.broadcasted_iota(jnp.int32, (1, LANES), 1).astype(jnp.float32)
     line = jnp.floor((lane + 0.5) * (1.0 / width))
     across = lane - line * width
@@ -356,52 +410,54 @@
     tile_y, in_y = parts(node_y, tile_rows)
     tile_x, in_x = parts(node_x, columns)
     side, in_half = parts(in_y, rows)
-    tile = tile_y * size_x + tile_x
-    per_section = size_y * size_x
-    flow_key = jnp.where(inside, (side * per_section + tile) * count + in_half * columns + in_x, -1)
-    mask_key = jnp.where(inside, tile * (2 * count) + in_y * columns + in_x, -1)
-    got = got_ref[...]
-    source = lax.broadcasted_iota(jnp.int32, (devices, LANES), 0)
-    sums = [jnp.zeros((devices, LANES), jnp.float32) for _ in range(2)]
-    for node in range(count):
-        hit = source * count + node == flow_key
-        for axis in range(2):
-            spot = axis * count + node
-            sums[axis] = sums[axis] + jnp.where(hit, got[:, spot : spot + 1], 0.0)
-    masks = [jnp.zeros((per_section, LANES), jnp.float32) for _ in range(2)]
-    source = source[:per_section]
-    for node in range(2 * count):
-        hit = source * (2 * count) + node == mask_key
-        spot = 2 * count + node
-        for section in range(2):
-            piece = got[section * per_section : (section + 1) * per_section, spot : spot + 1]
-            masks[section] = masks[section] + jnp.where(hit, piece, 0.0)
-    flows = jnp.concatenate([jnp.sum(total, 0, keepdims=True) for total in sums], 0)
-    weight = jnp.sum(masks[0], 0, keepdims=True) * jnp.sum(masks[1], 0, keepdims=True)
+    tile = jnp.where(inside, tile_y * size_x + tile_x, -1)
+    flow_spot = in_half * columns + in_x
+    spots = jnp.concatenate([flow_spot, flow_spot + count, 2 * count + in_y * columns + in_x], 1)
+    picked = lax.broadcasted_iota(jnp.int32, (LANES, 3 * LANES), 0) == spots
+    picker = picked.astype(jnp.float32).astype(jnp.bfloat16)
+    rest = got_ref[...]
+    spread = jnp.zeros((rest.shape[0], 3 * LANES), jnp.float32)
+    for _ in range(3):
+        piece = rest.astype(jnp.bfloat16)
+        rest = rest - piece.astype(jnp.float32)
+        spread = spread + dot(piece, picker)
+    source = lax.broadcasted_iota(jnp.int32, (2 * per_section, LANES), 0)
+    chosen = source == side * per_section + tile
+    chosen = chosen & (tile >= 0)
+    flow_y, flow_x = (
+        jnp.sum(jnp.where(chosen, spread[:, axis * LANES : (axis + 1) * LANES], 0.0), 0, keepdims=True)
+        for axis in range(2)
+    )
+    chosen = source[:per_section] == tile
+    mask_0, mask_1 = (
+        jnp.sum(jnp.where(chosen, spread[start : start + per_section, 2 * LANES :], 0.0), 0, keepdims=True)
+        for start in (0, per_section)
+    )
+    flows = jnp.concatenate([flow_y, flow_x], 0)
+    weight = mask_0 * mask_1
     kept = inside.astype(jnp.float32)
-    upper = jnp.zeros((2, LANES), jnp.float32)
-    lower = jnp.zeros((2, LANES), jnp.float32)
-
-    def laplacian_of(value):
-        left = jnp.where(across < 0.5, 0.0, pltpu.roll(value, 1, 1))
-        right = jnp.where(across > width - 1.5, 0.0, pltpu.roll(value, LANES - 1, 1))
-        return pltpu.roll(value, width, 1) + pltpu.roll(value, LANES - width, 1) + left + right - 4.0 * value
-
-    for _ in range(RELAX):
-        pull = weight * (upper - lower - flows)
-        lower, upper = (
-            (lower + STEP_SIZE * (STIFFNESS * laplacian_of(lower) + pull)) * kept,
-            (upper + STEP_SIZE * (STIFFNESS * laplacian_of(upper) - pull)) * kept,
-        )
+    sign = jnp.where(lax.broadcasted_iota(jnp.int32, (4, LANES), 0) < 2, 1.0, -1.0)
+    weight = weight * sign
+    offsets = jnp.zeros((4, LANES), jnp.float32)
+    for step in range(RELAX):
+        lower, upper = offsets[:2], offsets[2:]
+        pull = upper - lower - flows
+        forces = weight * jnp.concatenate([pull, pull], 0)
+        if step:
+            left = jnp.where(across < 0.5, 0.0, pltpu.roll(offsets, 1, 1))
+            right = jnp.where(across > width - 1.5, 0.0, pltpu.roll(offsets, LANES - 1, 1))
+            laplace = pltpu.roll(offsets, width, 1) + pltpu.roll(offsets, LANES - width, 1)
+            forces = STIFFNESS * (laplace + left + right - 4.0 * offsets) + forces
+        offsets = (offsets + STEP_SIZE * forces) * kept
     first = half == 0
-    result = jnp.where(first, lower, upper)
+    result = jnp.where(first, offsets[:2], offsets[2:])
     flows = jnp.where(first, flows, 0.0)
-    flow_ref[...] = jnp.zeros_like(flow_ref)
     for row in range(tile_rows):
         start = (RADIUS + row) * width + RADIUS
         for axis in range(2):
             offsets_ref[axis, 0, pl.ds(row, 1)] = result[axis : axis + 1, start : start + columns]
             flow_ref[axis, 0, pl.ds(row, 1)] = flows[axis : axis + 1, start : start + columns]
+    flow_ref[2:] = jnp.zeros((flow_ref.shape[0] - 2, *flow_ref.shape[1:]), jnp.float32)
 
 
 def vmem(count):
@@ -413,9 +469,8 @@
     count_y = images.shape[1] // STRIDE
     count_x = images.shape[2] // STRIDE
     rows = count_y // 2
-    half, at_y, at_x = (lax.axis_index(name) for name in ("gz", "gy", "gx"))
-    odd = at_x % 2
-    where = jnp.stack([half, odd, at_y, at_x]).astype(jnp.int32)
+    half = lax.axis_index("gz")
+    is_odd = lax.axis_index("gx") % 2 == 1
     other = lax.ppermute(images, "gz", [(0, 1), (1, 0)])
     both = jnp.concatenate([images, other], 0)
     edge = jnp.where(half == 1, both[:, PATCH - HALO :], both[:, :HALO])
@@ -426,7 +481,6 @@
     tall = jnp.concatenate([both, beyond[::-1]], 1)
     low_side = tall[:, :, :LANES]
     high_side = jnp.concatenate([tall[:, :, LANES:], tall[:, :, PATCH - LANES : LANES]], 2)
-    is_odd = odd == 1
     swaps = [
         [pair for left in range(offset, size_x - 1, 2) for pair in ((left, left + 1), (left + 1, left))]
         for offset in range(2)
@@ -434,38 +488,43 @@
     first = lax.ppermute(jnp.where(is_odd, low_side, high_side), "gx", swaps[0])
     second = lax.ppermute(jnp.where(is_odd, high_side, low_side), "gx", swaps[1])
     devices = sections * size_y * size_x
-    left, right = inverse_tables()
-    scalars = pl.BlockSpec(memory_space=pltpu.SMEM)
-    tables = [jnp.asarray(column_table()), jnp.asarray(row_table(2, rows)), jnp.asarray(left), jnp.asarray(right)]
+    tables = [jnp.asarray(table) for table in (column_table(), *row_tables(), *inverse_tables())]
 
     def flows(late, beside, before, lines):
-        patches = rows * count_x // 2
+        patches = count_x
+        held = PATCH + HALO
         return pl.pallas_call(
-            functools.partial(flow_kernel, rows, count_x, late),
+            functools.partial(flow_kernel, count_x, late),
             out_shape=jax.ShapeDtypeStruct((lines, LANES), jnp.float32),
-            in_specs=[scalars] + vmem(9),
+            in_specs=vmem(10),
             out_specs=vmem(1)[0],
-            scratch_shapes=[pltpu.VMEM((2, patches, PATCH), jnp.float32)],
+            scratch_shapes=[
+                pltpu.VMEM((patches * held, PATCH), jnp.bfloat16),
+                pltpu.VMEM((patches * held, 2 * LANES), jnp.float32),
+                pltpu.VMEM((patches * PATCH, 2 * LANES), jnp.bfloat16),
+                pltpu.VMEM((patches * PATCH, 2 * LANES), jnp.bfloat16),
+                pltpu.VMEM((2, patches, PATCH), jnp.float32),
+            ],
             compiler_params=pltpu.CompilerParams(vmem_limit_bytes=16 * 2**20),
             cost_estimate=pl.CostEstimate(
                 flops=patches * 2 * 2400 * 256 * 256, bytes_accessed=2**21, transcendentals=0
             ),
             name="flows",
-        )(where, images, other, beyond, beside, before, *tables)
+        )(images, other, beyond, beside, before, *tables)
 
     lines = flows(True, second, flows(False, first, tissue_mask, 1), devices)
     got = lax.all_to_all(lines, ("gz", "gy", "gx"), 0, 0, tiled=True)
     return pl.pallas_call(
-        functools.partial(relax_kernel, rows, count_x, (sections, size_y, size_x)),
+        functools.partial(relax_kernel, rows, count_x),
         out_shape=(
             jax.ShapeDtypeStruct((4, 1, count_y, count_x), jnp.float32),
             jax.ShapeDtypeStruct((2, 1, count_y, count_x), jnp.float32),
         ),
-        in_specs=[scalars] + vmem(1),
+        in_specs=vmem(1),
         out_specs=tuple(vmem(2)),
         compiler_params=pltpu.CompilerParams(vmem_limit_bytes=4 * 2**20),
         name="relax",
-    )(where, got)
+    )(got)
 
 
 def body(images, tissue_mask):

time: 37.4 us -> 35.8 us (0.957)
  Pallas kernels: 7.92 us -> 5.38 us
  blocking collectives: 20.5 us -> 21.4 us
    pallas_call x3, Pallas kernels: 7.92 us -> 5.38 us  [the longest x2 4.26 us: flows(): pl.pallas_call(functools.partial(flow_kernel, count_x, late), out_shape=j...]
    all_to_all x1, blocking collectives: 20.5 us -> 21.4 us  [pair_body(): got = lax.all_to_all(lines, ('gz', 'gy', 'gx'), 0, 0, tiled=True)]
    unnamed x13 -> x15, local copies, waits for them, and re-layouts: 0.97 us -> 0.97 us
  transfers between devices with their start and end apart: 4 -> 4, of which waited for: 2 -> 2; matrix products, arithmetic and copies ran while one was open for 3% -> 3% of each run, Pallas kernels for 8% -> 6%
where the time goes in v3:
time: 35.8 us; the launch traced here: 35.6 us
  blocking collectives  21.4 us (60%)
  Pallas kernels  5.38 us (15%)
  starting transfers between devices  4.44 us (12%)
  waiting for transfers between devices  2.37 us (7%)
  local copies, waits for them, and re-layouts  0.99 us (3%)
  between operations  0.82 us (2%)
    all_to_all x1, blocking collectives, pair_body(): got = lax.all_to_all(lines, ('gz', 'gy', 'gx'), 0, 0, tiled=True)  21.4 us
    pallas_call x2, Pallas kernels, flows(): pl.pallas_call(functools.partial(flow_kernel, count_x, late), out_shape=j...  4.26 us
    ppermute x1, starting transfers between devices, pair_body(): other = lax.ppermute(images, 'gz', [(0, 1), (1, 0)])  3.03 us
    ppermute x1, waiting for transfers between devices, pair_body(): other = lax.ppermute(images, 'gz', [(0, 1), (1, 0)])  1.73 us
    pallas_call x1, Pallas kernels, pair_body(): pl.pallas_call(functools.partial(relax_kernel, rows, count_x), out_shape=...  1.12 us
    unnamed x15, local copies, waits for them, and re-layouts  0.97 us
  transfers between devices with their start and end apart: 4, of which 2 were waited for; matrix products, arithmetic and copies ran while one was open for 3% of the time, Pallas kernels for 6%

profile of v3, /device:TPU:0, one launch (start us, length us, event | category | flops | bytes accessed | tf_op | source)
XLA Modules:
  0.0 35.6 jit_solution(18429507652643350527)
XLA Ops:
  0.6 3.0 %collective-permute-start = (bf16[1,160,160]{2,1,0:T(8,128)(2,1)}, bf16[1,160,160]{2,1,0:T(8,128)(2,1)S(1)}, u32[]{:S(2)}, u32[]{:S(2)}) collective-permute-start(bf16[1,160,160]{2,1,0:T(8,128)(2,1)} %own_ref.3), channel_id=1, source_target_pairs={{0,16},{16,0},{1,17},{17,1},{2,18},{18,2},{3,19},{19,3},{4,20},{20... | collective-permute-start | bytes 153608 | tf_op jit(solution)/shard_map/ppermute | solution.py:474
  3.7 0.9 %constant_dynamic-update-slice_fusion.1 = bf16[2,160,160]{2,1,0:T(8,128)(2,1)S(1)} fusion(bf16[1,160,160]{2,1,0:T(8,128)(2,1)} %own_ref.3), kind=kLoop, calls=%fused_computation.12 | loop fusion | bytes 133120
  4.6 1.7 %collective-permute-done.other_ref = bf16[1,160,160]{2,1,0:T(8,128)(2,1)S(1)} collective-permute-done((bf16[1,160,160]{2,1,0:T(8,128)(2,1)}, bf16[1,160,160]{2,1,0:T(8,128)(2,1)S(1)}, u32[]{:S(2)}, u32[]{:S(2)}) %collective-permute-start) | collective-permute-done | bytes 51232 | tf_op jit(solution)/shard_map/ppermute | solution.py:474
  6.3 0.7 %collective-permute-start.1 = (bf16[2,64,160]{2,1,0:T(8,128)(2,1)S(1)}, bf16[2,64,160]{2,1,0:T(8,128)(2,1)S(1)}, u32[]{:S(2)}, u32[]{:S(2)}) collective-permute-start(bf16[2,64,160]{2,1,0:T(8,128)(2,1)S(1)} %slice_select_fusion), channel_id=1, source_target_pairs={{16,4},{4,16},{20,8},{8,20},{24,12},{12,24},{17,5},{5,17},{21,9},{... | collective-permute-start | bytes 122888 | tf_op jit(solution)/shard_map/ppermute | solution.py:480
  7.0 0.0 collective-permute-done.1.diagonal_ref
  7.1 0.0 copy-start.5
  7.1 0.0 copy-start.6
  7.1 0.1 fusion
  7.2 0.0 copy-start
  7.2 0.0 copy-start.2
  7.2 0.0 copy-start.3
  7.3 0.0 copy-start.4
  7.3 0.1 broadcast_select_fusion
  7.4 0.0 copy-start.1
  7.4 0.1 collective-permute-start.3
  7.5 0.7 %collective-permute-start.2 = (bf16[2,224,128]{2,1,0:T(8,128)(2,1)S(1)}, bf16[2,224,128]{2,1,0:T(8,128)(2,1)S(1)}, u32[]{:S(2)}, u32[]{:S(2)}) collective-permute-start(bf16[2,224,128]{2,1,0:T(8,128)(2,1)S(1)} %get-tuple-element.3), channel_id=1, source_target_pairs={{1,2},{2,1},{5,6},{6,5},{9,10},{10,9},{13,14},{14,13},{17,18},{18,... | collective-permute-start | bytes 344072 | tf_op jit(solution)/shard_map/ppermute | solution.py:489
  8.2 0.6 %collective-permute-done.3.beside_ref = bf16[2,224,128]{2,1,0:T(8,128)(2,1)S(1)} collective-permute-done((bf16[2,224,128]{2,1,0:T(8,128)(2,1)S(1)}, bf16[2,224,128]{2,1,0:T(8,128)(2,1)S(1)}, u32[]{:S(2)}, u32[]{:S(2)}) %collective-permute-start.3) | collective-permute-done | bytes 114720 | tf_op jit(solution)/shard_map/ppermute | solution.py:488
  8.8 0.0 copy-done.5
  8.8 0.0 copy-done.6
  8.8 0.0 copy-done
  8.8 0.0 copy-done.2
  8.8 0.0 copy-done.3
  8.8 0.0 copy-done.4
  8.9 0.0 copy-done.1
  8.9 2.1 %flows.2.before_ref = f32[1,128]{1,0:T(1,128)S(1)} custom-call(bf16[1,160,160]{2,1,0:T(8,128)(2,1)S(1)} %copy-done, bf16[1,160,160]{2,1,0:T(8,128)(2,1)S(1)} %collective-permute-done.other_ref, bf16[2,64,160]{2,1,0:T(8,128)(2,1)S(1)} %collective-permute-done.1.diagonal_ref, bf16[2,224,128]{2,1,0:T(8,128)(2,1)S(1)} %collective-permute-done.3.beside_ref, ...), custom_call_target="tpu_custom_call" | custom-call | flops 1258291200 | bytes 2097152 | tf_op jit(solution)/shard_map/flows/pallas_call | solution.py:496
  11.0 0.0 collective-permute-done.2.beside_ref
  11.0 2.1 %flows.3 = f32[32,128]{1,0:T(8,128)S(1)} custom-call(bf16[1,160,160]{2,1,0:T(8,128)(2,1)S(1)} %copy-done, bf16[1,160,160]{2,1,0:T(8,128)(2,1)S(1)} %collective-permute-done.other_ref, bf16[2,64,160]{2,1,0:T(8,128)(2,1)S(1)} %collective-permute-done.1.diagonal_ref, bf16[2,224,128]{2,1,0:T(8,128)(2,1)S(1)} %collective-permute-done.2.beside_ref, ...), custom_call_target="tpu_custom_call" | custom-call | flops 1258291200 | bytes 2097152 | tf_op jit(solution)/shard_map/flows/pallas_call | solution.py:496
  13.1 21.4 %all_to_all.11 = f32[32,1,128]{2,1,0:T(1,128)S(1)} all-to-all(f32[32,1,128]{2,1,0:T(1,128)S(1)} %bitcast.5), channel_id=1, replica_groups=mesh['gz'=2,'gy'=4,'gx'=4] {'gz','gy','gx'}, dimensions={0} | all-to-all | bytes 32768 | tf_op jit(solution)/shard_map/all_to_all | solution.py:516
  34.5 1.1 %relax.1 = (f32[4,1,4,4]{3,2,1,0:T(4,128)}, f32[2,1,4,4]{3,2,1,0:T(4,128)}) custom-call(f32[32,128]{1,0:T(8,128)S(1)} %bitcast.4), custom_call_target="tpu_custom_call" | custom-call | tf_op jit(solution)/shard_map/relax/pallas_call | solution.py:517
  (4 shorter events, 0.0 us)
Async XLA Ops:
  0.6 5.7 %collective-permute-start = (bf16[1,160,160]{2,1,0:T(8,128)(2,1)}, bf16[1,160,160]{2,1,0:T(8,128)(2,1)S(1)}, u32[]{:S(2)}, u32[]{:S(2)}) collective-permute-start(bf16[1,160,160]{2,1,0:T(8,128)(2,1)} %own_ref.3), channel_id=1, source_target_pairs={{0,16},{16,0},{1,17},{17,1},{2,18},{18,2},{3,19},{19,3},{4,20},{20... | collective-permute-start | bytes 153608 | tf_op jit(solution)/shard_map/ppermute | solution.py:474
  6.3 0.7 %collective-permute-start.1 = (bf16[2,64,160]{2,1,0:T(8,128)(2,1)S(1)}, bf16[2,64,160]{2,1,0:T(8,128)(2,1)S(1)}, u32[]{:S(2)}, u32[]{:S(2)}) collective-permute-start(bf16[2,64,160]{2,1,0:T(8,128)(2,1)S(1)} %slice_select_fusion), channel_id=1, source_target_pairs={{16,4},{4,16},{20,8},{8,20},{24,12},{12,24},{17,5},{5,17},{21,9},{... | collective-permute-start | bytes 122888 | tf_op jit(solution)/shard_map/ppermute | solution.py:480
  7.1 1.7 %copy-start.5 = (bf16[160,480]{1,0:T(8,128)(2,1)S(1)}, bf16[160,480]{1,0:T(8,128)(2,1)}, u32[]{:S(2)}) copy-start(bf16[160,480]{1,0:T(8,128)(2,1)} %constant.35.clone.whole_ref) | copy-start | bytes 460804
  7.1 1.7 %copy-start.6 = (bf16[2,160,256]{2,1,0:T(8,128)(2,1)S(1)}, bf16[2,160,256]{2,1,0:T(8,128)(2,1)}, u32[]{:S(2)}) copy-start(bf16[2,160,256]{2,1,0:T(8,128)(2,1)} %constant.34.clone.column_ref) | copy-start | bytes 491524
  7.2 1.6 %copy-start = (bf16[1,160,160]{2,1,0:T(8,128)(2,1)S(1)}, bf16[1,160,160]{2,1,0:T(8,128)(2,1)}, u32[]{:S(2)}) copy-start(bf16[1,160,160]{2,1,0:T(8,128)(2,1)} %own_ref.3) | copy-start | bytes 153604
  7.2 1.6 %copy-start.2 = (bf16[2,256,160]{2,1,0:T(8,128)(2,1)S(1)}, bf16[2,256,160]{2,1,0:T(8,128)(2,1)}, u32[]{:S(2)}) copy-start(bf16[2,256,160]{2,1,0:T(8,128)(2,1)} %constant.38.clone.right_ref) | copy-start | bytes 491524
  7.2 1.6 %copy-start.3 = (bf16[160,480]{1,0:T(8,128)(2,1)S(1)}, bf16[160,480]{1,0:T(8,128)(2,1)}, u32[]{:S(2)}) copy-start(bf16[160,480]{1,0:T(8,128)(2,1)} %constant.37.clone.left_ref) | copy-start | bytes 460804
  7.3 1.6 %copy-start.4 = (bf16[2,160,144]{2,1,0:T(8,128)(2,1)S(1)}, bf16[2,160,144]{2,1,0:T(8,128)(2,1)}, u32[]{:S(2)}) copy-start(bf16[2,160,144]{2,1,0:T(8,128)(2,1)} %constant.36.clone.change_ref) | copy-start | bytes 276484
  7.4 1.4 %copy-start.1 = (s32[1,4,4]{2,1,0:T(4,128)S(1)}, s32[1,4,4]{2,1,0:T(4,128)}, u32[]{:S(2)}) copy-start(s32[1,4,4]{2,1,0:T(4,128)} %before_ref.1) | copy-start | bytes 196
  7.4 1.4 %collective-permute-start.3 = (bf16[2,224,128]{2,1,0:T(8,128)(2,1)S(1)}, bf16[2,224,128]{2,1,0:T(8,128)(2,1)S(1)}, u32[]{:S(2)}, u32[]{:S(2)}) collective-permute-start(bf16[2,224,128]{2,1,0:T(8,128)(2,1)S(1)} %get-tuple-element.2), channel_id=1, source_target_pairs={{0,1},{1,0},{2,3},{3,2},{4,5},{5,4},{6,7},{7,6},{8,9},{9,8},{10,11... | collective-permute-start | bytes 344072 | tf_op jit(solution)/shard_map/ppermute | solution.py:488
  7.5 3.5 %collective-permute-start.2 = (bf16[2,224,128]{2,1,0:T(8,128)(2,1)S(1)}, bf16[2,224,128]{2,1,0:T(8,128)(2,1)S(1)}, u32[]{:S(2)}, u32[]{:S(2)}) collective-permute-start(bf16[2,224,128]{2,1,0:T(8,128)(2,1)S(1)} %get-tuple-element.3), channel_id=1, source_target_pairs={{1,2},{2,1},{5,6},{6,5},{9,10},{10,9},{13,14},{14,13},{17,18},{18,... | collective-permute-start | bytes 344072 | tf_op jit(solution)/shard_map/ppermute | solution.py:489

commit v4 on v3

--- a/solution.py
+++ b/solution.py
@@ -178,6 +178,7 @@
 BAND = HALF - 1
 HALO = -(-MARGIN // 16) * 16
 RADIUS = RELAX - 1
+WIDE = 2 * LANES
 STEP_ROWS = (PATCH - MARGIN, MARGIN - STRIDE)
 STEP_HELD = STRIDE + SUBLANES
 TOP_CUT = PATCH - HALO
@@ -236,6 +237,20 @@
     return stacked(left), split_table(right)
 
 
+def all_tables():
+    column = column_table()
+    whole, change = row_tables()
+    left, right = inverse_tables()
+    blocks = [(column[0], column[1]), (whole,), (left,), (change[0], change[1]), (right[0], right[1])]
+    rows = []
+    for parts in blocks:
+        block = np.zeros((parts[0].shape[0], 2 * WIDE), jnp.bfloat16)
+        for at, part in enumerate(parts):
+            block[:, at * WIDE : at * WIDE + part.shape[1]] = part
+        rows.append(block)
+    return np.concatenate(rows, 0)
+
+
 def dot(left, right):
     return jnp.dot(left, right, preferred_element_type=jnp.float32)
 
@@ -276,9 +291,44 @@
     )
 
 
-def flow_kernel(columns, late, own_ref, other_ref, diagonal_ref, beside_ref, before_ref, column_ref,
-                whole_ref, change_ref, left_ref, right_ref, out_ref, pixel_ref, partial_ref,
-                high_ref, low_ref, rows_ref):
+def load_kernel(own_ref, table_ref, own_out, table_out, done):
+    copies = [
+        pltpu.make_async_copy(source, target, done.at[at])
+        for at, (source, target) in enumerate([(own_ref, own_out), (table_ref, table_out)])
+    ]
+    for copy in copies:
+        copy.start()
+    for copy in copies:
+        copy.wait()
+
+
+def edge_kernel(own_ref, other_ref, out_ref):
+    start = pl.multiple_of(jnp.where(lax.axis_index("gz") == 0, PATCH - HALO, 0), HALO // 2)
+    out_ref[0] = own_ref[0, pl.ds(start, HALO)]
+    out_ref[1] = other_ref[0, pl.ds(start, HALO)]
+
+
+def pack_kernel(own_ref, other_ref, beyond_ref, first_ref, second_ref):
+    wide, narrow = [], []
+    for image in range(2):
+        tile = own_ref[0] if image == 0 else other_ref[0]
+        tall = jnp.concatenate([tile, beyond_ref[image]], 0).astype(jnp.float32)
+        wide.append(tall[:, :LANES])
+        narrow.append(jnp.concatenate([tall[:, LANES:]] * (LANES // (PATCH - LANES)), 1))
+    lane = lax.broadcasted_iota(jnp.int32, wide[0].shape, 1)
+    middle = LANES // 2
+    extra = PATCH - LANES
+    low = jnp.where(lane < middle, wide[0], pltpu.roll(wide[1], middle, 1))
+    high = jnp.where(lane < middle, pltpu.roll(wide[0], middle, 1), wide[1])
+    high = jnp.where(lane < extra, narrow[0], high)
+    high = jnp.where((lane >= middle) & (lane < middle + extra), narrow[1], high)
+    odd = lax.rem(lax.axis_index("gx"), 2) == 1
+    first_ref[...] = jnp.where(odd, low, high).astype(jnp.bfloat16)
+    second_ref[...] = jnp.where(odd, high, low).astype(jnp.bfloat16)
+
+
+def flow_kernel(columns, late, own_ref, other_ref, beyond_ref, beside_ref, before_ref, table_ref, out_ref,
+                pixel_ref, partial_ref, high_ref, low_ref, rows_ref):
     half = lax.axis_index("gz")
     odd = lax.rem(lax.axis_index("gx"), 2)
     side = odd if late else 1 - odd
@@ -286,11 +336,15 @@
     lane = lax.broadcasted_iota(jnp.int32, (held, PATCH), 1)
     group = columns // 2
     base = side * group
+    beside = beside_ref[...].astype(jnp.float32)
+    turned = pltpu.roll(beside, LANES // 2, 1)
+    near_lanes = lax.broadcasted_iota(jnp.int32, (held, LANES), 1) < LANES // 2
     for image in range(2):
         tile = own_ref[0] if image == 0 else other_ref[0]
-        mine = jnp.concatenate([tile, diagonal_ref[1 - image]], 0).astype(jnp.float32)
-        halo = beside_ref[image].astype(jnp.float32)
-        halo = jnp.concatenate([halo, halo[:, : PATCH - LANES]], 1)
+        mine = jnp.concatenate([tile, beyond_ref[image]], 0).astype(jnp.float32)
+        here, there = (beside, turned) if image == 0 else (turned, beside)
+        halo = jnp.where(near_lanes, here, there)
+        halo = jnp.concatenate([halo, here[:, : PATCH - LANES]], 1)
         for column in range(group):
             start = (base + column) * STRIDE - MARGIN
             low_lane = jnp.where(side == 0, 0, start)
@@ -299,7 +353,14 @@
             spot = (2 * column + image) * held
             pixel_ref[spot : spot + held] = jnp.where(inside, mine, halo).astype(jnp.bfloat16)
     pixels = pixel_ref[...]
-    partial_ref[...] = dot(pixels, column_ref[0]) + dot(pixels, column_ref[1])
+    partial_ref[...] = dot(pixels, table_ref[:PATCH, :WIDE]) + dot(pixels, table_ref[:PATCH, WIDE:])
+    whole = table_ref[PATCH : 2 * PATCH, : 3 * PATCH]
+    left = table_ref[2 * PATCH : 3 * PATCH, : 3 * PATCH]
+    changes = (
+        table_ref[3 * PATCH : 4 * PATCH, start : start + 3 * STEP_HELD] for start in (0, WIDE)
+    )
+    step_table = jnp.where(half == 0, *changes)
+    right = [table_ref[4 * PATCH :, start : start + PATCH] for start in (0, WIDE)]
     sign = jnp.where(half == 0, 1.0, -1.0).astype(jnp.float32)
     upper = half == 0
     inner = lax.broadcasted_iota(jnp.int32, (SUBLANES, 2 * LANES), 0) < PATCH - MARGIN - TOP_CUT
@@ -335,16 +396,15 @@
             )
             change = rows_at(spot + TOP_CUT, spot + HALO - STEP_HELD, STEP_HELD)
             change = change - rows_at(halo_spot, halo_spot + HALO - STEP_HELD, STEP_HELD)
-            near = table_first(whole_ref[...], window)
-            spectra.append((near, near + table_first(change_ref[half], change)))
+            near = table_first(whole, window)
+            spectra.append((near, near + table_first(step_table, change)))
         for row in range(2):
             cross = cross_spectrum(spectra[0][row], spectra[1][row], sign)
-            high, low = halves_of(table_first(left_ref[...], cross))
+            high, low = halves_of(table_first(left, cross))
             spot = (row * group + column) * PATCH
             high_ref[spot : spot + PATCH] = high
             low_ref[spot : spot + PATCH] = low
-    correl = dot(high_ref[...], right_ref[0]) + dot(high_ref[...], right_ref[1])
-    correl = correl + dot(low_ref[...], right_ref[0])
+    correl = dot(high_ref[...], right[0]) + dot(high_ref[...], right[1]) + dot(low_ref[...], right[0])
     count = 2 * group
     for patch in range(count):
         squared = correl[patch * PATCH : (patch + 1) * PATCH]
@@ -469,26 +529,48 @@
     count_y = images.shape[1] // STRIDE
     count_x = images.shape[2] // STRIDE
     rows = count_y // 2
-    half = lax.axis_index("gz")
-    is_odd = lax.axis_index("gx") % 2 == 1
     other = lax.ppermute(images, "gz", [(0, 1), (1, 0)])
-    both = jnp.concatenate([images, other], 0)
-    edge = jnp.where(half == 1, both[:, PATCH - HALO :], both[:, :HALO])
-    diagonal = []
+    table = jnp.asarray(all_tables())
+    own, table = pl.pallas_call(
+        load_kernel,
+        out_shape=(
+            jax.ShapeDtypeStruct(images.shape, images.dtype),
+            jax.ShapeDtypeStruct(table.shape, table.dtype),
+        ),
+        in_specs=[pl.BlockSpec(memory_space=pltpu.HBM)] * 2,
+        out_specs=tuple(vmem(2)),
+        scratch_shapes=[pltpu.SemaphoreType.DMA((2,))],
+        compiler_params=pltpu.CompilerParams(vmem_limit_bytes=4 * 2**20),
+        cost_estimate=pl.CostEstimate(flops=0, bytes_accessed=4 * table.size, transcendentals=0),
+        name="load",
+    )(images, table)
+    edge = pl.pallas_call(
+        edge_kernel,
+        out_shape=jax.ShapeDtypeStruct((2, HALO, PATCH), jnp.bfloat16),
+        in_specs=vmem(2),
+        out_specs=vmem(1)[0],
+        compiler_params=pltpu.CompilerParams(vmem_limit_bytes=4 * 2**20),
+        name="edge",
+    )(own, other)
+    onward = []
     for tile in range(1, size_y):
-        diagonal += [(size_y + tile - 1, tile), (tile, size_y + tile - 1)]
-    beyond = lax.ppermute(edge, ("gz", "gy"), diagonal)
-    tall = jnp.concatenate([both, beyond[::-1]], 1)
-    low_side = tall[:, :, :LANES]
-    high_side = jnp.concatenate([tall[:, :, LANES:], tall[:, :, PATCH - LANES : LANES]], 2)
+        onward += [(tile - 1, tile), (size_y + tile, size_y + tile - 1)]
+    beyond = lax.ppermute(edge, ("gz", "gy"), onward)
     swaps = [
         [pair for left in range(offset, size_x - 1, 2) for pair in ((left, left + 1), (left + 1, left))]
         for offset in range(2)
     ]
-    first = lax.ppermute(jnp.where(is_odd, low_side, high_side), "gx", swaps[0])
-    second = lax.ppermute(jnp.where(is_odd, high_side, low_side), "gx", swaps[1])
+    packed = jax.ShapeDtypeStruct((PATCH + HALO, LANES), jnp.bfloat16)
+    sends = pl.pallas_call(
+        pack_kernel,
+        out_shape=(packed, packed),
+        in_specs=vmem(3),
+        out_specs=tuple(vmem(2)),
+        compiler_params=pltpu.CompilerParams(vmem_limit_bytes=4 * 2**20),
+        name="pack",
+    )(own, other, beyond)
+    first, second = (lax.ppermute(send, "gx", swap) for send, swap in zip(sends, swaps))
     devices = sections * size_y * size_x
-    tables = [jnp.asarray(table) for table in (column_table(), *row_tables(), *inverse_tables())]
 
     def flows(late, beside, before, lines):
         patches = count_x
@@ -496,7 +578,7 @@
         return pl.pallas_call(
             functools.partial(flow_kernel, count_x, late),
             out_shape=jax.ShapeDtypeStruct((lines, LANES), jnp.float32),
-            in_specs=vmem(10),
+            in_specs=vmem(6),
             out_specs=vmem(1)[0],
             scratch_shapes=[
                 pltpu.VMEM((patches * held, PATCH), jnp.bfloat16),
@@ -510,7 +592,7 @@
                 flops=patches * 2 * 2400 * 256 * 256, bytes_accessed=2**21, transcendentals=0
             ),
             name="flows",
-        )(images, other, beyond, beside, before, *tables)
+        )(own, other, beyond, beside, before, table)
 
     lines = flows(True, second, flows(False, first, tissue_mask, 1), devices)
     got = lax.all_to_all(lines, ("gz", "gy", "gx"), 0, 0, tiled=True)

time: 35.8 us -> 34.3 us (0.958)
  blocking collectives: 21.4 us -> 14.7 us
  starting transfers between devices: 4.44 us -> 7.75 us
  local copies, waits for them, and re-layouts: 0.99 us -> 2.07 us
  Pallas kernels: 5.38 us -> 6.14 us
    all_to_all x1, blocking collectives: 21.4 us -> 14.7 us  [pair_body(): got = lax.all_to_all(lines, ('gz', 'gy', 'gx'), 0, 0, tiled=True)]
    ppermute x3, starting transfers between devices: 1.4 us -> 4.71 us  [the longest x1 3.98 us: pair_body(): beyond = lax.ppermute(edge, ('gz', 'gy'), onward)]
    ppermute x3, waiting for transfers between devices: 0.64 us -> 2.44 us  [the longest x1 1.88 us: pair_body(): beyond = lax.ppermute(edge, ('gz', 'gy'), onward)]
    ppermute x1, waiting for transfers between devices: 1.73 us -> 0.26 us  [pair_body(): other = lax.ppermute(images, 'gz', [(0, 1), (1, 0)])]
    unnamed x15 -> x6, local copies, waits for them, and re-layouts: 0.97 us -> 2.07 us
    pallas_call x0 -> x3, Pallas kernels: none -> 0.53 us  [the longest x1 0.31 us: pair_body(): pl.pallas_call(load_kernel, out_shape=(jax.ShapeDtypeStruct(images.shape,...]
  transfers between devices with their start and end apart: 4 -> 4, of which waited for: 2 -> 3; matrix products, arithmetic and copies ran while one was open for 3% -> 0% of each run, Pallas kernels for 6% -> 8%
where the time goes in v4:
time: 34.3 us; the launch traced here: 34.1 us
  blocking collectives  14.7 us (43%)
  starting transfers between devices  7.75 us (23%)
  Pallas kernels  6.14 us (18%)
  waiting for transfers between devices  2.71 us (8%)
  local copies, waits for them, and re-layouts  2.07 us (6%)
  between operations  0.7 us (2%)
    all_to_all x1, blocking collectives, pair_body(): got = lax.all_to_all(lines, ('gz', 'gy', 'gx'), 0, 0, tiled=True)  14.7 us
    pallas_call x2, Pallas kernels, flows(): pl.pallas_call(functools.partial(flow_kernel, count_x, late), out_shape=j...  4.49 us
    ppermute x1, starting transfers between devices, pair_body(): beyond = lax.ppermute(edge, ('gz', 'gy'), onward)  3.98 us
    ppermute x1, starting transfers between devices, pair_body(): other = lax.ppermute(images, 'gz', [(0, 1), (1, 0)])  3.03 us
    unnamed x6, local copies, waits for them, and re-layouts  2.07 us
    ppermute x1, waiting for transfers between devices, pair_body(): beyond = lax.ppermute(edge, ('gz', 'gy'), onward)  1.88 us
    pallas_call x1, Pallas kernels, pair_body(): pl.pallas_call(functools.partial(relax_kernel, rows, count_x), out_shape=...  1.12 us
    ppermute x2, starting transfers between devices, pair_body(): lax.ppermute(send, 'gx', swap)  0.74 us
  transfers between devices with their start and end apart: 4, of which 3 were waited for; matrix products, arithmetic and copies ran while one was open for 0% of the time, Pallas kernels for 8%

profile of v4, /device:TPU:0, one launch (start us, length us, event | category | flops | bytes accessed | tf_op | source)
XLA Modules:
  0.0 34.1 jit_solution(669127420794394327)
XLA Ops:
  0.6 3.0 %collective-permute-start = (bf16[1,160,160]{2,1,0:T(8,128)(2,1)}, bf16[1,160,160]{2,1,0:T(8,128)(2,1)S(1)}, u32[]{:S(2)}, u32[]{:S(2)}) collective-permute-start(bf16[1,160,160]{2,1,0:T(8,128)(2,1)} %own_ref.1), channel_id=1, source_target_pairs={{0,16},{16,0},{1,17},{17,1},{2,18},{18,2},{3,19},{19,3},{4,20},{20... | collective-permute-start | bytes 153608 | tf_op jit(solution)/shard_map/ppermute | solution.py:532
  3.7 0.0 copy-start
  3.7 1.2 %copy-done = bf16[896,512]{1,0:T(8,128)(2,1)S(1)} copy-done((bf16[896,512]{1,0:T(8,128)(2,1)S(1)}, bf16[896,512]{1,0:T(8,128)(2,1)}, u32[]{:S(2)}) %copy-start) | copy-done | bytes 917528
  4.8 0.0 copy-start.1
  4.8 0.9 %copy-done.1 = bf16[1,160,160]{2,1,0:T(8,128)(2,1)S(1)} copy-done((bf16[1,160,160]{2,1,0:T(8,128)(2,1)S(1)}, bf16[1,160,160]{2,1,0:T(8,128)(2,1)}, u32[]{:S(2)}) %copy-start.1) | copy-done | bytes 51224
  5.7 0.3 load.1
  6.0 0.3 collective-permute-done.other_ref
  6.3 4.0 %collective-permute-start.1 = (bf16[2,64,160]{2,1,0:T(8,128)(2,1)S(1)}, bf16[2,64,160]{2,1,0:T(8,128)(2,1)S(1)}, u32[]{:S(2)}, u32[]{:S(2)}) collective-permute-start(bf16[2,64,160]{2,1,0:T(8,128)(2,1)S(1)} %edge.1), channel_id=1, source_target_pairs={{0,4},{20,16},{4,8},{24,20},{8,12},{28,24},{1,5},{21,17},{5,9},{25... | collective-permute-start | bytes 122888 | tf_op jit(solution)/shard_map/ppermute | solution.py:558
  10.3 1.9 %collective-permute-done.1.beyond_ref = bf16[2,64,160]{2,1,0:T(8,128)(2,1)S(1)} collective-permute-done((bf16[2,64,160]{2,1,0:T(8,128)(2,1)S(1)}, bf16[2,64,160]{2,1,0:T(8,128)(2,1)S(1)}, u32[]{:S(2)}, u32[]{:S(2)}) %collective-permute-start.1) | collective-permute-done | bytes 40992 | tf_op jit(solution)/shard_map/ppermute | solution.py:558
  12.2 0.2 pack.1
  12.4 0.0 copy-start.2
  12.4 0.1 collective-permute-start.3
  12.5 0.7 %collective-permute-start.2 = (bf16[224,128]{1,0:T(8,128)(2,1)S(1)}, bf16[224,128]{1,0:T(8,128)(2,1)S(1)}, u32[]{:S(2)}, u32[]{:S(2)}) collective-permute-start(bf16[224,128]{1,0:T(8,128)(2,1)S(1)} %get-tuple-element.7), channel_id=1, source_target_pairs={{1,2},{2,1},{5,6},{6,5},{9,10},{10,9},{13,14},{14,13},{17,18},{18,... | collective-permute-start | bytes 172040 | tf_op jit(solution)/shard_map/ppermute | solution.py:572
  13.2 0.6 %collective-permute-done.3.beside_ref = bf16[224,128]{1,0:T(8,128)(2,1)S(1)} collective-permute-done((bf16[224,128]{1,0:T(8,128)(2,1)S(1)}, bf16[224,128]{1,0:T(8,128)(2,1)S(1)}, u32[]{:S(2)}, u32[]{:S(2)}) %collective-permute-start.3) | collective-permute-done | bytes 57376 | tf_op jit(solution)/shard_map/ppermute | solution.py:572
  13.7 0.0 copy-done.2
  13.7 2.3 %flows.2.before_ref = f32[1,128]{1,0:T(1,128)S(1)} custom-call(bf16[1,160,160]{2,1,0:T(8,128)(2,1)S(1)} %get-tuple-element.6.own_ref, bf16[1,160,160]{2,1,0:T(8,128)(2,1)S(1)} %collective-permute-done.other_ref, bf16[2,64,160]{2,1,0:T(8,128)(2,1)S(1)} %collective-permute-done.1.beyond_ref, bf16[224,128]{1,0:T(8,128)(2,1)S(1)} %collective-permute-done.3.beside_ref, ...), custom_call_target="tpu_custom_call" | custom-call | flops 1258291200 | bytes 2097152 | tf_op jit(solution)/shard_map/flows/pallas_call | solution.py:578
  16.0 0.0 collective-permute-done.2.beside_ref
  16.0 2.2 %flows.3 = f32[32,128]{1,0:T(8,128)S(1)} custom-call(bf16[1,160,160]{2,1,0:T(8,128)(2,1)S(1)} %get-tuple-element.6.own_ref, bf16[1,160,160]{2,1,0:T(8,128)(2,1)S(1)} %collective-permute-done.other_ref, bf16[2,64,160]{2,1,0:T(8,128)(2,1)S(1)} %collective-permute-done.1.beyond_ref, bf16[224,128]{1,0:T(8,128)(2,1)S(1)} %collective-permute-done.2.beside_ref, ...), custom_call_target="tpu_custom_call" | custom-call | flops 1258291200 | bytes 2097152 | tf_op jit(solution)/shard_map/flows/pallas_call | solution.py:578
  18.2 14.7 %all_to_all.11 = f32[32,1,128]{2,1,0:T(1,128)S(1)} all-to-all(f32[32,1,128]{2,1,0:T(1,128)S(1)} %bitcast.5), channel_id=1, replica_groups=mesh['gz'=2,'gy'=4,'gx'=4] {'gz','gy','gx'}, dimensions={0} | all-to-all | bytes 32768 | tf_op jit(solution)/shard_map/all_to_all | solution.py:598
  32.9 1.1 %relax.1 = (f32[4,1,4,4]{3,2,1,0:T(4,128)}, f32[2,1,4,4]{3,2,1,0:T(4,128)}) custom-call(f32[32,128]{1,0:T(8,128)S(1)} %bitcast.4), custom_call_target="tpu_custom_call" | custom-call | tf_op jit(solution)/shard_map/relax/pallas_call | solution.py:599
  (1 shorter events, 0.0 us)
Async XLA Ops:
  0.6 5.7 %collective-permute-start = (bf16[1,160,160]{2,1,0:T(8,128)(2,1)}, bf16[1,160,160]{2,1,0:T(8,128)(2,1)S(1)}, u32[]{:S(2)}, u32[]{:S(2)}) collective-permute-start(bf16[1,160,160]{2,1,0:T(8,128)(2,1)} %own_ref.1), channel_id=1, source_target_pairs={{0,16},{16,0},{1,17},{17,1},{2,18},{18,2},{3,19},{19,3},{4,20},{20... | collective-permute-start | bytes 153608 | tf_op jit(solution)/shard_map/ppermute | solution.py:532
  3.7 1.2 %copy-start = (bf16[896,512]{1,0:T(8,128)(2,1)S(1)}, bf16[896,512]{1,0:T(8,128)(2,1)}, u32[]{:S(2)}) copy-start(bf16[896,512]{1,0:T(8,128)(2,1)} %constant.2.clone.table_ref) | copy-start | bytes 2752516
  4.8 0.9 %copy-start.1 = (bf16[1,160,160]{2,1,0:T(8,128)(2,1)S(1)}, bf16[1,160,160]{2,1,0:T(8,128)(2,1)}, u32[]{:S(2)}) copy-start(bf16[1,160,160]{2,1,0:T(8,128)(2,1)} %own_ref.1) | copy-start | bytes 153604
  6.3 5.9 %collective-permute-start.1 = (bf16[2,64,160]{2,1,0:T(8,128)(2,1)S(1)}, bf16[2,64,160]{2,1,0:T(8,128)(2,1)S(1)}, u32[]{:S(2)}, u32[]{:S(2)}) collective-permute-start(bf16[2,64,160]{2,1,0:T(8,128)(2,1)S(1)} %edge.1), channel_id=1, source_target_pairs={{0,4},{20,16},{4,8},{24,20},{8,12},{28,24},{1,5},{21,17},{5,9},{25... | collective-permute-start | bytes 122888 | tf_op jit(solution)/shard_map/ppermute | solution.py:558
  12.4 1.3 %copy-start.2 = (s32[1,4,4]{2,1,0:T(4,128)S(1)}, s32[1,4,4]{2,1,0:T(4,128)}, u32[]{:S(2)}) copy-start(s32[1,4,4]{2,1,0:T(4,128)} %before_ref.1) | copy-start | bytes 196
  12.4 1.3 %collective-permute-start.3 = (bf16[224,128]{1,0:T(8,128)(2,1)S(1)}, bf16[224,128]{1,0:T(8,128)(2,1)S(1)}, u32[]{:S(2)}, u32[]{:S(2)}) collective-permute-start(bf16[224,128]{1,0:T(8,128)(2,1)S(1)} %get-tuple-element.8), channel_id=1, source_target_pairs={{0,1},{1,0},{2,3},{3,2},{4,5},{5,4},{6,7},{7,6},{8,9},{9,8},{10,11... | collective-permute-start | bytes 172040 | tf_op jit(solution)/shard_map/ppermute | solution.py:572
  12.5 3.5 %collective-permute-start.2 = (bf16[224,128]{1,0:T(8,128)(2,1)S(1)}, bf16[224,128]{1,0:T(8,128)(2,1)S(1)}, u32[]{:S(2)}, u32[]{:S(2)}) collective-permute-start(bf16[224,128]{1,0:T(8,128)(2,1)S(1)} %get-tuple-element.7), channel_id=1, source_target_pairs={{1,2},{2,1},{5,6},{6,5},{9,10},{10,9},{13,14},{14,13},{17,18},{18,... | collective-permute-start | bytes 172040 | tf_op jit(solution)/shard_map/ppermute | solution.py:572

commit v5 on v4

--- a/solution.py
+++ b/solution.py
@@ -265,7 +265,7 @@
     return dot(table, jnp.concatenate([high, high, low], 0))
 
 
-def cross_spectrum(first, second, sign):
+def cross_spectrum(first, second):
     (acc, acs, asc, ass), (bcc, bcs, bsc, bss) = (
         (value[:BAND, :LANES], value[:BAND, LANES:], value[BAND:, :LANES], value[BAND:, LANES:])
         for value in (first, second)
@@ -274,7 +274,7 @@
     even_1 = asc * bsc + ass * bss
     column_0 = acs * bcc - acc * bcs
     column_1 = ass * bsc - asc * bss
-    by_row = sign * (asc * bcc - acc * bsc + ass * bcs - acs * bss)
+    by_row = asc * bcc - acc * bsc + ass * bcs - acs * bss
     both = acc * bss + ass * bcc - asc * bcs - acs * bsc
     top = SUBLANES
     lone = lax.broadcasted_iota(jnp.int32, (top, LANES), 0) == 0
@@ -284,8 +284,8 @@
 
     even = with_top(even_0 + even_1, even_0)
     by_row = with_top(by_row, even_1)
-    by_column = sign * with_top(column_0 + column_1, column_0)
-    both = with_top(both, sign * column_1[:top])
+    by_column = with_top(column_0 + column_1, column_0)
+    both = with_top(both, column_1)
     return jnp.concatenate(
         [jnp.concatenate([even, by_column], 1), jnp.concatenate([by_row, both], 1)], 0
     )
@@ -333,27 +333,32 @@
     odd = lax.rem(lax.axis_index("gx"), 2)
     side = odd if late else 1 - odd
     held = PATCH + HALO
-    lane = lax.broadcasted_iota(jnp.int32, (held, PATCH), 1)
     group = columns // 2
     base = side * group
     beside = beside_ref[...].astype(jnp.float32)
-    turned = pltpu.roll(beside, LANES // 2, 1)
-    near_lanes = lax.broadcasted_iota(jnp.int32, (held, LANES), 1) < LANES // 2
+    turned = pltpu.roll(beside, LANES // 2, 1).astype(jnp.bfloat16)
+    beside = beside_ref[...]
+    lane = lax.broadcasted_iota(jnp.int32, (held, PATCH), 1).astype(jnp.float32).astype(jnp.bfloat16)
+    near_lanes = lane[:, :LANES] < LANES // 2
     for image in range(2):
         tile = own_ref[0] if image == 0 else other_ref[0]
-        mine = jnp.concatenate([tile, beyond_ref[image]], 0).astype(jnp.float32)
+        mine = jnp.concatenate([tile, beyond_ref[image]], 0)
         here, there = (beside, turned) if image == 0 else (turned, beside)
         halo = jnp.where(near_lanes, here, there)
         halo = jnp.concatenate([halo, here[:, : PATCH - LANES]], 1)
         for column in range(group):
             start = (base + column) * STRIDE - MARGIN
-            low_lane = jnp.where(side == 0, 0, start)
-            high_lane = jnp.where(side == 0, start + PATCH, PATCH)
+            low_lane = jnp.where(side == 0, 0, start).astype(jnp.float32).astype(jnp.bfloat16)
+            high_lane = jnp.where(side == 0, start + PATCH, PATCH).astype(jnp.float32).astype(jnp.bfloat16)
             inside = (lane >= low_lane) & (lane < high_lane)
-            spot = (2 * column + image) * held
-            pixel_ref[spot : spot + held] = jnp.where(inside, mine, halo).astype(jnp.bfloat16)
-    pixels = pixel_ref[...]
-    partial_ref[...] = dot(pixels, table_ref[:PATCH, :WIDE]) + dot(pixels, table_ref[:PATCH, WIDE:])
+            section = half if image == 0 else 1 - half
+            spot = pl.multiple_of((2 * column + section) * held, HALO // 2)
+            pixel_ref[pl.ds(spot, held)] = jnp.where(inside, mine, halo)
+    for spot in range(0, pixel_ref.shape[0], held):
+        pixels = pixel_ref[spot : spot + held]
+        partial_ref[spot : spot + held] = dot(pixels, table_ref[:PATCH, :WIDE]) + dot(
+            pixels, table_ref[:PATCH, WIDE:]
+        )
     whole = table_ref[PATCH : 2 * PATCH, : 3 * PATCH]
     left = table_ref[2 * PATCH : 3 * PATCH, : 3 * PATCH]
     changes = (
@@ -361,11 +366,12 @@
     )
     step_table = jnp.where(half == 0, *changes)
     right = [table_ref[4 * PATCH :, start : start + PATCH] for start in (0, WIDE)]
-    sign = jnp.where(half == 0, 1.0, -1.0).astype(jnp.float32)
     upper = half == 0
     inner = lax.broadcasted_iota(jnp.int32, (SUBLANES, 2 * LANES), 0) < PATCH - MARGIN - TOP_CUT
+    every = []
     for column in range(group):
         spectra = []
+        every.append(spectra)
         for image in range(2):
             spot = (2 * column + image) * held
             halo_spot = spot + PATCH
@@ -398,26 +404,36 @@
             change = change - rows_at(halo_spot, halo_spot + HALO - STEP_HELD, STEP_HELD)
             near = table_first(whole, window)
             spectra.append((near, near + table_first(step_table, change)))
+    for column, spectra in enumerate(every):
         for row in range(2):
-            cross = cross_spectrum(spectra[0][row], spectra[1][row], sign)
+            cross = cross_spectrum(spectra[0][row], spectra[1][row])
             high, low = halves_of(table_first(left, cross))
             spot = (row * group + column) * PATCH
             high_ref[spot : spot + PATCH] = high
             low_ref[spot : spot + PATCH] = low
-    correl = dot(high_ref[...], right[0]) + dot(high_ref[...], right[1]) + dot(low_ref[...], right[0])
     count = 2 * group
     for patch in range(count):
-        squared = correl[patch * PATCH : (patch + 1) * PATCH]
+        if patch % group == 0:
+            block = slice(patch * PATCH, (patch + group) * PATCH)
+            correl = dot(high_ref[block], right[0]) + dot(high_ref[block], right[1])
+            correl = correl + dot(low_ref[block], right[0])
+        squared = correl[patch % group * PATCH : (patch % group + 1) * PATCH]
         squared = squared * squared
         weights = squared * squared
-        total = weights[:SUBLANES]
-        based = jnp.zeros_like(total)
-        for piece_at in range(1, PATCH // SUBLANES):
-            piece = weights[piece_at * SUBLANES : (piece_at + 1) * SUBLANES]
-            shift = piece_at * SUBLANES
-            shift = shift - PATCH if shift >= PATCH // 2 else shift
-            total = total + piece
-            based = based + piece * float(shift)
+        pieces = [weights[at : at + SUBLANES] for at in range(0, PATCH, SUBLANES)]
+        middle = len(pieces) // 2
+        above = pieces[middle - 1]
+        ranks = above
+        for piece in pieces[middle - 2 : 0 : -1]:
+            above = above + piece
+            ranks = ranks + above
+        below = pieces[middle]
+        depths = below
+        for piece in pieces[middle + 1 :]:
+            below = below + piece
+            depths = depths + below
+        total = pieces[0] + above + below
+        based = float(SUBLANES) * (ranks - depths)
         step = lax.broadcasted_iota(jnp.int32, (SUBLANES, PATCH), 0).astype(jnp.float32)
         based = based + step * total
         rows_ref[0, pl.ds(patch, 1)] = jnp.sum(total, 0, keepdims=True)

time: 34.3 us -> 33.8 us (0.985)
  Pallas kernels: 6.14 us -> 5.07 us
  blocking collectives: 14.7 us -> 15.2 us
    pallas_call x2, Pallas kernels: 4.49 us -> 3.42 us  [flows(): pl.pallas_call(functools.partial(flow_kernel, count_x, late), out_shape=j...]
    all_to_all x1, blocking collectives: 14.7 us -> 15.2 us  [pair_body(): got = lax.all_to_all(lines, ('gz', 'gy', 'gx'), 0, 0, tiled=True)]
  transfers between devices with their start and end apart: 4 -> 4, of which waited for: 3 -> 3; matrix products, arithmetic and copies ran while one was open for 0% -> 0% of each run, Pallas kernels for 8% -> 6%
where the time goes in v5:
time: 33.8 us; the launch traced here: 33.5 us
  blocking collectives  15.2 us (45%)
  starting transfers between devices  7.75 us (23%)
  Pallas kernels  5.07 us (15%)
  waiting for transfers between devices  2.71 us (8%)
  local copies, waits for them, and re-layouts  2.07 us (6%)
  between operations  0.7 us (2%)
    all_to_all x1, blocking collectives, pair_body(): got = lax.all_to_all(lines, ('gz', 'gy', 'gx'), 0, 0, tiled=True)  15.2 us
    ppermute x1, starting transfers between devices, pair_body(): beyond = lax.ppermute(edge, ('gz', 'gy'), onward)  3.98 us
    pallas_call x2, Pallas kernels, flows(): pl.pallas_call(functools.partial(flow_kernel, count_x, late), out_shape=j...  3.42 us
    ppermute x1, starting transfers between devices, pair_body(): other = lax.ppermute(images, 'gz', [(0, 1), (1, 0)])  3.03 us
    unnamed x6, local copies, waits for them, and re-layouts  2.07 us
    ppermute x1, waiting for transfers between devices, pair_body(): beyond = lax.ppermute(edge, ('gz', 'gy'), onward)  1.88 us
    pallas_call x1, Pallas kernels, pair_body(): pl.pallas_call(functools.partial(relax_kernel, rows, count_x), out_shape=...  1.12 us
    ppermute x2, starting transfers between devices, pair_body(): lax.ppermute(send, 'gx', swap)  0.74 us
  transfers between devices with their start and end apart: 4, of which 3 were waited for; matrix products, arithmetic and copies ran while one was open for 0% of the time, Pallas kernels for 6%

profile of v5, /device:TPU:0, one launch (start us, length us, event | category | flops | bytes accessed | tf_op | source)
XLA Modules:
  0.0 33.5 jit_solution(17844669946095462185)
XLA Ops:
  0.6 3.0 %collective-permute-start = (bf16[1,160,160]{2,1,0:T(8,128)(2,1)}, bf16[1,160,160]{2,1,0:T(8,128)(2,1)S(1)}, u32[]{:S(2)}, u32[]{:S(2)}) collective-permute-start(bf16[1,160,160]{2,1,0:T(8,128)(2,1)} %own_ref.1), channel_id=1, source_target_pairs={{0,16},{16,0},{1,17},{17,1},{2,18},{18,2},{3,19},{19,3},{4,20},{20... | collective-permute-start | bytes 153608 | tf_op jit(solution)/shard_map/ppermute | solution.py:548
  3.7 0.0 copy-start
  3.7 1.2 %copy-done = bf16[896,512]{1,0:T(8,128)(2,1)S(1)} copy-done((bf16[896,512]{1,0:T(8,128)(2,1)S(1)}, bf16[896,512]{1,0:T(8,128)(2,1)}, u32[]{:S(2)}) %copy-start) | copy-done | bytes 917528
  4.8 0.0 copy-start.1
  4.8 0.9 %copy-done.1 = bf16[1,160,160]{2,1,0:T(8,128)(2,1)S(1)} copy-done((bf16[1,160,160]{2,1,0:T(8,128)(2,1)S(1)}, bf16[1,160,160]{2,1,0:T(8,128)(2,1)}, u32[]{:S(2)}) %copy-start.1) | copy-done | bytes 51224
  5.7 0.3 load.1
  6.0 0.3 collective-permute-done.other_ref
  6.3 4.0 %collective-permute-start.1 = (bf16[2,64,160]{2,1,0:T(8,128)(2,1)S(1)}, bf16[2,64,160]{2,1,0:T(8,128)(2,1)S(1)}, u32[]{:S(2)}, u32[]{:S(2)}) collective-permute-start(bf16[2,64,160]{2,1,0:T(8,128)(2,1)S(1)} %edge.1), channel_id=1, source_target_pairs={{0,4},{20,16},{4,8},{24,20},{8,12},{28,24},{1,5},{21,17},{5,9},{25... | collective-permute-start | bytes 122888 | tf_op jit(solution)/shard_map/ppermute | solution.py:574
  10.3 1.9 %collective-permute-done.1.beyond_ref = bf16[2,64,160]{2,1,0:T(8,128)(2,1)S(1)} collective-permute-done((bf16[2,64,160]{2,1,0:T(8,128)(2,1)S(1)}, bf16[2,64,160]{2,1,0:T(8,128)(2,1)S(1)}, u32[]{:S(2)}, u32[]{:S(2)}) %collective-permute-start.1) | collective-permute-done | bytes 40992 | tf_op jit(solution)/shard_map/ppermute | solution.py:574
  12.2 0.2 pack.1
  12.4 0.0 copy-start.2
  12.4 0.1 collective-permute-start.3
  12.5 0.7 %collective-permute-start.2 = (bf16[224,128]{1,0:T(8,128)(2,1)S(1)}, bf16[224,128]{1,0:T(8,128)(2,1)S(1)}, u32[]{:S(2)}, u32[]{:S(2)}) collective-permute-start(bf16[224,128]{1,0:T(8,128)(2,1)S(1)} %get-tuple-element.7), channel_id=1, source_target_pairs={{1,2},{2,1},{5,6},{6,5},{9,10},{10,9},{13,14},{14,13},{17,18},{18,... | collective-permute-start | bytes 172040 | tf_op jit(solution)/shard_map/ppermute | solution.py:588
  13.2 0.6 %collective-permute-done.3.beside_ref = bf16[224,128]{1,0:T(8,128)(2,1)S(1)} collective-permute-done((bf16[224,128]{1,0:T(8,128)(2,1)S(1)}, bf16[224,128]{1,0:T(8,128)(2,1)S(1)}, u32[]{:S(2)}, u32[]{:S(2)}) %collective-permute-start.3) | collective-permute-done | bytes 57376 | tf_op jit(solution)/shard_map/ppermute | solution.py:588
  13.7 0.0 copy-done.2
  13.7 1.7 %flows.2.before_ref = f32[1,128]{1,0:T(1,128)S(1)} custom-call(bf16[1,160,160]{2,1,0:T(8,128)(2,1)S(1)} %get-tuple-element.6.own_ref, bf16[1,160,160]{2,1,0:T(8,128)(2,1)S(1)} %collective-permute-done.other_ref, bf16[2,64,160]{2,1,0:T(8,128)(2,1)S(1)} %collective-permute-done.1.beyond_ref, bf16[224,128]{1,0:T(8,128)(2,1)S(1)} %collective-permute-done.3.beside_ref, ...), custom_call_target="tpu_custom_call" | custom-call | flops 1258291200 | bytes 2097152 | tf_op jit(solution)/shard_map/flows/pallas_call | solution.py:594
  15.5 0.0 collective-permute-done.2.beside_ref
  15.5 1.7 %flows.3 = f32[32,128]{1,0:T(8,128)S(1)} custom-call(bf16[1,160,160]{2,1,0:T(8,128)(2,1)S(1)} %get-tuple-element.6.own_ref, bf16[1,160,160]{2,1,0:T(8,128)(2,1)S(1)} %collective-permute-done.other_ref, bf16[2,64,160]{2,1,0:T(8,128)(2,1)S(1)} %collective-permute-done.1.beyond_ref, bf16[224,128]{1,0:T(8,128)(2,1)S(1)} %collective-permute-done.2.beside_ref, ...), custom_call_target="tpu_custom_call" | custom-call | flops 1258291200 | bytes 2097152 | tf_op jit(solution)/shard_map/flows/pallas_call | solution.py:594
  17.2 15.2 %all_to_all.11 = f32[32,1,128]{2,1,0:T(1,128)S(1)} all-to-all(f32[32,1,128]{2,1,0:T(1,128)S(1)} %bitcast.5), channel_id=1, replica_groups=mesh['gz'=2,'gy'=4,'gx'=4] {'gz','gy','gx'}, dimensions={0} | all-to-all | bytes 32768 | tf_op jit(solution)/shard_map/all_to_all | solution.py:614
  32.4 1.1 %relax.1 = (f32[4,1,4,4]{3,2,1,0:T(4,128)}, f32[2,1,4,4]{3,2,1,0:T(4,128)}) custom-call(f32[32,128]{1,0:T(8,128)S(1)} %bitcast.4), custom_call_target="tpu_custom_call" | custom-call | tf_op jit(solution)/shard_map/relax/pallas_call | solution.py:615
  (1 shorter events, 0.0 us)
Async XLA Ops:
  0.6 5.7 %collective-permute-start = (bf16[1,160,160]{2,1,0:T(8,128)(2,1)}, bf16[1,160,160]{2,1,0:T(8,128)(2,1)S(1)}, u32[]{:S(2)}, u32[]{:S(2)}) collective-permute-start(bf16[1,160,160]{2,1,0:T(8,128)(2,1)} %own_ref.1), channel_id=1, source_target_pairs={{0,16},{16,0},{1,17},{17,1},{2,18},{18,2},{3,19},{19,3},{4,20},{20... | collective-permute-start | bytes 153608 | tf_op jit(solution)/shard_map/ppermute | solution.py:548
  3.7 1.2 %copy-start = (bf16[896,512]{1,0:T(8,128)(2,1)S(1)}, bf16[896,512]{1,0:T(8,128)(2,1)}, u32[]{:S(2)}) copy-start(bf16[896,512]{1,0:T(8,128)(2,1)} %constant.2.clone.table_ref) | copy-start | bytes 2752516
  4.8 0.9 %copy-start.1 = (bf16[1,160,160]{2,1,0:T(8,128)(2,1)S(1)}, bf16[1,160,160]{2,1,0:T(8,128)(2,1)}, u32[]{:S(2)}) copy-start(bf16[1,160,160]{2,1,0:T(8,128)(2,1)} %own_ref.1) | copy-start | bytes 153604
  6.3 5.9 %collective-permute-start.1 = (bf16[2,64,160]{2,1,0:T(8,128)(2,1)S(1)}, bf16[2,64,160]{2,1,0:T(8,128)(2,1)S(1)}, u32[]{:S(2)}, u32[]{:S(2)}) collective-permute-start(bf16[2,64,160]{2,1,0:T(8,128)(2,1)S(1)} %edge.1), channel_id=1, source_target_pairs={{0,4},{20,16},{4,8},{24,20},{8,12},{28,24},{1,5},{21,17},{5,9},{25... | collective-permute-start | bytes 122888 | tf_op jit(solution)/shard_map/ppermute | solution.py:574
  12.4 1.3 %copy-start.2 = (s32[1,4,4]{2,1,0:T(4,128)S(1)}, s32[1,4,4]{2,1,0:T(4,128)}, u32[]{:S(2)}) copy-start(s32[1,4,4]{2,1,0:T(4,128)} %before_ref.1) | copy-start | bytes 196
  12.4 1.3 %collective-permute-start.3 = (bf16[224,128]{1,0:T(8,128)(2,1)S(1)}, bf16[224,128]{1,0:T(8,128)(2,1)S(1)}, u32[]{:S(2)}, u32[]{:S(2)}) collective-permute-start(bf16[224,128]{1,0:T(8,128)(2,1)S(1)} %get-tuple-element.8), channel_id=1, source_target_pairs={{0,1},{1,0},{2,3},{3,2},{4,5},{5,4},{6,7},{7,6},{8,9},{9,8},{10,11... | collective-permute-start | bytes 172040 | tf_op jit(solution)/shard_map/ppermute | solution.py:588
  12.5 3.0 %collective-permute-start.2 = (bf16[224,128]{1,0:T(8,128)(2,1)S(1)}, bf16[224,128]{1,0:T(8,128)(2,1)S(1)}, u32[]{:S(2)}, u32[]{:S(2)}) collective-permute-start(bf16[224,128]{1,0:T(8,128)(2,1)S(1)} %get-tuple-element.7), channel_id=1, source_target_pairs={{1,2},{2,1},{5,6},{6,5},{9,10},{10,9},{13,14},{14,13},{17,18},{18,... | collective-permute-start | bytes 172040 | tf_op jit(solution)/shard_map/ppermute | solution.py:588

commit v6 on v5

--- a/solution.py
+++ b/solution.py
@@ -179,10 +179,12 @@
 HALO = -(-MARGIN // 16) * 16
 RADIUS = RELAX - 1
 WIDE = 2 * LANES
-STEP_ROWS = (PATCH - MARGIN, MARGIN - STRIDE)
-STEP_HELD = STRIDE + SUBLANES
-TOP_CUT = PATCH - HALO
-LOW_CUT = HALO - SUBLANES
+HELD = PATCH + HALO
+SIDE = LANES // 2
+HALO_AT = PATCH
+ROWS_AT = HALO_AT + 2 * 3 * SIDE
+LEFT_AT = ROWS_AT + 2 * 2 * PATCH
+RIGHT_AT = LEFT_AT + PATCH
 
 
 def split_table(table):
@@ -196,12 +198,21 @@
     return np.cos(angle), np.sin(angle)
 
 
-def column_table():
+def column_tables():
     cosine, sine = trig(np.arange(PATCH), np.arange(HALF))
-    table = np.zeros((PATCH, 2 * LANES))
+    table = np.zeros((PATCH, WIDE))
     table[:, :HALF] = cosine
     table[:, LANES : LANES + HALF] = sine
-    return split_table(table)
+    spot = np.arange(SIDE)
+    before = np.where(spot < PATCH - LANES, LANES + spot, SIDE + spot)
+    outer = []
+    for window in range(PATCH // STRIDE):
+        start = window * STRIDE - MARGIN
+        column = before if start < 0 else spot
+        used = column >= start + PATCH if start < 0 else column < start
+        high, low = split_table(table[column] * used[:, None])
+        outer.append(np.concatenate([high, high, low], 0))
+    return split_table(table), outer
 
 
 def stacked(table):
@@ -215,14 +226,18 @@
 
 
 def row_tables():
-    whole = stacked(frequency_rows(np.arange(PATCH)))
-    changes = []
+    tables = []
     for half in range(2):
-        first = (STEP_ROWS[half] // SUBLANES) * SUBLANES
-        positions = first + np.arange(STEP_HELD)
-        used = (positions >= STEP_ROWS[half]) & (positions < STEP_ROWS[half] + STRIDE)
-        changes.append(stacked(frequency_rows(positions) * used))
-    return whole, np.stack(changes)
+        first = PATCH - HALO if half == 0 else 0
+        position = np.concatenate([np.arange(PATCH), first + np.arange(HALO)])
+        image_row = position + np.where(np.arange(HELD) < PATCH, 0, -PATCH if half == 0 else PATCH)
+        rows = frequency_rows(position)
+        windows = []
+        for window in (2 * half, 2 * half + 1):
+            start = window * STRIDE - MARGIN
+            windows.append(rows * ((image_row >= start) & (image_row < start + PATCH)))
+        tables.append(split_table(np.concatenate(windows, 0)))
+    return tables
 
 
 def inverse_tables():
@@ -238,10 +253,9 @@
 
 
 def all_tables():
-    column = column_table()
-    whole, change = row_tables()
+    mine, outer = column_tables()
     left, right = inverse_tables()
-    blocks = [(column[0], column[1]), (whole,), (left,), (change[0], change[1]), (right[0], right[1])]
+    blocks = [mine, outer[:2], outer[2:], *row_tables(), (left,), right]
     rows = []
     for parts in blocks:
         block = np.zeros((parts[0].shape[0], 2 * WIDE), jnp.bfloat16)
@@ -327,97 +341,54 @@
     second_ref[...] = jnp.where(odd, high, low).astype(jnp.bfloat16)
 
 
-def flow_kernel(columns, late, own_ref, other_ref, beyond_ref, beside_ref, before_ref, table_ref, out_ref,
-                pixel_ref, partial_ref, high_ref, low_ref, rows_ref):
+def to_row_frequencies(table_ref, half, pixels):
+    start = pl.multiple_of(ROWS_AT + half * (2 * PATCH), PATCH)
+    high = table_ref[pl.ds(start, 2 * PATCH), :HELD]
+    low = table_ref[pl.ds(start, 2 * PATCH), WIDE : WIDE + HELD]
+    return dot(high, pixels) + dot(low, pixels)
+
+
+def finish(columns, side, own_spectra, own_side, beside_ref, table_ref, high_ref, low_ref, rows_ref):
     half = lax.axis_index("gz")
-    odd = lax.rem(lax.axis_index("gx"), 2)
-    side = odd if late else 1 - odd
-    held = PATCH + HALO
     group = columns // 2
-    base = side * group
-    beside = beside_ref[...].astype(jnp.float32)
-    turned = pltpu.roll(beside, LANES // 2, 1).astype(jnp.bfloat16)
-    beside = beside_ref[...]
-    lane = lax.broadcasted_iota(jnp.int32, (held, PATCH), 1).astype(jnp.float32).astype(jnp.bfloat16)
-    near_lanes = lane[:, :LANES] < LANES // 2
+    beside = to_row_frequencies(table_ref, half, beside_ref[...]) - own_side
+    lane = lax.broadcasted_iota(jnp.int32, beside.shape, 1)
+    parts = []
+    for value in (beside, pltpu.roll(beside, SIDE, 1)):
+        high = value.astype(jnp.bfloat16).astype(jnp.float32)
+        parts.append((high, value - high))
+    factors = []
     for image in range(2):
-        tile = own_ref[0] if image == 0 else other_ref[0]
-        mine = jnp.concatenate([tile, beyond_ref[image]], 0)
-        here, there = (beside, turned) if image == 0 else (turned, beside)
-        halo = jnp.where(near_lanes, here, there)
-        halo = jnp.concatenate([halo, here[:, : PATCH - LANES]], 1)
-        for column in range(group):
-            start = (base + column) * STRIDE - MARGIN
-            low_lane = jnp.where(side == 0, 0, start).astype(jnp.float32).astype(jnp.bfloat16)
-            high_lane = jnp.where(side == 0, start + PATCH, PATCH).astype(jnp.float32).astype(jnp.bfloat16)
-            inside = (lane >= low_lane) & (lane < high_lane)
-            section = half if image == 0 else 1 - half
-            spot = pl.multiple_of((2 * column + section) * held, HALO // 2)
-            pixel_ref[pl.ds(spot, held)] = jnp.where(inside, mine, halo)
-    for spot in range(0, pixel_ref.shape[0], held):
-        pixels = pixel_ref[spot : spot + held]
-        partial_ref[spot : spot + held] = dot(pixels, table_ref[:PATCH, :WIDE]) + dot(
-            pixels, table_ref[:PATCH, WIDE:]
-        )
-    whole = table_ref[PATCH : 2 * PATCH, : 3 * PATCH]
-    left = table_ref[2 * PATCH : 3 * PATCH, : 3 * PATCH]
-    changes = (
-        table_ref[3 * PATCH : 4 * PATCH, start : start + 3 * STEP_HELD] for start in (0, WIDE)
-    )
-    step_table = jnp.where(half == 0, *changes)
-    right = [table_ref[4 * PATCH :, start : start + PATCH] for start in (0, WIDE)]
+        high = parts[image][0]
+        both = jnp.where(lane < SIDE, high, parts[1 - image][1])
+        factors.append(jnp.concatenate([both, high[:, :SIDE]], 1).astype(jnp.bfloat16))
     upper = half == 0
-    inner = lax.broadcasted_iota(jnp.int32, (SUBLANES, 2 * LANES), 0) < PATCH - MARGIN - TOP_CUT
-    every = []
+    start = pl.multiple_of(HALO_AT + side * (3 * SIDE), SIDE)
+    spectra = []
     for column in range(group):
-        spectra = []
-        every.append(spectra)
-        for image in range(2):
-            spot = (2 * column + image) * held
-            halo_spot = spot + PATCH
-
-            def rows_at(upper_start, lower_start, size):
-                start = pl.multiple_of(jnp.where(upper, upper_start, lower_start), SUBLANES)
-                return partial_ref[pl.ds(start, size)]
-
-            low_mix = jnp.where(
-                inner & (half == 1),
-                partial_ref[halo_spot + LOW_CUT : halo_spot + HALO],
-                partial_ref[spot + LOW_CUT : spot + HALO],
-            )
-            top_mix = jnp.where(
-                inner | (half == 1),
-                partial_ref[spot + TOP_CUT : spot + TOP_CUT + SUBLANES],
-                partial_ref[halo_spot : halo_spot + SUBLANES],
-            )
-            window = jnp.concatenate(
-                [
-                    rows_at(spot, halo_spot, LOW_CUT),
-                    low_mix,
-                    partial_ref[spot + HALO : spot + TOP_CUT],
-                    top_mix,
-                    rows_at(halo_spot + SUBLANES, spot + TOP_CUT + SUBLANES, HALO - SUBLANES),
-                ],
-                0,
-            )
-            change = rows_at(spot + TOP_CUT, spot + HALO - STEP_HELD, STEP_HELD)
-            change = change - rows_at(halo_spot, halo_spot + HALO - STEP_HELD, STEP_HELD)
-            near = table_first(whole, window)
-            spectra.append((near, near + table_first(step_table, change)))
-    for column, spectra in enumerate(every):
-        for row in range(2):
-            cross = cross_spectrum(spectra[0][row], spectra[1][row])
-            high, low = halves_of(table_first(left, cross))
-            spot = (row * group + column) * PATCH
-            high_ref[spot : spot + PATCH] = high
-            low_ref[spot : spot + PATCH] = low
+        table = table_ref[pl.ds(start, 3 * SIDE), column * WIDE : (column + 1) * WIDE]
+        for section in range(2):
+            factor = jnp.where(upper, factors[section], factors[1 - section])
+            spot = slice(section * 2 * PATCH, (section + 1) * 2 * PATCH)
+            spectra.append(own_spectra[spot] + dot(factor, table))
+    left = table_ref[LEFT_AT:RIGHT_AT, : 3 * PATCH]
+    right = [table_ref[RIGHT_AT:, start : start + PATCH] for start in (0, WIDE)]
     count = 2 * group
     for patch in range(count):
-        if patch % group == 0:
-            block = slice(patch * PATCH, (patch + group) * PATCH)
+        row, column = patch % 2, patch // 2
+        start = row * PATCH
+        cross = cross_spectrum(
+            *(value[start : start + PATCH] for value in spectra[2 * column : 2 * column + 2])
+        )
+        high, low = halves_of(table_first(left, cross))
+        high_ref[patch * PATCH : (patch + 1) * PATCH] = high
+        low_ref[patch * PATCH : (patch + 1) * PATCH] = low
+    for patch in range(count):
+        if patch % 2 == 0:
+            block = slice(patch * PATCH, (patch + 2) * PATCH)
             correl = dot(high_ref[block], right[0]) + dot(high_ref[block], right[1])
             correl = correl + dot(low_ref[block], right[0])
-        squared = correl[patch % group * PATCH : (patch % group + 1) * PATCH]
+        squared = correl[patch % 2 * PATCH : (patch % 2 + 1) * PATCH]
         squared = squared * squared
         weights = squared * squared
         pieces = [weights[at : at + SUBLANES] for at in range(0, PATCH, SUBLANES)]
@@ -446,21 +417,51 @@
     flow_x = jnp.sum(totals * shift, 1, keepdims=True) / below
     at = lax.broadcasted_iota(jnp.int32, (count, LANES), 1)
     patch = lax.broadcasted_iota(jnp.int32, (count, LANES), 0)
-    second_row = (patch >= group).astype(jnp.int32)
-    row = jnp.where(upper, second_row, 1 - second_row)
-    spot = patch - group * second_row + columns * row + base
+    spot = (patch >> 1) + columns * (patch & 1) + side * group
     line = jnp.where(at == spot, flow_y, 0.0) + jnp.where(at == spot + 2 * count, flow_x, 0.0)
-    line = jnp.sum(line, 0, keepdims=True)
-    if late:
-        line = line + before_ref[...]
-    else:
-        lanes = lax.broadcasted_iota(jnp.int32, (1, LANES), 1)
-        mask = before_ref[0].astype(jnp.float32)
-        for row in range(mask.shape[0]):
-            for column in range(columns):
-                spot = 4 * count + row * columns + column
-                line = jnp.where(lanes == spot, mask[row : row + 1, column : column + 1], line)
-    out_ref[...] = jnp.broadcast_to(line, out_ref.shape)
+    return jnp.sum(line, 0, keepdims=True)
+
+
+def early_kernel(columns, own_ref, other_ref, beyond_ref, early_side_ref, late_side_ref, beside_ref,
+                 mask_ref, table_ref, line_ref, own_spectra_ref, own_side_ref, high_rows_ref,
+                 low_rows_ref, high_ref, low_ref, rows_ref):
+    half = lax.axis_index("gz")
+    side = 1 - lax.rem(lax.axis_index("gx"), 2)
+    images = [
+        jnp.concatenate([tile, beyond_ref[image]], 0)
+        for image, tile in enumerate((own_ref[0], other_ref[0]))
+    ]
+    upper = half == 0
+    one, two = (table_ref[:PATCH, at : at + WIDE] for at in (0, WIDE))
+    for section in range(2):
+        pixels = jnp.where(upper, images[section], images[1 - section])
+        spot = slice(section * 2 * PATCH, (section + 1) * 2 * PATCH)
+        high_rows_ref[spot], low_rows_ref[spot] = halves_of(
+            to_row_frequencies(table_ref, half, pixels)
+        )
+        high, low = high_rows_ref[spot], low_rows_ref[spot]
+        own_spectra_ref[spot] = dot(high, one) + dot(high, two) + dot(low, one)
+    own_side_ref[...] = to_row_frequencies(table_ref, half, late_side_ref[...])
+    own_side = to_row_frequencies(table_ref, half, early_side_ref[...])
+    line = finish(
+        columns, side, own_spectra_ref, own_side, beside_ref, table_ref, high_ref, low_ref, rows_ref
+    )
+    lanes = lax.broadcasted_iota(jnp.int32, (1, LANES), 1)
+    mask = mask_ref[0].astype(jnp.float32)
+    for row in range(mask.shape[0]):
+        for column in range(columns):
+            spot = 4 * columns + row * columns + column
+            line = jnp.where(lanes == spot, mask[row : row + 1, column : column + 1], line)
+    line_ref[...] = line
+
+
+def late_kernel(columns, line_ref, own_spectra_ref, own_side_ref, beside_ref, table_ref, out_ref,
+                high_ref, low_ref, rows_ref):
+    side = lax.rem(lax.axis_index("gx"), 2)
+    line = finish(
+        columns, side, own_spectra_ref, own_side_ref[...], beside_ref, table_ref, high_ref, low_ref, rows_ref
+    )
+    out_ref[...] = jnp.broadcast_to(line_ref[...] + line, out_ref.shape)
 
 
 def relax_kernel(rows, columns, got_ref, flow_ref, offsets_ref):
@@ -588,29 +589,37 @@
     first, second = (lax.ppermute(send, "gx", swap) for send, swap in zip(sends, swaps))
     devices = sections * size_y * size_x
 
-    def flows(late, beside, before, lines):
-        patches = count_x
-        held = PATCH + HALO
-        return pl.pallas_call(
-            functools.partial(flow_kernel, count_x, late),
-            out_shape=jax.ShapeDtypeStruct((lines, LANES), jnp.float32),
-            in_specs=vmem(6),
-            out_specs=vmem(1)[0],
-            scratch_shapes=[
-                pltpu.VMEM((patches * held, PATCH), jnp.bfloat16),
-                pltpu.VMEM((patches * held, 2 * LANES), jnp.float32),
-                pltpu.VMEM((patches * PATCH, 2 * LANES), jnp.bfloat16),
-                pltpu.VMEM((patches * PATCH, 2 * LANES), jnp.bfloat16),
-                pltpu.VMEM((2, patches, PATCH), jnp.float32),
-            ],
-            compiler_params=pltpu.CompilerParams(vmem_limit_bytes=16 * 2**20),
-            cost_estimate=pl.CostEstimate(
-                flops=patches * 2 * 2400 * 256 * 256, bytes_accessed=2**21, transcendentals=0
-            ),
-            name="flows",
-        )(own, other, beyond, beside, before, table)
-
-    lines = flows(True, second, flows(False, first, tissue_mask, 1), devices)
+    patches = rows * count_x // 2
+    common = [
+        pltpu.VMEM((patches * PATCH, WIDE), jnp.bfloat16),
+        pltpu.VMEM((patches * PATCH, WIDE), jnp.bfloat16),
+        pltpu.VMEM((2, patches, PATCH), jnp.float32),
+    ]
+    params = pltpu.CompilerParams(vmem_limit_bytes=16 * 2**20)
+    line, own_spectra, own_side = pl.pallas_call(
+        functools.partial(early_kernel, count_x),
+        out_shape=(
+            jax.ShapeDtypeStruct((1, LANES), jnp.float32),
+            jax.ShapeDtypeStruct((4 * PATCH, WIDE), jnp.float32),
+            jax.ShapeDtypeStruct((2 * PATCH, LANES), jnp.float32),
+        ),
+        in_specs=vmem(8),
+        out_specs=tuple(vmem(3)),
+        scratch_shapes=[pltpu.VMEM((4 * PATCH, PATCH), jnp.bfloat16)] * 2 + common,
+        compiler_params=params,
+        cost_estimate=pl.CostEstimate(flops=2 * 10**9, bytes_accessed=2**21, transcendentals=0),
+        name="early",
+    )(own, other, beyond, sends[1], sends[0], first, tissue_mask, table)
+    lines = pl.pallas_call(
+        functools.partial(late_kernel, count_x),
+        out_shape=jax.ShapeDtypeStruct((devices, LANES), jnp.float32),
+        in_specs=vmem(5),
+        out_specs=vmem(1)[0],
+        scratch_shapes=common,
+        compiler_params=params,
+        cost_estimate=pl.CostEstimate(flops=10**9, bytes_accessed=2**21, transcendentals=0),
+        name="late",
+    )(line, own_spectra, own_side, second, table)
     got = lax.all_to_all(lines, ("gz", "gy", "gx"), 0, 0, tiled=True)
     return pl.pallas_call(
         functools.partial(relax_kernel, rows, count_x),

time: 33.8 us -> 33.5 us (level)
  blocking collectives: 15.2 us -> 14.8 us
    all_to_all x1, blocking collectives: 15.2 us -> 14.8 us  [pair_body(): got = lax.all_to_all(lines, ('gz', 'gy', 'gx'), 0, 0, tiled=True)]
  transfers between devices with their start and end apart: 4 -> 4, of which waited for: 3 -> 2; matrix products, arithmetic and copies ran while one was open for 0% -> 0% of each run, Pallas kernels for 6% -> 7%
where the time goes in v6:
time: 33.5 us; the launch traced here: 33.3 us
  blocking collectives  14.8 us (44%)
  starting transfers between devices  7.75 us (23%)
  Pallas kernels  5.31 us (16%)
  waiting for transfers between devices  2.48 us (7%)
  local copies, waits for them, and re-layouts  2.32 us (7%)
  between operations  0.69 us (2%)
    all_to_all x1, blocking collectives, pair_body(): got = lax.all_to_all(lines, ('gz', 'gy', 'gx'), 0, 0, tiled=True)  14.8 us
    ppermute x1, starting transfers between devices, pair_body(): beyond = lax.ppermute(edge, ('gz', 'gy'), onward)  3.98 us
    ppermute x1, starting transfers between devices, pair_body(): other = lax.ppermute(images, 'gz', [(0, 1), (1, 0)])  3.03 us
    unnamed x6, local copies, waits for them, and re-layouts  2.32 us
    pallas_call x1, Pallas kernels, pair_body(): pl.pallas_call(functools.partial(early_kernel, count_x), out_shape=(jax.S...  2.17 us
    ppermute x1, waiting for transfers between devices, pair_body(): beyond = lax.ppermute(edge, ('gz', 'gy'), onward)  1.88 us
    pallas_call x1, Pallas kernels, pair_body(): pl.pallas_call(functools.partial(late_kernel, count_x), out_shape=jax.Sha...  1.51 us
    pallas_call x1, Pallas kernels, pair_body(): pl.pallas_call(functools.partial(relax_kernel, rows, count_x), out_shape=...  1.12 us
  transfers between devices with their start and end apart: 4, of which 2 were waited for; matrix products, arithmetic and copies ran while one was open for 0% of the time, Pallas kernels for 7%

profile of v6, /device:TPU:0, one launch (start us, length us, event | category | flops | bytes accessed | tf_op | source)
XLA Modules:
  0.0 33.3 jit_solution(7744745840964557581)
XLA Ops:
  0.6 3.0 %collective-permute-start = (bf16[1,160,160]{2,1,0:T(8,128)(2,1)}, bf16[1,160,160]{2,1,0:T(8,128)(2,1)S(1)}, u32[]{:S(2)}, u32[]{:S(2)}) collective-permute-start(bf16[1,160,160]{2,1,0:T(8,128)(2,1)} %own_ref.1), channel_id=1, source_target_pairs={{0,16},{16,0},{1,17},{17,1},{2,18},{18,2},{3,19},{19,3},{4,20},{20... | collective-permute-start | bytes 153608 | tf_op jit(solution)/shard_map/ppermute | solution.py:549
  3.7 0.0 copy-start
  3.7 1.4 %copy-done = bf16[1600,512]{1,0:T(8,128)(2,1)S(1)} copy-done((bf16[1600,512]{1,0:T(8,128)(2,1)S(1)}, bf16[1600,512]{1,0:T(8,128)(2,1)}, u32[]{:S(2)}) %copy-start) | copy-done | bytes 1638424
  5.1 0.0 copy-start.1
  5.1 0.9 %copy-done.1 = bf16[1,160,160]{2,1,0:T(8,128)(2,1)S(1)} copy-done((bf16[1,160,160]{2,1,0:T(8,128)(2,1)S(1)}, bf16[1,160,160]{2,1,0:T(8,128)(2,1)}, u32[]{:S(2)}) %copy-start.1) | copy-done | bytes 51224
  6.0 0.0 copy-start.2
  6.0 0.3 load.1
  6.3 0.0 collective-permute-done.other_ref
  6.3 4.0 %collective-permute-start.1 = (bf16[2,64,160]{2,1,0:T(8,128)(2,1)S(1)}, bf16[2,64,160]{2,1,0:T(8,128)(2,1)S(1)}, u32[]{:S(2)}, u32[]{:S(2)}) collective-permute-start(bf16[2,64,160]{2,1,0:T(8,128)(2,1)S(1)} %edge.1), channel_id=1, source_target_pairs={{0,4},{20,16},{4,8},{24,20},{8,12},{28,24},{1,5},{21,17},{5,9},{25... | collective-permute-start | bytes 122888 | tf_op jit(solution)/shard_map/ppermute | solution.py:575
  10.3 1.9 %collective-permute-done.1.beyond_ref = bf16[2,64,160]{2,1,0:T(8,128)(2,1)S(1)} collective-permute-done((bf16[2,64,160]{2,1,0:T(8,128)(2,1)S(1)}, bf16[2,64,160]{2,1,0:T(8,128)(2,1)S(1)}, u32[]{:S(2)}, u32[]{:S(2)}) %collective-permute-start.1) | collective-permute-done | bytes 40992 | tf_op jit(solution)/shard_map/ppermute | solution.py:575
  12.2 0.2 pack.1
  12.4 0.1 collective-permute-start.2
  12.5 0.7 %collective-permute-start.3 = (bf16[224,128]{1,0:T(8,128)(2,1)S(1)}, bf16[224,128]{1,0:T(8,128)(2,1)S(1)}, u32[]{:S(2)}, u32[]{:S(2)}) collective-permute-start(bf16[224,128]{1,0:T(8,128)(2,1)S(1)} %get-tuple-element.10.early_side_ref), channel_id=1, source_target_pairs={{1,2},{2,1},{5,6},{6,5},{9,10},{10,9},{13,14},{14,13},{17,18},{18,... | collective-permute-start | bytes 172040 | tf_op jit(solution)/shard_map/ppermute | solution.py:589
  13.2 0.6 %collective-permute-done.2.beside_ref = bf16[224,128]{1,0:T(8,128)(2,1)S(1)} collective-permute-done((bf16[224,128]{1,0:T(8,128)(2,1)S(1)}, bf16[224,128]{1,0:T(8,128)(2,1)S(1)}, u32[]{:S(2)}, u32[]{:S(2)}) %collective-permute-start.2) | collective-permute-done | bytes 57376 | tf_op jit(solution)/shard_map/ppermute | solution.py:589
  13.7 0.0 copy-done.2
  13.7 2.2 %early.1 = (f32[1,128]{1,0:T(1,128)S(1)}, f32[640,256]{1,0:T(8,128)S(1)}, f32[320,128]{1,0:T(8,128)S(1)}) custom-call(bf16[1,160,160]{2,1,0:T(8,128)(2,1)S(1)} %get-tuple-element.9.own_ref, bf16[1,160,160]{2,1,0:T(8,128)(2,1)S(1)} %collective-permute-done.other_ref, bf16[2,64,160]{2,1,0:T(8,128)(2,1)S(1)} %collective-permute-done.1.beyond_ref, ...), custom_call_target="tpu_custom_call" | custom-call | flops 2000000000 | bytes 2097152 | tf_op jit(solution)/shard_map/early/pallas_call | solution.py:599
  15.9 0.0 collective-permute-done.3.beside_ref
  15.9 1.5 %late.1 = f32[32,128]{1,0:T(8,128)S(1)} custom-call(f32[1,128]{1,0:T(1,128)S(1)} %get-tuple-element.13.line_ref, f32[640,256]{1,0:T(8,128)S(1)} %get-tuple-element.14.own_spectra_ref, f32[320,128]{1,0:T(8,128)S(1)} %get-tuple-element.15.own_side_ref, bf16[224,128]{1,0:T(8,128)(2,1)S(1)} %collective-permute-done.3.beside_ref, ...), custom_call_target="tpu_custom_call" | custom-call | flops 1000000000 | bytes 2097152 | tf_op jit(solution)/shard_map/late/pallas_call | solution.py:613
  17.4 14.8 %all_to_all.11 = f32[32,1,128]{2,1,0:T(1,128)S(1)} all-to-all(f32[32,1,128]{2,1,0:T(1,128)S(1)} %bitcast.5), channel_id=1, replica_groups=mesh['gz'=2,'gy'=4,'gx'=4] {'gz','gy','gx'}, dimensions={0} | all-to-all | bytes 32768 | tf_op jit(solution)/shard_map/all_to_all | solution.py:623
  32.2 1.1 %relax.1 = (f32[4,1,4,4]{3,2,1,0:T(4,128)}, f32[2,1,4,4]{3,2,1,0:T(4,128)}) custom-call(f32[32,128]{1,0:T(8,128)S(1)} %bitcast.4), custom_call_target="tpu_custom_call" | custom-call | tf_op jit(solution)/shard_map/relax/pallas_call | solution.py:624
  (1 shorter events, 0.0 us)
Async XLA Ops:
  0.6 5.7 %collective-permute-start = (bf16[1,160,160]{2,1,0:T(8,128)(2,1)}, bf16[1,160,160]{2,1,0:T(8,128)(2,1)S(1)}, u32[]{:S(2)}, u32[]{:S(2)}) collective-permute-start(bf16[1,160,160]{2,1,0:T(8,128)(2,1)} %own_ref.1), channel_id=1, source_target_pairs={{0,16},{16,0},{1,17},{17,1},{2,18},{18,2},{3,19},{19,3},{4,20},{20... | collective-permute-start | bytes 153608 | tf_op jit(solution)/shard_map/ppermute | solution.py:549
  3.7 1.4 %copy-start = (bf16[1600,512]{1,0:T(8,128)(2,1)S(1)}, bf16[1600,512]{1,0:T(8,128)(2,1)}, u32[]{:S(2)}) copy-start(bf16[1600,512]{1,0:T(8,128)(2,1)} %constant.2.clone.table_ref) | copy-start | bytes 4915204
  5.1 0.9 %copy-start.1 = (bf16[1,160,160]{2,1,0:T(8,128)(2,1)S(1)}, bf16[1,160,160]{2,1,0:T(8,128)(2,1)}, u32[]{:S(2)}) copy-start(bf16[1,160,160]{2,1,0:T(8,128)(2,1)} %own_ref.1) | copy-start | bytes 153604
  6.0 7.7 %copy-start.2 = (s32[1,4,4]{2,1,0:T(4,128)S(1)}, s32[1,4,4]{2,1,0:T(4,128)}, u32[]{:S(2)}) copy-start(s32[1,4,4]{2,1,0:T(4,128)} %mask_ref.1) | copy-start | bytes 196
  6.3 5.9 %collective-permute-start.1 = (bf16[2,64,160]{2,1,0:T(8,128)(2,1)S(1)}, bf16[2,64,160]{2,1,0:T(8,128)(2,1)S(1)}, u32[]{:S(2)}, u32[]{:S(2)}) collective-permute-start(bf16[2,64,160]{2,1,0:T(8,128)(2,1)S(1)} %edge.1), channel_id=1, source_target_pairs={{0,4},{20,16},{4,8},{24,20},{8,12},{28,24},{1,5},{21,17},{5,9},{25... | collective-permute-start | bytes 122888 | tf_op jit(solution)/shard_map/ppermute | solution.py:575
  12.4 1.3 %collective-permute-start.2 = (bf16[224,128]{1,0:T(8,128)(2,1)S(1)}, bf16[224,128]{1,0:T(8,128)(2,1)S(1)}, u32[]{:S(2)}, u32[]{:S(2)}) collective-permute-start(bf16[224,128]{1,0:T(8,128)(2,1)S(1)} %get-tuple-element.11.late_side_ref), channel_id=1, source_target_pairs={{0,1},{1,0},{2,3},{3,2},{4,5},{5,4},{6,7},{7,6},{8,9},{9,8},{10,11... | collective-permute-start | bytes 172040 | tf_op jit(solution)/shard_map/ppermute | solution.py:589
  12.5 3.4 %collective-permute-start.3 = (bf16[224,128]{1,0:T(8,128)(2,1)S(1)}, bf16[224,128]{1,0:T(8,128)(2,1)S(1)}, u32[]{:S(2)}, u32[]{:S(2)}) collective-permute-start(bf16[224,128]{1,0:T(8,128)(2,1)S(1)} %get-tuple-element.10.early_side_ref), channel_id=1, source_target_pairs={{1,2},{2,1},{5,6},{6,5},{9,10},{10,9},{13,14},{14,13},{17,18},{18,... | collective-permute-start | bytes 172040 | tf_op jit(solution)/shard_map/ppermute | solution.py:589

commit v7 on v6

--- a/solution.py
+++ b/solution.py
@@ -316,29 +316,56 @@
         copy.wait()
 
 
+def repeated(tail):
+    return jnp.concatenate([tail] * (LANES // (PATCH - LANES)), 1)
+
+
 def edge_kernel(own_ref, other_ref, out_ref):
     start = pl.multiple_of(jnp.where(lax.axis_index("gz") == 0, PATCH - HALO, 0), HALO // 2)
-    out_ref[0] = own_ref[0, pl.ds(start, HALO)]
-    out_ref[1] = other_ref[0, pl.ds(start, HALO)]
-
-
-def pack_kernel(own_ref, other_ref, beyond_ref, first_ref, second_ref):
-    wide, narrow = [], []
-    for image in range(2):
-        tile = own_ref[0] if image == 0 else other_ref[0]
-        tall = jnp.concatenate([tile, beyond_ref[image]], 0).astype(jnp.float32)
-        wide.append(tall[:, :LANES])
-        narrow.append(jnp.concatenate([tall[:, LANES:]] * (LANES // (PATCH - LANES)), 1))
+    rows = [ref[0, pl.ds(start, HALO)].astype(jnp.float32) for ref in (own_ref, other_ref)]
+    lane = lax.broadcasted_iota(jnp.int32, (HALO, LANES), 1)
+    tails = [repeated(value[:, LANES:]) for value in rows]
+    tail = jnp.where(lane < PATCH - LANES, *tails)
+    parts = [rows[0][:, :LANES], rows[1][:, :LANES], tail]
+    out_ref[...] = jnp.concatenate(parts, 1).astype(jnp.bfloat16)
+
+
+def edge_rows(beyond_ref):
+    tail = beyond_ref[:, 2 * LANES :].astype(jnp.float32)
+    turned = pltpu.roll(tail, LANES - (PATCH - LANES), 1)
+    return [
+        jnp.concatenate(
+            [
+                beyond_ref[:, image * LANES : (image + 1) * LANES],
+                value[:, : PATCH - LANES].astype(jnp.bfloat16),
+            ],
+            1,
+        )
+        for image, value in enumerate((tail, turned))
+    ]
+
+
+def side_columns(tiles):
+    tiles = [tile.astype(jnp.float32) for tile in tiles]
+    wide = [tile[:, :LANES] for tile in tiles]
+    narrow = [repeated(tile[:, LANES:]) for tile in tiles]
     lane = lax.broadcasted_iota(jnp.int32, wide[0].shape, 1)
-    middle = LANES // 2
     extra = PATCH - LANES
-    low = jnp.where(lane < middle, wide[0], pltpu.roll(wide[1], middle, 1))
-    high = jnp.where(lane < middle, pltpu.roll(wide[0], middle, 1), wide[1])
+    low = jnp.where(lane < SIDE, wide[0], pltpu.roll(wide[1], SIDE, 1))
+    high = jnp.where(lane < SIDE, pltpu.roll(wide[0], SIDE, 1), wide[1])
     high = jnp.where(lane < extra, narrow[0], high)
-    high = jnp.where((lane >= middle) & (lane < middle + extra), narrow[1], high)
+    high = jnp.where((lane >= SIDE) & (lane < SIDE + extra), narrow[1], high)
     odd = lax.rem(lax.axis_index("gx"), 2) == 1
-    first_ref[...] = jnp.where(odd, low, high).astype(jnp.bfloat16)
-    second_ref[...] = jnp.where(odd, high, low).astype(jnp.bfloat16)
+    return [jnp.where(odd, *pair).astype(jnp.bfloat16) for pair in ((low, high), (high, low))]
+
+
+def pack_kernel(own_ref, other_ref, first_ref, second_ref):
+    first_ref[:PATCH], second_ref[:PATCH] = side_columns([own_ref[0], other_ref[0]])
+
+
+def pack_edge_kernel(beyond_ref, first_in, second_in, first_ref, second_ref):
+    del first_in, second_in
+    first_ref[PATCH:], second_ref[PATCH:] = side_columns(edge_rows(beyond_ref))
 
 
 def to_row_frequencies(table_ref, half, pixels):
@@ -427,10 +454,8 @@
                  low_rows_ref, high_ref, low_ref, rows_ref):
     half = lax.axis_index("gz")
     side = 1 - lax.rem(lax.axis_index("gx"), 2)
-    images = [
-        jnp.concatenate([tile, beyond_ref[image]], 0)
-        for image, tile in enumerate((own_ref[0], other_ref[0]))
-    ]
+    tiles = (own_ref[0], other_ref[0])
+    images = [jnp.concatenate(pair, 0) for pair in zip(tiles, edge_rows(beyond_ref))]
     upper = half == 0
     one, two = (table_ref[:PATCH, at : at + WIDE] for at in (0, WIDE))
     for section in range(2):
@@ -563,7 +588,7 @@
     )(images, table)
     edge = pl.pallas_call(
         edge_kernel,
-        out_shape=jax.ShapeDtypeStruct((2, HALO, PATCH), jnp.bfloat16),
+        out_shape=jax.ShapeDtypeStruct((HALO, 3 * LANES), jnp.bfloat16),
         in_specs=vmem(2),
         out_specs=vmem(1)[0],
         compiler_params=pltpu.CompilerParams(vmem_limit_bytes=4 * 2**20),
@@ -577,15 +602,26 @@
         [pair for left in range(offset, size_x - 1, 2) for pair in ((left, left + 1), (left + 1, left))]
         for offset in range(2)
     ]
-    packed = jax.ShapeDtypeStruct((PATCH + HALO, LANES), jnp.bfloat16)
+    packed = jax.ShapeDtypeStruct((HELD, LANES), jnp.bfloat16)
+    small = pltpu.CompilerParams(vmem_limit_bytes=4 * 2**20)
     sends = pl.pallas_call(
         pack_kernel,
         out_shape=(packed, packed),
+        in_specs=vmem(2),
+        out_specs=tuple(vmem(2)),
+        compiler_params=small,
+        cost_estimate=pl.CostEstimate(flops=10**6, bytes_accessed=2**18, transcendentals=0),
+        name="pack",
+    )(own, other)
+    sends = pl.pallas_call(
+        pack_edge_kernel,
+        out_shape=(packed, packed),
         in_specs=vmem(3),
         out_specs=tuple(vmem(2)),
-        compiler_params=pltpu.CompilerParams(vmem_limit_bytes=4 * 2**20),
-        name="pack",
-    )(own, other, beyond)
+        input_output_aliases={1: 0, 2: 1},
+        compiler_params=small,
+        name="pack_edge",
+    )(beyond, *sends)
     first, second = (lax.ppermute(send, "gx", swap) for send, swap in zip(sends, swaps))
     devices = sections * size_y * size_x
 

time: 33.5 us -> 33.4 us (level)
  transfers between devices with their start and end apart: 4 -> 4, of which waited for: 2 -> 2; matrix products, arithmetic and copies ran while one was open for 0% -> 0% of each run, Pallas kernels for 7% -> 8%
where the time goes in v7:
time: 33.4 us; the launch traced here: 33.2 us
  blocking collectives  14.7 us (44%)
  starting transfers between devices  7.76 us (23%)
  Pallas kernels  5.51 us (16%)
  local copies, waits for them, and re-layouts  2.32 us (7%)
  waiting for transfers between devices  2.15 us (6%)
  between operations  0.71 us (2%)
    all_to_all x1, blocking collectives, pair_body(): got = lax.all_to_all(lines, ('gz', 'gy', 'gx'), 0, 0, tiled=True)  14.7 us
    ppermute x1, starting transfers between devices, pair_body(): beyond = lax.ppermute(edge, ('gz', 'gy'), onward)  3.99 us
    ppermute x1, starting transfers between devices, pair_body(): other = lax.ppermute(images, 'gz', [(0, 1), (1, 0)])  3.03 us
    unnamed x6, local copies, waits for them, and re-layouts  2.32 us
    pallas_call x1, Pallas kernels, pair_body(): pl.pallas_call(functools.partial(early_kernel, count_x), out_shape=(jax.S...  2.2 us
    ppermute x1, waiting for transfers between devices, pair_body(): beyond = lax.ppermute(edge, ('gz', 'gy'), onward)  1.56 us
    pallas_call x1, Pallas kernels, pair_body(): pl.pallas_call(functools.partial(late_kernel, count_x), out_shape=jax.Sha...  1.47 us
    pallas_call x1, Pallas kernels, pair_body(): pl.pallas_call(functools.partial(relax_kernel, rows, count_x), out_shape=...  1.12 us
  transfers between devices with their start and end apart: 4, of which 2 were waited for; matrix products, arithmetic and copies ran while one was open for 0% of the time, Pallas kernels for 8%

profile of v7, /device:TPU:0, one launch (start us, length us, event | category | flops | bytes accessed | tf_op | source)
XLA Modules:
  0.0 33.2 jit_solution(14321424206217660383)
XLA Ops:
  0.6 3.0 %collective-permute-start = (bf16[1,160,160]{2,1,0:T(8,128)(2,1)}, bf16[1,160,160]{2,1,0:T(8,128)(2,1)S(1)}, u32[]{:S(2)}, u32[]{:S(2)}) collective-permute-start(bf16[1,160,160]{2,1,0:T(8,128)(2,1)} %own_ref.1), channel_id=1, source_target_pairs={{0,16},{16,0},{1,17},{17,1},{2,18},{18,2},{3,19},{19,3},{4,20},{20... | collective-permute-start | bytes 153608 | tf_op jit(solution)/shard_map/ppermute | solution.py:574
  3.7 0.0 copy-start
  3.7 1.4 %copy-done = bf16[1600,512]{1,0:T(8,128)(2,1)S(1)} copy-done((bf16[1600,512]{1,0:T(8,128)(2,1)S(1)}, bf16[1600,512]{1,0:T(8,128)(2,1)}, u32[]{:S(2)}) %copy-start) | copy-done | bytes 1638424
  5.1 0.0 copy-start.1
  5.1 0.9 %copy-done.1 = bf16[1,160,160]{2,1,0:T(8,128)(2,1)S(1)} copy-done((bf16[1,160,160]{2,1,0:T(8,128)(2,1)S(1)}, bf16[1,160,160]{2,1,0:T(8,128)(2,1)}, u32[]{:S(2)}) %copy-start.1) | copy-done | bytes 51224
  6.0 0.0 copy-start.2
  6.0 0.3 load.1
  6.3 0.0 collective-permute-done.other_ref
  6.3 0.1 edge.1
  6.4 4.0 %collective-permute-start.1 = (bf16[64,384]{1,0:T(8,128)(2,1)S(1)}, bf16[64,384]{1,0:T(8,128)(2,1)S(1)}, u32[]{:S(2)}, u32[]{:S(2)}) collective-permute-start(bf16[64,384]{1,0:T(8,128)(2,1)S(1)} %edge.1), channel_id=1, source_target_pairs={{0,4},{20,16},{4,8},{24,20},{8,12},{28,24},{1,5},{21,17},{5,9},{25... | collective-permute-start | bytes 147464 | tf_op jit(solution)/shard_map/ppermute | solution.py:600
  10.4 0.2 pack.1
  10.6 1.6 %collective-permute-done.1.beyond_ref = bf16[64,384]{1,0:T(8,128)(2,1)S(1)} collective-permute-done((bf16[64,384]{1,0:T(8,128)(2,1)S(1)}, bf16[64,384]{1,0:T(8,128)(2,1)S(1)}, u32[]{:S(2)}, u32[]{:S(2)}) %collective-permute-start.1) | collective-permute-done | bytes 49184 | tf_op jit(solution)/shard_map/ppermute | solution.py:600
  12.1 0.2 pack_edge.1
  12.3 0.1 collective-permute-start.2
  12.4 0.7 %collective-permute-start.3 = (bf16[224,128]{1,0:T(8,128)(2,1)S(1)}, bf16[224,128]{1,0:T(8,128)(2,1)S(1)}, u32[]{:S(2)}, u32[]{:S(2)}) collective-permute-start(bf16[224,128]{1,0:T(8,128)(2,1)S(1)} %get-tuple-element.14.early_side_ref), channel_id=1, source_target_pairs={{1,2},{2,1},{5,6},{6,5},{9,10},{10,9},{13,14},{14,13},{17,18},{18,... | collective-permute-start | bytes 172040 | tf_op jit(solution)/shard_map/ppermute | solution.py:625
  13.1 0.6 %collective-permute-done.2.beside_ref = bf16[224,128]{1,0:T(8,128)(2,1)S(1)} collective-permute-done((bf16[224,128]{1,0:T(8,128)(2,1)S(1)}, bf16[224,128]{1,0:T(8,128)(2,1)S(1)}, u32[]{:S(2)}, u32[]{:S(2)}) %collective-permute-start.2) | collective-permute-done | bytes 57376 | tf_op jit(solution)/shard_map/ppermute | solution.py:625
  13.6 0.0 copy-done.2
  13.6 2.2 %early.1 = (f32[1,128]{1,0:T(1,128)S(1)}, f32[640,256]{1,0:T(8,128)S(1)}, f32[320,128]{1,0:T(8,128)S(1)}) custom-call(bf16[1,160,160]{2,1,0:T(8,128)(2,1)S(1)} %get-tuple-element.11.own_ref, bf16[1,160,160]{2,1,0:T(8,128)(2,1)S(1)} %collective-permute-done.other_ref, bf16[64,384]{1,0:T(8,128)(2,1)S(1)} %collective-permute-done.1.beyond_ref, ...), custom_call_target="tpu_custom_call" | custom-call | flops 2000000000 | bytes 2097152 | tf_op jit(solution)/shard_map/early/pallas_call | solution.py:635
  15.8 0.0 collective-permute-done.3.beside_ref
  15.8 1.5 %late.1 = f32[32,128]{1,0:T(8,128)S(1)} custom-call(f32[1,128]{1,0:T(1,128)S(1)} %get-tuple-element.17.line_ref, f32[640,256]{1,0:T(8,128)S(1)} %get-tuple-element.18.own_spectra_ref, f32[320,128]{1,0:T(8,128)S(1)} %get-tuple-element.19.own_side_ref, bf16[224,128]{1,0:T(8,128)(2,1)S(1)} %collective-permute-done.3.beside_ref, ...), custom_call_target="tpu_custom_call" | custom-call | flops 1000000000 | bytes 2097152 | tf_op jit(solution)/shard_map/late/pallas_call | solution.py:649
  17.3 14.7 %all_to_all.11 = f32[32,1,128]{2,1,0:T(1,128)S(1)} all-to-all(f32[32,1,128]{2,1,0:T(1,128)S(1)} %bitcast.5), channel_id=1, replica_groups=mesh['gz'=2,'gy'=4,'gx'=4] {'gz','gy','gx'}, dimensions={0} | all-to-all | bytes 32768 | tf_op jit(solution)/shard_map/all_to_all | solution.py:659
  32.0 1.1 %relax.1 = (f32[4,1,4,4]{3,2,1,0:T(4,128)}, f32[2,1,4,4]{3,2,1,0:T(4,128)}) custom-call(f32[32,128]{1,0:T(8,128)S(1)} %bitcast.4), custom_call_target="tpu_custom_call" | custom-call | tf_op jit(solution)/shard_map/relax/pallas_call | solution.py:660
Async XLA Ops:
  0.6 5.7 %collective-permute-start = (bf16[1,160,160]{2,1,0:T(8,128)(2,1)}, bf16[1,160,160]{2,1,0:T(8,128)(2,1)S(1)}, u32[]{:S(2)}, u32[]{:S(2)}) collective-permute-start(bf16[1,160,160]{2,1,0:T(8,128)(2,1)} %own_ref.1), channel_id=1, source_target_pairs={{0,16},{16,0},{1,17},{17,1},{2,18},{18,2},{3,19},{19,3},{4,20},{20... | collective-permute-start | bytes 153608 | tf_op jit(solution)/shard_map/ppermute | solution.py:574
  3.7 1.4 %copy-start = (bf16[1600,512]{1,0:T(8,128)(2,1)S(1)}, bf16[1600,512]{1,0:T(8,128)(2,1)}, u32[]{:S(2)}) copy-start(bf16[1600,512]{1,0:T(8,128)(2,1)} %constant.2.clone.table_ref) | copy-start | bytes 4915204
  5.1 0.9 %copy-start.1 = (bf16[1,160,160]{2,1,0:T(8,128)(2,1)S(1)}, bf16[1,160,160]{2,1,0:T(8,128)(2,1)}, u32[]{:S(2)}) copy-start(bf16[1,160,160]{2,1,0:T(8,128)(2,1)} %own_ref.1) | copy-start | bytes 153604
  6.0 7.6 %copy-start.2 = (s32[1,4,4]{2,1,0:T(4,128)S(1)}, s32[1,4,4]{2,1,0:T(4,128)}, u32[]{:S(2)}) copy-start(s32[1,4,4]{2,1,0:T(4,128)} %mask_ref.1) | copy-start | bytes 196
  6.4 5.7 %collective-permute-start.1 = (bf16[64,384]{1,0:T(8,128)(2,1)S(1)}, bf16[64,384]{1,0:T(8,128)(2,1)S(1)}, u32[]{:S(2)}, u32[]{:S(2)}) collective-permute-start(bf16[64,384]{1,0:T(8,128)(2,1)S(1)} %edge.1), channel_id=1, source_target_pairs={{0,4},{20,16},{4,8},{24,20},{8,12},{28,24},{1,5},{21,17},{5,9},{25... | collective-permute-start | bytes 147464 | tf_op jit(solution)/shard_map/ppermute | solution.py:600
  12.3 1.3 %collective-permute-start.2 = (bf16[224,128]{1,0:T(8,128)(2,1)S(1)}, bf16[224,128]{1,0:T(8,128)(2,1)S(1)}, u32[]{:S(2)}, u32[]{:S(2)}) collective-permute-start(bf16[224,128]{1,0:T(8,128)(2,1)S(1)} %get-tuple-element.15.late_side_ref), channel_id=1, source_target_pairs={{0,1},{1,0},{2,3},{3,2},{4,5},{5,4},{6,7},{7,6},{8,9},{9,8},{10,11... | collective-permute-start | bytes 172040 | tf_op jit(solution)/shard_map/ppermute | solution.py:625
  12.4 3.4 %collective-permute-start.3 = (bf16[224,128]{1,0:T(8,128)(2,1)S(1)}, bf16[224,128]{1,0:T(8,128)(2,1)S(1)}, u32[]{:S(2)}, u32[]{:S(2)}) collective-permute-start(bf16[224,128]{1,0:T(8,128)(2,1)S(1)} %get-tuple-element.14.early_side_ref), channel_id=1, source_target_pairs={{1,2},{2,1},{5,6},{6,5},{9,10},{10,9},{13,14},{14,13},{17,18},{18,... | collective-permute-start | bytes 172040 | tf_op jit(solution)/shard_map/ppermute | solution.py:625

commit v8 on v7

--- a/solution.py
+++ b/solution.py
@@ -369,7 +369,7 @@
 
 
 def to_row_frequencies(table_ref, half, pixels):
-    start = pl.multiple_of(ROWS_AT + half * (2 * PATCH), PATCH)
+    start = pl.multiple_of(ROWS_AT + half * (2 * PATCH), HALO // 2)
     high = table_ref[pl.ds(start, 2 * PATCH), :HELD]
     low = table_ref[pl.ds(start, 2 * PATCH), WIDE : WIDE + HELD]
     return dot(high, pixels) + dot(low, pixels)
@@ -390,7 +390,7 @@
         both = jnp.where(lane < SIDE, high, parts[1 - image][1])
         factors.append(jnp.concatenate([both, high[:, :SIDE]], 1).astype(jnp.bfloat16))
     upper = half == 0
-    start = pl.multiple_of(HALO_AT + side * (3 * SIDE), SIDE)
+    start = pl.multiple_of(HALO_AT + side * (3 * SIDE), HALO // 2)
     spectra = []
     for column in range(group):
         table = table_ref[pl.ds(start, 3 * SIDE), column * WIDE : (column + 1) * WIDE]

time: 33.4 us -> 33.4 us (level)
  no operation moved by 1% of the time
where the time goes in v8:
time: 33.4 us; the launch traced here: 33.2 us
  blocking collectives  14.7 us (44%)
  starting transfers between devices  7.76 us (23%)
  Pallas kernels  5.51 us (16%)
  local copies, waits for them, and re-layouts  2.32 us (7%)
  waiting for transfers between devices  2.15 us (6%)
  between operations  0.71 us (2%)
    all_to_all x1, blocking collectives, pair_body(): got = lax.all_to_all(lines, ('gz', 'gy', 'gx'), 0, 0, tiled=True)  14.7 us
    ppermute x1, starting transfers between devices, pair_body(): beyond = lax.ppermute(edge, ('gz', 'gy'), onward)  3.99 us
    ppermute x1, starting transfers between devices, pair_body(): other = lax.ppermute(images, 'gz', [(0, 1), (1, 0)])  3.03 us
    unnamed x6, local copies, waits for them, and re-layouts  2.32 us
    pallas_call x1, Pallas kernels, pair_body(): pl.pallas_call(functools.partial(early_kernel, count_x), out_shape=(jax.S...  2.2 us
    ppermute x1, waiting for transfers between devices, pair_body(): beyond = lax.ppermute(edge, ('gz', 'gy'), onward)  1.56 us
    pallas_call x1, Pallas kernels, pair_body(): pl.pallas_call(functools.partial(late_kernel, count_x), out_shape=jax.Sha...  1.47 us
    pallas_call x1, Pallas kernels, pair_body(): pl.pallas_call(functools.partial(relax_kernel, rows, count_x), out_shape=...  1.12 us
  transfers between devices with their start and end apart: 4, of which 2 were waited for; matrix products, arithmetic and copies ran while one was open for 0% of the time, Pallas kernels for 8%

profile of v8, /device:TPU:0, one launch (start us, length us, event | category | flops | bytes accessed | tf_op | source)
XLA Modules:
  0.0 33.2 jit_solution(14321424206217660383)
XLA Ops:
  0.6 3.0 %collective-permute-start = (bf16[1,160,160]{2,1,0:T(8,128)(2,1)}, bf16[1,160,160]{2,1,0:T(8,128)(2,1)S(1)}, u32[]{:S(2)}, u32[]{:S(2)}) collective-permute-start(bf16[1,160,160]{2,1,0:T(8,128)(2,1)} %own_ref.1), channel_id=1, source_target_pairs={{0,16},{16,0},{1,17},{17,1},{2,18},{18,2},{3,19},{19,3},{4,20},{20... | collective-permute-start | bytes 153608 | tf_op jit(solution)/shard_map/ppermute | solution.py:574
  3.7 0.0 copy-start
  3.7 1.4 %copy-done = bf16[1600,512]{1,0:T(8,128)(2,1)S(1)} copy-done((bf16[1600,512]{1,0:T(8,128)(2,1)S(1)}, bf16[1600,512]{1,0:T(8,128)(2,1)}, u32[]{:S(2)}) %copy-start) | copy-done | bytes 1638424
  5.1 0.0 copy-start.1
  5.1 0.9 %copy-done.1 = bf16[1,160,160]{2,1,0:T(8,128)(2,1)S(1)} copy-done((bf16[1,160,160]{2,1,0:T(8,128)(2,1)S(1)}, bf16[1,160,160]{2,1,0:T(8,128)(2,1)}, u32[]{:S(2)}) %copy-start.1) | copy-done | bytes 51224
  6.0 0.0 copy-start.2
  6.0 0.3 load.1
  6.3 0.0 collective-permute-done.other_ref
  6.3 0.1 edge.1
  6.4 4.0 %collective-permute-start.1 = (bf16[64,384]{1,0:T(8,128)(2,1)S(1)}, bf16[64,384]{1,0:T(8,128)(2,1)S(1)}, u32[]{:S(2)}, u32[]{:S(2)}) collective-permute-start(bf16[64,384]{1,0:T(8,128)(2,1)S(1)} %edge.1), channel_id=1, source_target_pairs={{0,4},{20,16},{4,8},{24,20},{8,12},{28,24},{1,5},{21,17},{5,9},{25... | collective-permute-start | bytes 147464 | tf_op jit(solution)/shard_map/ppermute | solution.py:600
  10.4 0.2 pack.1
  10.6 1.6 %collective-permute-done.1.beyond_ref = bf16[64,384]{1,0:T(8,128)(2,1)S(1)} collective-permute-done((bf16[64,384]{1,0:T(8,128)(2,1)S(1)}, bf16[64,384]{1,0:T(8,128)(2,1)S(1)}, u32[]{:S(2)}, u32[]{:S(2)}) %collective-permute-start.1) | collective-permute-done | bytes 49184 | tf_op jit(solution)/shard_map/ppermute | solution.py:600
  12.1 0.2 pack_edge.1
  12.3 0.1 collective-permute-start.2
  12.4 0.7 %collective-permute-start.3 = (bf16[224,128]{1,0:T(8,128)(2,1)S(1)}, bf16[224,128]{1,0:T(8,128)(2,1)S(1)}, u32[]{:S(2)}, u32[]{:S(2)}) collective-permute-start(bf16[224,128]{1,0:T(8,128)(2,1)S(1)} %get-tuple-element.14.early_side_ref), channel_id=1, source_target_pairs={{1,2},{2,1},{5,6},{6,5},{9,10},{10,9},{13,14},{14,13},{17,18},{18,... | collective-permute-start | bytes 172040 | tf_op jit(solution)/shard_map/ppermute | solution.py:625
  13.1 0.6 %collective-permute-done.2.beside_ref = bf16[224,128]{1,0:T(8,128)(2,1)S(1)} collective-permute-done((bf16[224,128]{1,0:T(8,128)(2,1)S(1)}, bf16[224,128]{1,0:T(8,128)(2,1)S(1)}, u32[]{:S(2)}, u32[]{:S(2)}) %collective-permute-start.2) | collective-permute-done | bytes 57376 | tf_op jit(solution)/shard_map/ppermute | solution.py:625
  13.6 0.0 copy-done.2
  13.6 2.2 %early.1 = (f32[1,128]{1,0:T(1,128)S(1)}, f32[640,256]{1,0:T(8,128)S(1)}, f32[320,128]{1,0:T(8,128)S(1)}) custom-call(bf16[1,160,160]{2,1,0:T(8,128)(2,1)S(1)} %get-tuple-element.11.own_ref, bf16[1,160,160]{2,1,0:T(8,128)(2,1)S(1)} %collective-permute-done.other_ref, bf16[64,384]{1,0:T(8,128)(2,1)S(1)} %collective-permute-done.1.beyond_ref, ...), custom_call_target="tpu_custom_call" | custom-call | flops 2000000000 | bytes 2097152 | tf_op jit(solution)/shard_map/early/pallas_call | solution.py:635
  15.8 0.0 collective-permute-done.3.beside_ref
  15.8 1.5 %late.1 = f32[32,128]{1,0:T(8,128)S(1)} custom-call(f32[1,128]{1,0:T(1,128)S(1)} %get-tuple-element.17.line_ref, f32[640,256]{1,0:T(8,128)S(1)} %get-tuple-element.18.own_spectra_ref, f32[320,128]{1,0:T(8,128)S(1)} %get-tuple-element.19.own_side_ref, bf16[224,128]{1,0:T(8,128)(2,1)S(1)} %collective-permute-done.3.beside_ref, ...), custom_call_target="tpu_custom_call" | custom-call | flops 1000000000 | bytes 2097152 | tf_op jit(solution)/shard_map/late/pallas_call | solution.py:649
  17.3 14.7 %all_to_all.11 = f32[32,1,128]{2,1,0:T(1,128)S(1)} all-to-all(f32[32,1,128]{2,1,0:T(1,128)S(1)} %bitcast.5), channel_id=1, replica_groups=mesh['gz'=2,'gy'=4,'gx'=4] {'gz','gy','gx'}, dimensions={0} | all-to-all | bytes 32768 | tf_op jit(solution)/shard_map/all_to_all | solution.py:659
  32.0 1.1 %relax.1 = (f32[4,1,4,4]{3,2,1,0:T(4,128)}, f32[2,1,4,4]{3,2,1,0:T(4,128)}) custom-call(f32[32,128]{1,0:T(8,128)S(1)} %bitcast.4), custom_call_target="tpu_custom_call" | custom-call | tf_op jit(solution)/shard_map/relax/pallas_call | solution.py:660
Async XLA Ops:
  0.6 5.7 %collective-permute-start = (bf16[1,160,160]{2,1,0:T(8,128)(2,1)}, bf16[1,160,160]{2,1,0:T(8,128)(2,1)S(1)}, u32[]{:S(2)}, u32[]{:S(2)}) collective-permute-start(bf16[1,160,160]{2,1,0:T(8,128)(2,1)} %own_ref.1), channel_id=1, source_target_pairs={{0,16},{16,0},{1,17},{17,1},{2,18},{18,2},{3,19},{19,3},{4,20},{20... | collective-permute-start | bytes 153608 | tf_op jit(solution)/shard_map/ppermute | solution.py:574
  3.7 1.4 %copy-start = (bf16[1600,512]{1,0:T(8,128)(2,1)S(1)}, bf16[1600,512]{1,0:T(8,128)(2,1)}, u32[]{:S(2)}) copy-start(bf16[1600,512]{1,0:T(8,128)(2,1)} %constant.2.clone.table_ref) | copy-start | bytes 4915204
  5.1 0.9 %copy-start.1 = (bf16[1,160,160]{2,1,0:T(8,128)(2,1)S(1)}, bf16[1,160,160]{2,1,0:T(8,128)(2,1)}, u32[]{:S(2)}) copy-start(bf16[1,160,160]{2,1,0:T(8,128)(2,1)} %own_ref.1) | copy-start | bytes 153604
  6.0 7.6 %copy-start.2 = (s32[1,4,4]{2,1,0:T(4,128)S(1)}, s32[1,4,4]{2,1,0:T(4,128)}, u32[]{:S(2)}) copy-start(s32[1,4,4]{2,1,0:T(4,128)} %mask_ref.1) | copy-start | bytes 196
  6.4 5.7 %collective-permute-start.1 = (bf16[64,384]{1,0:T(8,128)(2,1)S(1)}, bf16[64,384]{1,0:T(8,128)(2,1)S(1)}, u32[]{:S(2)}, u32[]{:S(2)}) collective-permute-start(bf16[64,384]{1,0:T(8,128)(2,1)S(1)} %edge.1), channel_id=1, source_target_pairs={{0,4},{20,16},{4,8},{24,20},{8,12},{28,24},{1,5},{21,17},{5,9},{25... | collective-permute-start | bytes 147464 | tf_op jit(solution)/shard_map/ppermute | solution.py:600
  12.3 1.3 %collective-permute-start.2 = (bf16[224,128]{1,0:T(8,128)(2,1)S(1)}, bf16[224,128]{1,0:T(8,128)(2,1)S(1)}, u32[]{:S(2)}, u32[]{:S(2)}) collective-permute-start(bf16[224,128]{1,0:T(8,128)(2,1)S(1)} %get-tuple-element.15.late_side_ref), channel_id=1, source_target_pairs={{0,1},{1,0},{2,3},{3,2},{4,5},{5,4},{6,7},{7,6},{8,9},{9,8},{10,11... | collective-permute-start | bytes 172040 | tf_op jit(solution)/shard_map/ppermute | solution.py:625
  12.4 3.4 %collective-permute-start.3 = (bf16[224,128]{1,0:T(8,128)(2,1)S(1)}, bf16[224,128]{1,0:T(8,128)(2,1)S(1)}, u32[]{:S(2)}, u32[]{:S(2)}) collective-permute-start(bf16[224,128]{1,0:T(8,128)(2,1)S(1)} %get-tuple-element.14.early_side_ref), channel_id=1, source_target_pairs={{1,2},{2,1},{5,6},{6,5},{9,10},{10,9},{13,14},{14,13},{17,18},{18,... | collective-permute-start | bytes 172040 | tf_op jit(solution)/shard_map/ppermute | solution.py:625

commit v9 on v8

--- a/solution.py
+++ b/solution.py
@@ -514,25 +514,21 @@
     side, in_half = parts(in_y, rows)
     tile = jnp.where(inside, tile_y * size_x + tile_x, -1)
     flow_spot = in_half * columns + in_x
-    spots = jnp.concatenate([flow_spot, flow_spot + count, 2 * count + in_y * columns + in_x], 1)
-    picked = lax.broadcasted_iota(jnp.int32, (LANES, 3 * LANES), 0) == spots
-    picker = picked.astype(jnp.float32).astype(jnp.bfloat16)
-    rest = got_ref[...]
-    spread = jnp.zeros((rest.shape[0], 3 * LANES), jnp.float32)
-    for _ in range(3):
-        piece = rest.astype(jnp.bfloat16)
-        rest = rest - piece.astype(jnp.float32)
-        spread = spread + dot(piece, picker)
+    got = got_ref[...]
+    spread = []
+    for spot in (flow_spot, flow_spot + count, 2 * count + in_y * columns + in_x):
+        lanes = jnp.broadcast_to(jnp.where(inside, spot, 0), got.shape)
+        spread.append(jnp.take_along_axis(got, lanes, axis=1, mode="promise_in_bounds"))
     source = lax.broadcasted_iota(jnp.int32, (2 * per_section, LANES), 0)
     chosen = source == side * per_section + tile
     chosen = chosen & (tile >= 0)
     flow_y, flow_x = (
-        jnp.sum(jnp.where(chosen, spread[:, axis * LANES : (axis + 1) * LANES], 0.0), 0, keepdims=True)
+        jnp.sum(jnp.where(chosen, spread[axis], 0.0), 0, keepdims=True)
         for axis in range(2)
     )
     chosen = source[:per_section] == tile
     mask_0, mask_1 = (
-        jnp.sum(jnp.where(chosen, spread[start : start + per_section, 2 * LANES :], 0.0), 0, keepdims=True)
+        jnp.sum(jnp.where(chosen, spread[2][start : start + per_section], 0.0), 0, keepdims=True)
         for start in (0, per_section)
     )
     flows = jnp.concatenate([flow_y, flow_x], 0)

time: 33.4 us -> 33.3 us (level)
  no operation moved by 1% of the time
where the time goes in v9:
time: 33.3 us; the launch traced here: 33.1 us
  blocking collectives  14.7 us (44%)
  starting transfers between devices  7.76 us (23%)
  Pallas kernels  5.41 us (16%)
  local copies, waits for them, and re-layouts  2.32 us (7%)
  waiting for transfers between devices  2.15 us (6%)
  between operations  0.71 us (2%)
    all_to_all x1, blocking collectives, pair_body(): got = lax.all_to_all(lines, ('gz', 'gy', 'gx'), 0, 0, tiled=True)  14.7 us
    ppermute x1, starting transfers between devices, pair_body(): beyond = lax.ppermute(edge, ('gz', 'gy'), onward)  3.99 us
    ppermute x1, starting transfers between devices, pair_body(): other = lax.ppermute(images, 'gz', [(0, 1), (1, 0)])  3.03 us
    unnamed x6, local copies, waits for them, and re-layouts  2.32 us
    pallas_call x1, Pallas kernels, pair_body(): pl.pallas_call(functools.partial(early_kernel, count_x), out_shape=(jax.S...  2.2 us
    ppermute x1, waiting for transfers between devices, pair_body(): beyond = lax.ppermute(edge, ('gz', 'gy'), onward)  1.56 us
    pallas_call x1, Pallas kernels, pair_body(): pl.pallas_call(functools.partial(late_kernel, count_x), out_shape=jax.Sha...  1.47 us
    pallas_call x1, Pallas kernels, pair_body(): pl.pallas_call(functools.partial(relax_kernel, rows, count_x), out_shape=...  1.03 us
  transfers between devices with their start and end apart: 4, of which 2 were waited for; matrix products, arithmetic and copies ran while one was open for 0% of the time, Pallas kernels for 8%

profile of v9, /device:TPU:0, one launch (start us, length us, event | category | flops | bytes accessed | tf_op | source)
XLA Modules:
  0.0 33.1 jit_solution(5901044460736083355)
XLA Ops:
  0.6 3.0 %collective-permute-start = (bf16[1,160,160]{2,1,0:T(8,128)(2,1)}, bf16[1,160,160]{2,1,0:T(8,128)(2,1)S(1)}, u32[]{:S(2)}, u32[]{:S(2)}) collective-permute-start(bf16[1,160,160]{2,1,0:T(8,128)(2,1)} %own_ref.1), channel_id=1, source_target_pairs={{0,16},{16,0},{1,17},{17,1},{2,18},{18,2},{3,19},{19,3},{4,20},{20... | collective-permute-start | bytes 153608 | tf_op jit(solution)/shard_map/ppermute | solution.py:570
  3.7 0.0 copy-start
  3.7 1.4 %copy-done = bf16[1600,512]{1,0:T(8,128)(2,1)S(1)} copy-done((bf16[1600,512]{1,0:T(8,128)(2,1)S(1)}, bf16[1600,512]{1,0:T(8,128)(2,1)}, u32[]{:S(2)}) %copy-start) | copy-done | bytes 1638424
  5.1 0.0 copy-start.1
  5.1 0.9 %copy-done.1 = bf16[1,160,160]{2,1,0:T(8,128)(2,1)S(1)} copy-done((bf16[1,160,160]{2,1,0:T(8,128)(2,1)S(1)}, bf16[1,160,160]{2,1,0:T(8,128)(2,1)}, u32[]{:S(2)}) %copy-start.1) | copy-done | bytes 51224
  6.0 0.0 copy-start.2
  6.0 0.3 load.1
  6.3 0.0 collective-permute-done.other_ref
  6.3 0.1 edge.1
  6.4 4.0 %collective-permute-start.1 = (bf16[64,384]{1,0:T(8,128)(2,1)S(1)}, bf16[64,384]{1,0:T(8,128)(2,1)S(1)}, u32[]{:S(2)}, u32[]{:S(2)}) collective-permute-start(bf16[64,384]{1,0:T(8,128)(2,1)S(1)} %edge.1), channel_id=1, source_target_pairs={{0,4},{20,16},{4,8},{24,20},{8,12},{28,24},{1,5},{21,17},{5,9},{25... | collective-permute-start | bytes 147464 | tf_op jit(solution)/shard_map/ppermute | solution.py:596
  10.4 0.2 pack.1
  10.6 1.6 %collective-permute-done.1.beyond_ref = bf16[64,384]{1,0:T(8,128)(2,1)S(1)} collective-permute-done((bf16[64,384]{1,0:T(8,128)(2,1)S(1)}, bf16[64,384]{1,0:T(8,128)(2,1)S(1)}, u32[]{:S(2)}, u32[]{:S(2)}) %collective-permute-start.1) | collective-permute-done | bytes 49184 | tf_op jit(solution)/shard_map/ppermute | solution.py:596
  12.1 0.2 pack_edge.1
  12.3 0.1 collective-permute-start.2
  12.4 0.7 %collective-permute-start.3 = (bf16[224,128]{1,0:T(8,128)(2,1)S(1)}, bf16[224,128]{1,0:T(8,128)(2,1)S(1)}, u32[]{:S(2)}, u32[]{:S(2)}) collective-permute-start(bf16[224,128]{1,0:T(8,128)(2,1)S(1)} %get-tuple-element.14.early_side_ref), channel_id=1, source_target_pairs={{1,2},{2,1},{5,6},{6,5},{9,10},{10,9},{13,14},{14,13},{17,18},{18,... | collective-permute-start | bytes 172040 | tf_op jit(solution)/shard_map/ppermute | solution.py:621
  13.1 0.6 %collective-permute-done.2.beside_ref = bf16[224,128]{1,0:T(8,128)(2,1)S(1)} collective-permute-done((bf16[224,128]{1,0:T(8,128)(2,1)S(1)}, bf16[224,128]{1,0:T(8,128)(2,1)S(1)}, u32[]{:S(2)}, u32[]{:S(2)}) %collective-permute-start.2) | collective-permute-done | bytes 57376 | tf_op jit(solution)/shard_map/ppermute | solution.py:621
  13.6 0.0 copy-done.2
  13.6 2.2 %early.1 = (f32[1,128]{1,0:T(1,128)S(1)}, f32[640,256]{1,0:T(8,128)S(1)}, f32[320,128]{1,0:T(8,128)S(1)}) custom-call(bf16[1,160,160]{2,1,0:T(8,128)(2,1)S(1)} %get-tuple-element.11.own_ref, bf16[1,160,160]{2,1,0:T(8,128)(2,1)S(1)} %collective-permute-done.other_ref, bf16[64,384]{1,0:T(8,128)(2,1)S(1)} %collective-permute-done.1.beyond_ref, ...), custom_call_target="tpu_custom_call" | custom-call | flops 2000000000 | bytes 2097152 | tf_op jit(solution)/shard_map/early/pallas_call | solution.py:631
  15.8 0.0 collective-permute-done.3.beside_ref
  15.8 1.5 %late.1 = f32[32,128]{1,0:T(8,128)S(1)} custom-call(f32[1,128]{1,0:T(1,128)S(1)} %get-tuple-element.17.line_ref, f32[640,256]{1,0:T(8,128)S(1)} %get-tuple-element.18.own_spectra_ref, f32[320,128]{1,0:T(8,128)S(1)} %get-tuple-element.19.own_side_ref, bf16[224,128]{1,0:T(8,128)(2,1)S(1)} %collective-permute-done.3.beside_ref, ...), custom_call_target="tpu_custom_call" | custom-call | flops 1000000000 | bytes 2097152 | tf_op jit(solution)/shard_map/late/pallas_call | solution.py:645
  17.3 14.7 %all_to_all.11 = f32[32,1,128]{2,1,0:T(1,128)S(1)} all-to-all(f32[32,1,128]{2,1,0:T(1,128)S(1)} %bitcast.5), channel_id=1, replica_groups=mesh['gz'=2,'gy'=4,'gx'=4] {'gz','gy','gx'}, dimensions={0} | all-to-all | bytes 32768 | tf_op jit(solution)/shard_map/all_to_all | solution.py:655
  32.0 1.0 %relax.1 = (f32[4,1,4,4]{3,2,1,0:T(4,128)}, f32[2,1,4,4]{3,2,1,0:T(4,128)}) custom-call(f32[32,128]{1,0:T(8,128)S(1)} %bitcast.4), custom_call_target="tpu_custom_call" | custom-call | tf_op jit(solution)/shard_map/relax/pallas_call | solution.py:656
Async XLA Ops:
  0.6 5.7 %collective-permute-start = (bf16[1,160,160]{2,1,0:T(8,128)(2,1)}, bf16[1,160,160]{2,1,0:T(8,128)(2,1)S(1)}, u32[]{:S(2)}, u32[]{:S(2)}) collective-permute-start(bf16[1,160,160]{2,1,0:T(8,128)(2,1)} %own_ref.1), channel_id=1, source_target_pairs={{0,16},{16,0},{1,17},{17,1},{2,18},{18,2},{3,19},{19,3},{4,20},{20... | collective-permute-start | bytes 153608 | tf_op jit(solution)/shard_map/ppermute | solution.py:570
  3.7 1.4 %copy-start = (bf16[1600,512]{1,0:T(8,128)(2,1)S(1)}, bf16[1600,512]{1,0:T(8,128)(2,1)}, u32[]{:S(2)}) copy-start(bf16[1600,512]{1,0:T(8,128)(2,1)} %constant.2.clone.table_ref) | copy-start | bytes 4915204
  5.1 0.9 %copy-start.1 = (bf16[1,160,160]{2,1,0:T(8,128)(2,1)S(1)}, bf16[1,160,160]{2,1,0:T(8,128)(2,1)}, u32[]{:S(2)}) copy-start(bf16[1,160,160]{2,1,0:T(8,128)(2,1)} %own_ref.1) | copy-start | bytes 153604
  6.0 7.6 %copy-start.2 = (s32[1,4,4]{2,1,0:T(4,128)S(1)}, s32[1,4,4]{2,1,0:T(4,128)}, u32[]{:S(2)}) copy-start(s32[1,4,4]{2,1,0:T(4,128)} %mask_ref.1) | copy-start | bytes 196
  6.4 5.7 %collective-permute-start.1 = (bf16[64,384]{1,0:T(8,128)(2,1)S(1)}, bf16[64,384]{1,0:T(8,128)(2,1)S(1)}, u32[]{:S(2)}, u32[]{:S(2)}) collective-permute-start(bf16[64,384]{1,0:T(8,128)(2,1)S(1)} %edge.1), channel_id=1, source_target_pairs={{0,4},{20,16},{4,8},{24,20},{8,12},{28,24},{1,5},{21,17},{5,9},{25... | collective-permute-start | bytes 147464 | tf_op jit(solution)/shard_map/ppermute | solution.py:596
  12.3 1.3 %collective-permute-start.2 = (bf16[224,128]{1,0:T(8,128)(2,1)S(1)}, bf16[224,128]{1,0:T(8,128)(2,1)S(1)}, u32[]{:S(2)}, u32[]{:S(2)}) collective-permute-start(bf16[224,128]{1,0:T(8,128)(2,1)S(1)} %get-tuple-element.15.late_side_ref), channel_id=1, source_target_pairs={{0,1},{1,0},{2,3},{3,2},{4,5},{5,4},{6,7},{7,6},{8,9},{9,8},{10,11... | collective-permute-start | bytes 172040 | tf_op jit(solution)/shard_map/ppermute | solution.py:621
  12.4 3.4 %collective-permute-start.3 = (bf16[224,128]{1,0:T(8,128)(2,1)S(1)}, bf16[224,128]{1,0:T(8,128)(2,1)S(1)}, u32[]{:S(2)}, u32[]{:S(2)}) collective-permute-start(bf16[224,128]{1,0:T(8,128)(2,1)S(1)} %get-tuple-element.14.early_side_ref), channel_id=1, source_target_pairs={{1,2},{2,1},{5,6},{6,5},{9,10},{10,9},{13,14},{14,13},{17,18},{18,... | collective-permute-start | bytes 172040 | tf_op jit(solution)/shard_map/ppermute | solution.py:621

commit v10 on v9

--- a/solution.py
+++ b/solution.py
@@ -411,11 +411,13 @@
         high_ref[patch * PATCH : (patch + 1) * PATCH] = high
         low_ref[patch * PATCH : (patch + 1) * PATCH] = low
     for patch in range(count):
-        if patch % 2 == 0:
-            block = slice(patch * PATCH, (patch + 2) * PATCH)
+        if patch in (0, 3):
+            first = patch
+            ahead = [start for start in (0, 3) if start > patch] + [count]
+            block = slice(first * PATCH, ahead[0] * PATCH)
             correl = dot(high_ref[block], right[0]) + dot(high_ref[block], right[1])
             correl = correl + dot(low_ref[block], right[0])
-        squared = correl[patch % 2 * PATCH : (patch % 2 + 1) * PATCH]
+        squared = correl[(patch - first) * PATCH : (patch - first + 1) * PATCH]
         squared = squared * squared
         weights = squared * squared
         pieces = [weights[at : at + SUBLANES] for at in range(0, PATCH, SUBLANES)]

time: 33.3 us -> 33.2 us (level)
  no operation moved by 1% of the time
where the time goes in v10:
time: 33.2 us; the launch traced here: 33 us
  blocking collectives  14.7 us (44%)
  starting transfers between devices  7.76 us (23%)
  Pallas kernels  5.35 us (16%)
  local copies, waits for them, and re-layouts  2.32 us (7%)
  waiting for transfers between devices  2.15 us (6%)
  between operations  0.71 us (2%)
    all_to_all x1, blocking collectives, pair_body(): got = lax.all_to_all(lines, ('gz', 'gy', 'gx'), 0, 0, tiled=True)  14.7 us
    ppermute x1, starting transfers between devices, pair_body(): beyond = lax.ppermute(edge, ('gz', 'gy'), onward)  3.99 us
    ppermute x1, starting transfers between devices, pair_body(): other = lax.ppermute(images, 'gz', [(0, 1), (1, 0)])  3.03 us
    unnamed x6, local copies, waits for them, and re-layouts  2.32 us
    pallas_call x1, Pallas kernels, pair_body(): pl.pallas_call(functools.partial(early_kernel, count_x), out_shape=(jax.S...  2.18 us
    ppermute x1, waiting for transfers between devices, pair_body(): beyond = lax.ppermute(edge, ('gz', 'gy'), onward)  1.56 us
    pallas_call x1, Pallas kernels, pair_body(): pl.pallas_call(functools.partial(late_kernel, count_x), out_shape=jax.Sha...  1.43 us
    pallas_call x1, Pallas kernels, pair_body(): pl.pallas_call(functools.partial(relax_kernel, rows, count_x), out_shape=...  1.03 us
  transfers between devices with their start and end apart: 4, of which 2 were waited for; matrix products, arithmetic and copies ran while one was open for 0% of the time, Pallas kernels for 8%

profile of v10, /device:TPU:0, one launch (start us, length us, event | category | flops | bytes accessed | tf_op | source)
XLA Modules:
  0.0 33.0 jit_solution(17235168091069233500)
XLA Ops:
  0.6 3.0 %collective-permute-start = (bf16[1,160,160]{2,1,0:T(8,128)(2,1)}, bf16[1,160,160]{2,1,0:T(8,128)(2,1)S(1)}, u32[]{:S(2)}, u32[]{:S(2)}) collective-permute-start(bf16[1,160,160]{2,1,0:T(8,128)(2,1)} %own_ref.1), channel_id=1, source_target_pairs={{0,16},{16,0},{1,17},{17,1},{2,18},{18,2},{3,19},{19,3},{4,20},{20... | collective-permute-start | bytes 153608 | tf_op jit(solution)/shard_map/ppermute | solution.py:572
  3.7 0.0 copy-start
  3.7 1.4 %copy-done = bf16[1600,512]{1,0:T(8,128)(2,1)S(1)} copy-done((bf16[1600,512]{1,0:T(8,128)(2,1)S(1)}, bf16[1600,512]{1,0:T(8,128)(2,1)}, u32[]{:S(2)}) %copy-start) | copy-done | bytes 1638424
  5.1 0.0 copy-start.1
  5.1 0.9 %copy-done.1 = bf16[1,160,160]{2,1,0:T(8,128)(2,1)S(1)} copy-done((bf16[1,160,160]{2,1,0:T(8,128)(2,1)S(1)}, bf16[1,160,160]{2,1,0:T(8,128)(2,1)}, u32[]{:S(2)}) %copy-start.1) | copy-done | bytes 51224
  6.0 0.0 copy-start.2
  6.0 0.3 load.1
  6.3 0.0 collective-permute-done.other_ref
  6.3 0.1 edge.1
  6.4 4.0 %collective-permute-start.1 = (bf16[64,384]{1,0:T(8,128)(2,1)S(1)}, bf16[64,384]{1,0:T(8,128)(2,1)S(1)}, u32[]{:S(2)}, u32[]{:S(2)}) collective-permute-start(bf16[64,384]{1,0:T(8,128)(2,1)S(1)} %edge.1), channel_id=1, source_target_pairs={{0,4},{20,16},{4,8},{24,20},{8,12},{28,24},{1,5},{21,17},{5,9},{25... | collective-permute-start | bytes 147464 | tf_op jit(solution)/shard_map/ppermute | solution.py:598
  10.4 0.2 pack.1
  10.6 1.6 %collective-permute-done.1.beyond_ref = bf16[64,384]{1,0:T(8,128)(2,1)S(1)} collective-permute-done((bf16[64,384]{1,0:T(8,128)(2,1)S(1)}, bf16[64,384]{1,0:T(8,128)(2,1)S(1)}, u32[]{:S(2)}, u32[]{:S(2)}) %collective-permute-start.1) | collective-permute-done | bytes 49184 | tf_op jit(solution)/shard_map/ppermute | solution.py:598
  12.1 0.2 pack_edge.1
  12.3 0.1 collective-permute-start.2
  12.4 0.7 %collective-permute-start.3 = (bf16[224,128]{1,0:T(8,128)(2,1)S(1)}, bf16[224,128]{1,0:T(8,128)(2,1)S(1)}, u32[]{:S(2)}, u32[]{:S(2)}) collective-permute-start(bf16[224,128]{1,0:T(8,128)(2,1)S(1)} %get-tuple-element.14.early_side_ref), channel_id=1, source_target_pairs={{1,2},{2,1},{5,6},{6,5},{9,10},{10,9},{13,14},{14,13},{17,18},{18,... | collective-permute-start | bytes 172040 | tf_op jit(solution)/shard_map/ppermute | solution.py:623
  13.1 0.6 %collective-permute-done.2.beside_ref = bf16[224,128]{1,0:T(8,128)(2,1)S(1)} collective-permute-done((bf16[224,128]{1,0:T(8,128)(2,1)S(1)}, bf16[224,128]{1,0:T(8,128)(2,1)S(1)}, u32[]{:S(2)}, u32[]{:S(2)}) %collective-permute-start.2) | collective-permute-done | bytes 57376 | tf_op jit(solution)/shard_map/ppermute | solution.py:623
  13.6 0.0 copy-done.2
  13.6 2.2 %early.1 = (f32[1,128]{1,0:T(1,128)S(1)}, f32[640,256]{1,0:T(8,128)S(1)}, f32[320,128]{1,0:T(8,128)S(1)}) custom-call(bf16[1,160,160]{2,1,0:T(8,128)(2,1)S(1)} %get-tuple-element.11.own_ref, bf16[1,160,160]{2,1,0:T(8,128)(2,1)S(1)} %collective-permute-done.other_ref, bf16[64,384]{1,0:T(8,128)(2,1)S(1)} %collective-permute-done.1.beyond_ref, ...), custom_call_target="tpu_custom_call" | custom-call | flops 2000000000 | bytes 2097152 | tf_op jit(solution)/shard_map/early/pallas_call | solution.py:633
  15.8 0.0 collective-permute-done.3.beside_ref
  15.8 1.4 %late.1 = f32[32,128]{1,0:T(8,128)S(1)} custom-call(f32[1,128]{1,0:T(1,128)S(1)} %get-tuple-element.17.line_ref, f32[640,256]{1,0:T(8,128)S(1)} %get-tuple-element.18.own_spectra_ref, f32[320,128]{1,0:T(8,128)S(1)} %get-tuple-element.19.own_side_ref, bf16[224,128]{1,0:T(8,128)(2,1)S(1)} %collective-permute-done.3.beside_ref, ...), custom_call_target="tpu_custom_call" | custom-call | flops 1000000000 | bytes 2097152 | tf_op jit(solution)/shard_map/late/pallas_call | solution.py:647
  17.3 14.7 %all_to_all.11 = f32[32,1,128]{2,1,0:T(1,128)S(1)} all-to-all(f32[32,1,128]{2,1,0:T(1,128)S(1)} %bitcast.5), channel_id=1, replica_groups=mesh['gz'=2,'gy'=4,'gx'=4] {'gz','gy','gx'}, dimensions={0} | all-to-all | bytes 32768 | tf_op jit(solution)/shard_map/all_to_all | solution.py:657
  32.0 1.0 %relax.1 = (f32[4,1,4,4]{3,2,1,0:T(4,128)}, f32[2,1,4,4]{3,2,1,0:T(4,128)}) custom-call(f32[32,128]{1,0:T(8,128)S(1)} %bitcast.4), custom_call_target="tpu_custom_call" | custom-call | tf_op jit(solution)/shard_map/relax/pallas_call | solution.py:658
Async XLA Ops:
  0.6 5.7 %collective-permute-start = (bf16[1,160,160]{2,1,0:T(8,128)(2,1)}, bf16[1,160,160]{2,1,0:T(8,128)(2,1)S(1)}, u32[]{:S(2)}, u32[]{:S(2)}) collective-permute-start(bf16[1,160,160]{2,1,0:T(8,128)(2,1)} %own_ref.1), channel_id=1, source_target_pairs={{0,16},{16,0},{1,17},{17,1},{2,18},{18,2},{3,19},{19,3},{4,20},{20... | collective-permute-start | bytes 153608 | tf_op jit(solution)/shard_map/ppermute | solution.py:572
  3.7 1.4 %copy-start = (bf16[1600,512]{1,0:T(8,128)(2,1)S(1)}, bf16[1600,512]{1,0:T(8,128)(2,1)}, u32[]{:S(2)}) copy-start(bf16[1600,512]{1,0:T(8,128)(2,1)} %constant.2.clone.table_ref) | copy-start | bytes 4915204
  5.1 0.9 %copy-start.1 = (bf16[1,160,160]{2,1,0:T(8,128)(2,1)S(1)}, bf16[1,160,160]{2,1,0:T(8,128)(2,1)}, u32[]{:S(2)}) copy-start(bf16[1,160,160]{2,1,0:T(8,128)(2,1)} %own_ref.1) | copy-start | bytes 153604
  6.0 7.6 %copy-start.2 = (s32[1,4,4]{2,1,0:T(4,128)S(1)}, s32[1,4,4]{2,1,0:T(4,128)}, u32[]{:S(2)}) copy-start(s32[1,4,4]{2,1,0:T(4,128)} %mask_ref.1) | copy-start | bytes 196
  6.4 5.7 %collective-permute-start.1 = (bf16[64,384]{1,0:T(8,128)(2,1)S(1)}, bf16[64,384]{1,0:T(8,128)(2,1)S(1)}, u32[]{:S(2)}, u32[]{:S(2)}) collective-permute-start(bf16[64,384]{1,0:T(8,128)(2,1)S(1)} %edge.1), channel_id=1, source_target_pairs={{0,4},{20,16},{4,8},{24,20},{8,12},{28,24},{1,5},{21,17},{5,9},{25... | collective-permute-start | bytes 147464 | tf_op jit(solution)/shard_map/ppermute | solution.py:598
  12.3 1.3 %collective-permute-start.2 = (bf16[224,128]{1,0:T(8,128)(2,1)S(1)}, bf16[224,128]{1,0:T(8,128)(2,1)S(1)}, u32[]{:S(2)}, u32[]{:S(2)}) collective-permute-start(bf16[224,128]{1,0:T(8,128)(2,1)S(1)} %get-tuple-element.15.late_side_ref), channel_id=1, source_target_pairs={{0,1},{1,0},{2,3},{3,2},{4,5},{5,4},{6,7},{7,6},{8,9},{9,8},{10,11... | collective-permute-start | bytes 172040 | tf_op jit(solution)/shard_map/ppermute | solution.py:623
  12.4 3.4 %collective-permute-start.3 = (bf16[224,128]{1,0:T(8,128)(2,1)S(1)}, bf16[224,128]{1,0:T(8,128)(2,1)S(1)}, u32[]{:S(2)}, u32[]{:S(2)}) collective-permute-start(bf16[224,128]{1,0:T(8,128)(2,1)S(1)} %get-tuple-element.14.early_side_ref), channel_id=1, source_target_pairs={{1,2},{2,1},{5,6},{6,5},{9,10},{10,9},{13,14},{14,13},{17,18},{18,... | collective-permute-start | bytes 172040 | tf_op jit(solution)/shard_map/ppermute | solution.py:623

commit v11 on v10

--- a/solution.py
+++ b/solution.py
@@ -359,8 +359,9 @@
     return [jnp.where(odd, *pair).astype(jnp.bfloat16) for pair in ((low, high), (high, low))]
 
 
-def pack_kernel(own_ref, other_ref, first_ref, second_ref):
+def pack_kernel(rows, columns, own_ref, other_ref, first_ref, second_ref, *plan_refs):
     first_ref[:PATCH], second_ref[:PATCH] = side_columns([own_ref[0], other_ref[0]])
+    plan_nodes(rows, columns, *plan_refs)
 
 
 def pack_edge_kernel(beyond_ref, first_in, second_in, first_ref, second_ref):
@@ -491,9 +492,9 @@
     out_ref[...] = jnp.broadcast_to(line_ref[...] + line, out_ref.shape)
 
 
-def relax_kernel(rows, columns, got_ref, flow_ref, offsets_ref):
+def plan_nodes(rows, columns, spots_ref, chosen_ref, masks_ref):
     size_y, size_x = lax.axis_size("gy"), lax.axis_size("gx")
-    half, at_y, at_x = lax.axis_index("gz"), lax.axis_index("gy"), lax.axis_index("gx")
+    at_y, at_x = lax.axis_index("gy"), lax.axis_index("gx")
     count = rows * columns
     tile_rows = 2 * rows
     width = columns + 2 * RADIUS
@@ -514,28 +515,40 @@
     tile_y, in_y = parts(node_y, tile_rows)
     tile_x, in_x = parts(node_x, columns)
     side, in_half = parts(in_y, rows)
-    tile = jnp.where(inside, tile_y * size_x + tile_x, -1)
+    tile = tile_y * size_x + tile_x
     flow_spot = in_half * columns + in_x
+    spots = [flow_spot, flow_spot + count, 2 * count + in_y * columns + in_x]
+    spots_ref[...] = jnp.concatenate([jnp.where(inside, spot, 0) for spot in spots], 0)
+    source = lax.broadcasted_iota(jnp.int32, (2 * per_section, LANES), 0)
+    flow_source = (source == side * per_section + tile) & inside
+    mask_source = ((source == tile) | (source == per_section + tile)) & inside
+    chosen_ref[...] = jnp.concatenate(
+        [flow_source.astype(jnp.float32), mask_source.astype(jnp.float32)], 1
+    )
+    not_first = (across > 0.5).astype(jnp.float32)
+    not_last = (across < width - 1.5).astype(jnp.float32)
+    masks_ref[...] = jnp.concatenate([inside.astype(jnp.float32), not_first, not_last], 0)
+
+
+def relax_kernel(rows, columns, got_ref, spots_ref, chosen_ref, masks_ref, flow_ref, offsets_ref):
+    half = lax.axis_index("gz")
+    tile_rows = 2 * rows
+    width = columns + 2 * RADIUS
+    devices = got_ref.shape[0]
     got = got_ref[...]
-    spread = []
-    for spot in (flow_spot, flow_spot + count, 2 * count + in_y * columns + in_x):
-        lanes = jnp.broadcast_to(jnp.where(inside, spot, 0), got.shape)
-        spread.append(jnp.take_along_axis(got, lanes, axis=1, mode="promise_in_bounds"))
-    source = lax.broadcasted_iota(jnp.int32, (2 * per_section, LANES), 0)
-    chosen = source == side * per_section + tile
-    chosen = chosen & (tile >= 0)
-    flow_y, flow_x = (
-        jnp.sum(jnp.where(chosen, spread[axis], 0.0), 0, keepdims=True)
-        for axis in range(2)
-    )
-    chosen = source[:per_section] == tile
-    mask_0, mask_1 = (
-        jnp.sum(jnp.where(chosen, spread[2][start : start + per_section], 0.0), 0, keepdims=True)
-        for start in (0, per_section)
-    )
+    spread = [
+        jnp.take_along_axis(
+            got, jnp.broadcast_to(spots_ref[at : at + 1], got.shape), axis=1, mode="promise_in_bounds"
+        )
+        for at in range(3)
+    ]
+    from_one, from_both = chosen_ref[:, :LANES], chosen_ref[:, LANES:]
+    flow_y, flow_x = (jnp.sum(spread[axis] * from_one, 0, keepdims=True) for axis in range(2))
+    masks = spread[2] * from_both
+    middle = devices // 2
+    weight = jnp.sum(masks[:middle], 0, keepdims=True) * jnp.sum(masks[middle:], 0, keepdims=True)
     flows = jnp.concatenate([flow_y, flow_x], 0)
-    weight = mask_0 * mask_1
-    kept = inside.astype(jnp.float32)
+    kept, not_first, not_last = (masks_ref[at : at + 1] for at in range(3))
     sign = jnp.where(lax.broadcasted_iota(jnp.int32, (4, LANES), 0) < 2, 1.0, -1.0)
     weight = weight * sign
     offsets = jnp.zeros((4, LANES), jnp.float32)
@@ -544,20 +557,20 @@
         pull = upper - lower - flows
         forces = weight * jnp.concatenate([pull, pull], 0)
         if step:
-            left = jnp.where(across < 0.5, 0.0, pltpu.roll(offsets, 1, 1))
-            right = jnp.where(across > width - 1.5, 0.0, pltpu.roll(offsets, LANES - 1, 1))
+            left = pltpu.roll(offsets, 1, 1) * not_first
+            right = pltpu.roll(offsets, LANES - 1, 1) * not_last
             laplace = pltpu.roll(offsets, width, 1) + pltpu.roll(offsets, LANES - width, 1)
             forces = STIFFNESS * (laplace + left + right - 4.0 * offsets) + forces
         offsets = (offsets + STEP_SIZE * forces) * kept
     first = half == 0
     result = jnp.where(first, offsets[:2], offsets[2:])
-    flows = jnp.where(first, flows, 0.0)
+    result = jnp.concatenate([result, jnp.where(first, flows, 0.0)], 0)
+    flow_ref[2:] = jnp.zeros((flow_ref.shape[0] - 2, *flow_ref.shape[1:]), jnp.float32)
     for row in range(tile_rows):
         start = (RADIUS + row) * width + RADIUS
-        for axis in range(2):
-            offsets_ref[axis, 0, pl.ds(row, 1)] = result[axis : axis + 1, start : start + columns]
-            flow_ref[axis, 0, pl.ds(row, 1)] = flows[axis : axis + 1, start : start + columns]
-    flow_ref[2:] = jnp.zeros((flow_ref.shape[0] - 2, *flow_ref.shape[1:]), jnp.float32)
+        part = result[:, start : start + columns]
+        offsets_ref[:, 0, row, :] = part[:2]
+        flow_ref[:2, 0, row, :] = part[2:]
 
 
 def vmem(count):
@@ -602,11 +615,18 @@
     ]
     packed = jax.ShapeDtypeStruct((HELD, LANES), jnp.bfloat16)
     small = pltpu.CompilerParams(vmem_limit_bytes=4 * 2**20)
-    sends = pl.pallas_call(
-        pack_kernel,
-        out_shape=(packed, packed),
+    devices = sections * size_y * size_x
+    *sends, spots, chosen, masks = pl.pallas_call(
+        functools.partial(pack_kernel, rows, count_x),
+        out_shape=(
+            packed,
+            packed,
+            jax.ShapeDtypeStruct((3, LANES), jnp.int32),
+            jax.ShapeDtypeStruct((devices, 2 * LANES), jnp.float32),
+            jax.ShapeDtypeStruct((3, LANES), jnp.float32),
+        ),
         in_specs=vmem(2),
-        out_specs=tuple(vmem(2)),
+        out_specs=tuple(vmem(5)),
         compiler_params=small,
         cost_estimate=pl.CostEstimate(flops=10**6, bytes_accessed=2**18, transcendentals=0),
         name="pack",
@@ -621,7 +641,6 @@
         name="pack_edge",
     )(beyond, *sends)
     first, second = (lax.ppermute(send, "gx", swap) for send, swap in zip(sends, swaps))
-    devices = sections * size_y * size_x
 
     patches = rows * count_x // 2
     common = [
@@ -661,11 +680,11 @@
             jax.ShapeDtypeStruct((4, 1, count_y, count_x), jnp.float32),
             jax.ShapeDtypeStruct((2, 1, count_y, count_x), jnp.float32),
         ),
-        in_specs=vmem(1),
+        in_specs=vmem(4),
         out_specs=tuple(vmem(2)),
-        compiler_params=pltpu.CompilerParams(vmem_limit_bytes=4 * 2**20),
+        compiler_params=small,
         name="relax",
-    )(got)
+    )(got, spots, chosen, masks)
 
 
 def body(images, tissue_mask):

time: 33.2 us -> 33.2 us (level)
  no operation moved by 1% of the time
where the time goes in v11:
time: 33.2 us; the launch traced here: 33 us
  blocking collectives  14.7 us (44%)
  starting transfers between devices  7.76 us (23%)
  Pallas kernels  5.35 us (16%)
  local copies, waits for them, and re-layouts  2.32 us (7%)
  waiting for transfers between devices  2.15 us (6%)
  between operations  0.71 us (2%)
    all_to_all x1, blocking collectives, pair_body(): got = lax.all_to_all(lines, ('gz', 'gy', 'gx'), 0, 0, tiled=True)  14.7 us
    ppermute x1, starting transfers between devices, pair_body(): beyond = lax.ppermute(edge, ('gz', 'gy'), onward)  3.99 us
    ppermute x1, starting transfers between devices, pair_body(): other = lax.ppermute(images, 'gz', [(0, 1), (1, 0)])  3.03 us
    unnamed x6, local copies, waits for them, and re-layouts  2.32 us
    pallas_call x1, Pallas kernels, pair_body(): pl.pallas_call(functools.partial(early_kernel, count_x), out_shape=(jax.S...  2.18 us
    ppermute x1, waiting for transfers between devices, pair_body(): beyond = lax.ppermute(edge, ('gz', 'gy'), onward)  1.56 us
    pallas_call x1, Pallas kernels, pair_body(): pl.pallas_call(functools.partial(late_kernel, count_x), out_shape=jax.Sha...  1.43 us
    pallas_call x1, Pallas kernels, pair_body(): pl.pallas_call(functools.partial(relax_kernel, rows, count_x), out_shape=...  1.02 us
  transfers between devices with their start and end apart: 4, of which 2 were waited for; matrix products, arithmetic and copies ran while one was open for 0% of the time, Pallas kernels for 8%

profile of v11, /device:TPU:0, one launch (start us, length us, event | category | flops | bytes accessed | tf_op | source)
XLA Modules:
  0.0 33.0 jit_solution(14112765434092218679)
XLA Ops:
  0.6 3.0 %collective-permute-start = (bf16[1,160,160]{2,1,0:T(8,128)(2,1)}, bf16[1,160,160]{2,1,0:T(8,128)(2,1)S(1)}, u32[]{:S(2)}, u32[]{:S(2)}) collective-permute-start(bf16[1,160,160]{2,1,0:T(8,128)(2,1)} %own_ref.1), channel_id=1, source_target_pairs={{0,16},{16,0},{1,17},{17,1},{2,18},{18,2},{3,19},{19,3},{4,20},{20... | collective-permute-start | bytes 153608 | tf_op jit(solution)/shard_map/ppermute | solution.py:585
  3.7 0.0 copy-start
  3.7 1.4 %copy-done = bf16[1600,512]{1,0:T(8,128)(2,1)S(1)} copy-done((bf16[1600,512]{1,0:T(8,128)(2,1)S(1)}, bf16[1600,512]{1,0:T(8,128)(2,1)}, u32[]{:S(2)}) %copy-start) | copy-done | bytes 1638424
  5.1 0.0 copy-start.1
  5.1 0.9 %copy-done.1 = bf16[1,160,160]{2,1,0:T(8,128)(2,1)S(1)} copy-done((bf16[1,160,160]{2,1,0:T(8,128)(2,1)S(1)}, bf16[1,160,160]{2,1,0:T(8,128)(2,1)}, u32[]{:S(2)}) %copy-start.1) | copy-done | bytes 51224
  6.0 0.0 copy-start.2
  6.0 0.3 load.1
  6.3 0.0 collective-permute-done.other_ref
  6.3 0.1 edge.1
  6.4 4.0 %collective-permute-start.1 = (bf16[64,384]{1,0:T(8,128)(2,1)S(1)}, bf16[64,384]{1,0:T(8,128)(2,1)S(1)}, u32[]{:S(2)}, u32[]{:S(2)}) collective-permute-start(bf16[64,384]{1,0:T(8,128)(2,1)S(1)} %edge.1), channel_id=1, source_target_pairs={{0,4},{20,16},{4,8},{24,20},{8,12},{28,24},{1,5},{21,17},{5,9},{25... | collective-permute-start | bytes 147464 | tf_op jit(solution)/shard_map/ppermute | solution.py:611
  10.4 0.2 pack.1
  10.6 1.6 %collective-permute-done.1.beyond_ref = bf16[64,384]{1,0:T(8,128)(2,1)S(1)} collective-permute-done((bf16[64,384]{1,0:T(8,128)(2,1)S(1)}, bf16[64,384]{1,0:T(8,128)(2,1)S(1)}, u32[]{:S(2)}, u32[]{:S(2)}) %collective-permute-start.1) | collective-permute-done | bytes 49184 | tf_op jit(solution)/shard_map/ppermute | solution.py:611
  12.1 0.2 pack_edge.1
  12.3 0.1 collective-permute-start.2
  12.4 0.7 %collective-permute-start.3 = (bf16[224,128]{1,0:T(8,128)(2,1)S(1)}, bf16[224,128]{1,0:T(8,128)(2,1)S(1)}, u32[]{:S(2)}, u32[]{:S(2)}) collective-permute-start(bf16[224,128]{1,0:T(8,128)(2,1)S(1)} %get-tuple-element.17.early_side_ref), channel_id=1, source_target_pairs={{1,2},{2,1},{5,6},{6,5},{9,10},{10,9},{13,14},{14,13},{17,18},{18,... | collective-permute-start | bytes 172040 | tf_op jit(solution)/shard_map/ppermute | solution.py:643
  13.1 0.6 %collective-permute-done.2.beside_ref = bf16[224,128]{1,0:T(8,128)(2,1)S(1)} collective-permute-done((bf16[224,128]{1,0:T(8,128)(2,1)S(1)}, bf16[224,128]{1,0:T(8,128)(2,1)S(1)}, u32[]{:S(2)}, u32[]{:S(2)}) %collective-permute-start.2) | collective-permute-done | bytes 57376 | tf_op jit(solution)/shard_map/ppermute | solution.py:643
  13.6 0.0 copy-done.2
  13.6 2.2 %early.1 = (f32[1,128]{1,0:T(1,128)S(1)}, f32[640,256]{1,0:T(8,128)S(1)}, f32[320,128]{1,0:T(8,128)S(1)}) custom-call(bf16[1,160,160]{2,1,0:T(8,128)(2,1)S(1)} %get-tuple-element.14.own_ref, bf16[1,160,160]{2,1,0:T(8,128)(2,1)S(1)} %collective-permute-done.other_ref, bf16[64,384]{1,0:T(8,128)(2,1)S(1)} %collective-permute-done.1.beyond_ref, ...), custom_call_target="tpu_custom_call" | custom-call | flops 2000000000 | bytes 2097152 | tf_op jit(solution)/shard_map/early/pallas_call | solution.py:652
  15.8 0.0 collective-permute-done.3.beside_ref
  15.8 1.4 %late.1 = f32[32,128]{1,0:T(8,128)S(1)} custom-call(f32[1,128]{1,0:T(1,128)S(1)} %get-tuple-element.20.line_ref, f32[640,256]{1,0:T(8,128)S(1)} %get-tuple-element.21.own_spectra_ref, f32[320,128]{1,0:T(8,128)S(1)} %get-tuple-element.22.own_side_ref, bf16[224,128]{1,0:T(8,128)(2,1)S(1)} %collective-permute-done.3.beside_ref, ...), custom_call_target="tpu_custom_call" | custom-call | flops 1000000000 | bytes 2097152 | tf_op jit(solution)/shard_map/late/pallas_call | solution.py:666
  17.3 14.7 %all_to_all.11 = f32[32,1,128]{2,1,0:T(1,128)S(1)} all-to-all(f32[32,1,128]{2,1,0:T(1,128)S(1)} %bitcast.5), channel_id=1, replica_groups=mesh['gz'=2,'gy'=4,'gx'=4] {'gz','gy','gx'}, dimensions={0} | all-to-all | bytes 32768 | tf_op jit(solution)/shard_map/all_to_all | solution.py:676
  32.0 1.0 %relax.1 = (f32[4,1,4,4]{3,2,1,0:T(4,128)}, f32[2,1,4,4]{3,2,1,0:T(4,128)}) custom-call(f32[32,128]{1,0:T(8,128)S(1)} %bitcast.4, s32[3,128]{1,0:T(4,128)S(1)} %get-tuple-element.23.spots_ref, f32[32,256]{1,0:T(8,128)S(1)} %get-tuple-element.24.chosen_ref, f32[3,128]{1,0:T(4,128)S(1)} %get-tuple-element.25.masks_ref), custom_call_target="tpu_custom_call" | custom-call | tf_op jit(solution)/shard_map/relax/pallas_call | solution.py:677
Async XLA Ops:
  0.6 5.7 %collective-permute-start = (bf16[1,160,160]{2,1,0:T(8,128)(2,1)}, bf16[1,160,160]{2,1,0:T(8,128)(2,1)S(1)}, u32[]{:S(2)}, u32[]{:S(2)}) collective-permute-start(bf16[1,160,160]{2,1,0:T(8,128)(2,1)} %own_ref.1), channel_id=1, source_target_pairs={{0,16},{16,0},{1,17},{17,1},{2,18},{18,2},{3,19},{19,3},{4,20},{20... | collective-permute-start | bytes 153608 | tf_op jit(solution)/shard_map/ppermute | solution.py:585
  3.7 1.4 %copy-start = (bf16[1600,512]{1,0:T(8,128)(2,1)S(1)}, bf16[1600,512]{1,0:T(8,128)(2,1)}, u32[]{:S(2)}) copy-start(bf16[1600,512]{1,0:T(8,128)(2,1)} %constant.2.clone.table_ref) | copy-start | bytes 4915204
  5.1 0.9 %copy-start.1 = (bf16[1,160,160]{2,1,0:T(8,128)(2,1)S(1)}, bf16[1,160,160]{2,1,0:T(8,128)(2,1)}, u32[]{:S(2)}) copy-start(bf16[1,160,160]{2,1,0:T(8,128)(2,1)} %own_ref.1) | copy-start | bytes 153604
  6.0 7.6 %copy-start.2 = (s32[1,4,4]{2,1,0:T(4,128)S(1)}, s32[1,4,4]{2,1,0:T(4,128)}, u32[]{:S(2)}) copy-start(s32[1,4,4]{2,1,0:T(4,128)} %mask_ref.1) | copy-start | bytes 196
  6.4 5.7 %collective-permute-start.1 = (bf16[64,384]{1,0:T(8,128)(2,1)S(1)}, bf16[64,384]{1,0:T(8,128)(2,1)S(1)}, u32[]{:S(2)}, u32[]{:S(2)}) collective-permute-start(bf16[64,384]{1,0:T(8,128)(2,1)S(1)} %edge.1), channel_id=1, source_target_pairs={{0,4},{20,16},{4,8},{24,20},{8,12},{28,24},{1,5},{21,17},{5,9},{25... | collective-permute-start | bytes 147464 | tf_op jit(solution)/shard_map/ppermute | solution.py:611
  12.3 1.3 %collective-permute-start.2 = (bf16[224,128]{1,0:T(8,128)(2,1)S(1)}, bf16[224,128]{1,0:T(8,128)(2,1)S(1)}, u32[]{:S(2)}, u32[]{:S(2)}) collective-permute-start(bf16[224,128]{1,0:T(8,128)(2,1)S(1)} %get-tuple-element.18.late_side_ref), channel_id=1, source_target_pairs={{0,1},{1,0},{2,3},{3,2},{4,5},{5,4},{6,7},{7,6},{8,9},{9,8},{10,11... | collective-permute-start | bytes 172040 | tf_op jit(solution)/shard_map/ppermute | solution.py:643
  12.4 3.4 %collective-permute-start.3 = (bf16[224,128]{1,0:T(8,128)(2,1)S(1)}, bf16[224,128]{1,0:T(8,128)(2,1)S(1)}, u32[]{:S(2)}, u32[]{:S(2)}) collective-permute-start(bf16[224,128]{1,0:T(8,128)(2,1)S(1)} %get-tuple-element.17.early_side_ref), channel_id=1, source_target_pairs={{1,2},{2,1},{5,6},{6,5},{9,10},{10,9},{13,14},{14,13},{17,18},{18,... | collective-permute-start | bytes 172040 | tf_op jit(solution)/shard_map/ppermute | solution.py:643

commit v12 on v10

--- a/solution.py
+++ b/solution.py
@@ -322,12 +322,14 @@
 
 def edge_kernel(own_ref, other_ref, out_ref):
     start = pl.multiple_of(jnp.where(lax.axis_index("gz") == 0, PATCH - HALO, 0), HALO // 2)
-    rows = [ref[0, pl.ds(start, HALO)].astype(jnp.float32) for ref in (own_ref, other_ref)]
     lane = lax.broadcasted_iota(jnp.int32, (HALO, LANES), 1)
-    tails = [repeated(value[:, LANES:]) for value in rows]
+    tails = []
+    for image, ref in enumerate((own_ref, other_ref)):
+        rows = ref[0, pl.ds(start, HALO)]
+        out_ref[:, image * LANES : (image + 1) * LANES] = rows[:, :LANES]
+        tails.append(repeated(rows[:, LANES:].astype(jnp.float32)))
     tail = jnp.where(lane < PATCH - LANES, *tails)
-    parts = [rows[0][:, :LANES], rows[1][:, :LANES], tail]
-    out_ref[...] = jnp.concatenate(parts, 1).astype(jnp.bfloat16)
+    out_ref[:, 2 * LANES :] = tail.astype(jnp.bfloat16)
 
 
 def edge_rows(beyond_ref):
@@ -355,8 +357,9 @@
     high = jnp.where(lane < SIDE, pltpu.roll(wide[0], SIDE, 1), wide[1])
     high = jnp.where(lane < extra, narrow[0], high)
     high = jnp.where((lane >= SIDE) & (lane < SIDE + extra), narrow[1], high)
+    low, high = low.astype(jnp.bfloat16), high.astype(jnp.bfloat16)
     odd = lax.rem(lax.axis_index("gx"), 2) == 1
-    return [jnp.where(odd, *pair).astype(jnp.bfloat16) for pair in ((low, high), (high, low))]
+    return [jnp.where(odd, *pair) for pair in ((low, high), (high, low))]
 
 
 def pack_kernel(own_ref, other_ref, first_ref, second_ref):

time: 33.2 us -> 33.3 us (level)
  no operation moved by 1% of the time
where the time goes in v12:
time: 33.3 us; the launch traced here: 33 us
  blocking collectives  14.7 us (44%)
  starting transfers between devices  7.76 us (23%)
  Pallas kernels  5.35 us (16%)
  local copies, waits for them, and re-layouts  2.32 us (7%)
  waiting for transfers between devices  2.15 us (6%)
  between operations  0.71 us (2%)
    all_to_all x1, blocking collectives, pair_body(): got = lax.all_to_all(lines, ('gz', 'gy', 'gx'), 0, 0, tiled=True)  14.7 us
    ppermute x1, starting transfers between devices, pair_body(): beyond = lax.ppermute(edge, ('gz', 'gy'), onward)  3.99 us
    ppermute x1, starting transfers between devices, pair_body(): other = lax.ppermute(images, 'gz', [(0, 1), (1, 0)])  3.03 us
    unnamed x6, local copies, waits for them, and re-layouts  2.32 us
    pallas_call x1, Pallas kernels, pair_body(): pl.pallas_call(functools.partial(early_kernel, count_x), out_shape=(jax.S...  2.18 us
    ppermute x1, waiting for transfers between devices, pair_body(): beyond = lax.ppermute(edge, ('gz', 'gy'), onward)  1.56 us
    pallas_call x1, Pallas kernels, pair_body(): pl.pallas_call(functools.partial(late_kernel, count_x), out_shape=jax.Sha...  1.42 us
    pallas_call x1, Pallas kernels, pair_body(): pl.pallas_call(functools.partial(relax_kernel, rows, count_x), out_shape=...  1.03 us
  transfers between devices with their start and end apart: 4, of which 2 were waited for; matrix products, arithmetic and copies ran while one was open for 0% of the time, Pallas kernels for 8%

profile of v12, /device:TPU:0, one launch (start us, length us, event | category | flops | bytes accessed | tf_op | source)
XLA Modules:
  0.0 33.0 jit_solution(8975787489086536646)
XLA Ops:
  0.6 3.0 %collective-permute-start = (bf16[1,160,160]{2,1,0:T(8,128)(2,1)}, bf16[1,160,160]{2,1,0:T(8,128)(2,1)S(1)}, u32[]{:S(2)}, u32[]{:S(2)}) collective-permute-start(bf16[1,160,160]{2,1,0:T(8,128)(2,1)} %own_ref.1), channel_id=1, source_target_pairs={{0,16},{16,0},{1,17},{17,1},{2,18},{18,2},{3,19},{19,3},{4,20},{20... | collective-permute-start | bytes 153608 | tf_op jit(solution)/shard_map/ppermute | solution.py:575
  3.7 0.0 copy-start
  3.7 1.4 %copy-done = bf16[1600,512]{1,0:T(8,128)(2,1)S(1)} copy-done((bf16[1600,512]{1,0:T(8,128)(2,1)S(1)}, bf16[1600,512]{1,0:T(8,128)(2,1)}, u32[]{:S(2)}) %copy-start) | copy-done | bytes 1638424
  5.1 0.0 copy-start.1
  5.1 0.9 %copy-done.1 = bf16[1,160,160]{2,1,0:T(8,128)(2,1)S(1)} copy-done((bf16[1,160,160]{2,1,0:T(8,128)(2,1)S(1)}, bf16[1,160,160]{2,1,0:T(8,128)(2,1)}, u32[]{:S(2)}) %copy-start.1) | copy-done | bytes 51224
  6.0 0.0 copy-start.2
  6.0 0.3 load.1
  6.3 0.0 collective-permute-done.other_ref
  6.3 0.1 edge.1
  6.4 4.0 %collective-permute-start.1 = (bf16[64,384]{1,0:T(8,128)(2,1)S(1)}, bf16[64,384]{1,0:T(8,128)(2,1)S(1)}, u32[]{:S(2)}, u32[]{:S(2)}) collective-permute-start(bf16[64,384]{1,0:T(8,128)(2,1)S(1)} %edge.1), channel_id=1, source_target_pairs={{0,4},{20,16},{4,8},{24,20},{8,12},{28,24},{1,5},{21,17},{5,9},{25... | collective-permute-start | bytes 147464 | tf_op jit(solution)/shard_map/ppermute | solution.py:601
  10.4 0.2 pack.1
  10.6 1.6 %collective-permute-done.1.beyond_ref = bf16[64,384]{1,0:T(8,128)(2,1)S(1)} collective-permute-done((bf16[64,384]{1,0:T(8,128)(2,1)S(1)}, bf16[64,384]{1,0:T(8,128)(2,1)S(1)}, u32[]{:S(2)}, u32[]{:S(2)}) %collective-permute-start.1) | collective-permute-done | bytes 49184 | tf_op jit(solution)/shard_map/ppermute | solution.py:601
  12.2 0.2 pack_edge.1
  12.3 0.1 collective-permute-start.2
  12.4 0.7 %collective-permute-start.3 = (bf16[224,128]{1,0:T(8,128)(2,1)S(1)}, bf16[224,128]{1,0:T(8,128)(2,1)S(1)}, u32[]{:S(2)}, u32[]{:S(2)}) collective-permute-start(bf16[224,128]{1,0:T(8,128)(2,1)S(1)} %get-tuple-element.14.early_side_ref), channel_id=1, source_target_pairs={{1,2},{2,1},{5,6},{6,5},{9,10},{10,9},{13,14},{14,13},{17,18},{18,... | collective-permute-start | bytes 172040 | tf_op jit(solution)/shard_map/ppermute | solution.py:626
  13.1 0.6 %collective-permute-done.2.beside_ref = bf16[224,128]{1,0:T(8,128)(2,1)S(1)} collective-permute-done((bf16[224,128]{1,0:T(8,128)(2,1)S(1)}, bf16[224,128]{1,0:T(8,128)(2,1)S(1)}, u32[]{:S(2)}, u32[]{:S(2)}) %collective-permute-start.2) | collective-permute-done | bytes 57376 | tf_op jit(solution)/shard_map/ppermute | solution.py:626
  13.6 0.0 copy-done.2
  13.6 2.2 %early.1 = (f32[1,128]{1,0:T(1,128)S(1)}, f32[640,256]{1,0:T(8,128)S(1)}, f32[320,128]{1,0:T(8,128)S(1)}) custom-call(bf16[1,160,160]{2,1,0:T(8,128)(2,1)S(1)} %get-tuple-element.11.own_ref, bf16[1,160,160]{2,1,0:T(8,128)(2,1)S(1)} %collective-permute-done.other_ref, bf16[64,384]{1,0:T(8,128)(2,1)S(1)} %collective-permute-done.1.beyond_ref, ...), custom_call_target="tpu_custom_call" | custom-call | flops 2000000000 | bytes 2097152 | tf_op jit(solution)/shard_map/early/pallas_call | solution.py:636
  15.8 0.0 collective-permute-done.3.beside_ref
  15.8 1.4 %late.1 = f32[32,128]{1,0:T(8,128)S(1)} custom-call(f32[1,128]{1,0:T(1,128)S(1)} %get-tuple-element.17.line_ref, f32[640,256]{1,0:T(8,128)S(1)} %get-tuple-element.18.own_spectra_ref, f32[320,128]{1,0:T(8,128)S(1)} %get-tuple-element.19.own_side_ref, bf16[224,128]{1,0:T(8,128)(2,1)S(1)} %collective-permute-done.3.beside_ref, ...), custom_call_target="tpu_custom_call" | custom-call | flops 1000000000 | bytes 2097152 | tf_op jit(solution)/shard_map/late/pallas_call | solution.py:650
  17.3 14.7 %all_to_all.11 = f32[32,1,128]{2,1,0:T(1,128)S(1)} all-to-all(f32[32,1,128]{2,1,0:T(1,128)S(1)} %bitcast.5), channel_id=1, replica_groups=mesh['gz'=2,'gy'=4,'gx'=4] {'gz','gy','gx'}, dimensions={0} | all-to-all | bytes 32768 | tf_op jit(solution)/shard_map/all_to_all | solution.py:660
  32.0 1.0 %relax.1 = (f32[4,1,4,4]{3,2,1,0:T(4,128)}, f32[2,1,4,4]{3,2,1,0:T(4,128)}) custom-call(f32[32,128]{1,0:T(8,128)S(1)} %bitcast.4), custom_call_target="tpu_custom_call" | custom-call | tf_op jit(solution)/shard_map/relax/pallas_call | solution.py:661
Async XLA Ops:
  0.6 5.7 %collective-permute-start = (bf16[1,160,160]{2,1,0:T(8,128)(2,1)}, bf16[1,160,160]{2,1,0:T(8,128)(2,1)S(1)}, u32[]{:S(2)}, u32[]{:S(2)}) collective-permute-start(bf16[1,160,160]{2,1,0:T(8,128)(2,1)} %own_ref.1), channel_id=1, source_target_pairs={{0,16},{16,0},{1,17},{17,1},{2,18},{18,2},{3,19},{19,3},{4,20},{20... | collective-permute-start | bytes 153608 | tf_op jit(solution)/shard_map/ppermute | solution.py:575
  3.7 1.4 %copy-start = (bf16[1600,512]{1,0:T(8,128)(2,1)S(1)}, bf16[1600,512]{1,0:T(8,128)(2,1)}, u32[]{:S(2)}) copy-start(bf16[1600,512]{1,0:T(8,128)(2,1)} %constant.2.clone.table_ref) | copy-start | bytes 4915204
  5.1 0.9 %copy-start.1 = (bf16[1,160,160]{2,1,0:T(8,128)(2,1)S(1)}, bf16[1,160,160]{2,1,0:T(8,128)(2,1)}, u32[]{:S(2)}) copy-start(bf16[1,160,160]{2,1,0:T(8,128)(2,1)} %own_ref.1) | copy-start | bytes 153604
  6.0 7.6 %copy-start.2 = (s32[1,4,4]{2,1,0:T(4,128)S(1)}, s32[1,4,4]{2,1,0:T(4,128)}, u32[]{:S(2)}) copy-start(s32[1,4,4]{2,1,0:T(4,128)} %mask_ref.1) | copy-start | bytes 196
  6.4 5.7 %collective-permute-start.1 = (bf16[64,384]{1,0:T(8,128)(2,1)S(1)}, bf16[64,384]{1,0:T(8,128)(2,1)S(1)}, u32[]{:S(2)}, u32[]{:S(2)}) collective-permute-start(bf16[64,384]{1,0:T(8,128)(2,1)S(1)} %edge.1), channel_id=1, source_target_pairs={{0,4},{20,16},{4,8},{24,20},{8,12},{28,24},{1,5},{21,17},{5,9},{25... | collective-permute-start | bytes 147464 | tf_op jit(solution)/shard_map/ppermute | solution.py:601
  12.3 1.3 %collective-permute-start.2 = (bf16[224,128]{1,0:T(8,128)(2,1)S(1)}, bf16[224,128]{1,0:T(8,128)(2,1)S(1)}, u32[]{:S(2)}, u32[]{:S(2)}) collective-permute-start(bf16[224,128]{1,0:T(8,128)(2,1)S(1)} %get-tuple-element.15.late_side_ref), channel_id=1, source_target_pairs={{0,1},{1,0},{2,3},{3,2},{4,5},{5,4},{6,7},{7,6},{8,9},{9,8},{10,11... | collective-permute-start | bytes 172040 | tf_op jit(solution)/shard_map/ppermute | solution.py:626
  12.4 3.4 %collective-permute-start.3 = (bf16[224,128]{1,0:T(8,128)(2,1)S(1)}, bf16[224,128]{1,0:T(8,128)(2,1)S(1)}, u32[]{:S(2)}, u32[]{:S(2)}) collective-permute-start(bf16[224,128]{1,0:T(8,128)(2,1)S(1)} %get-tuple-element.14.early_side_ref), channel_id=1, source_target_pairs={{1,2},{2,1},{5,6},{6,5},{9,10},{10,9},{13,14},{14,13},{17,18},{18,... | collective-permute-start | bytes 172040 | tf_op jit(solution)/shard_map/ppermute | solution.py:626
